TPU v7x, 128 devices: a whole 4x4x4 slice. The times are simulated.
128 devices in a mesh: az: 16 (over z_lo, x, core), rg: 8 (over z_hi, y).
Axes of the slice: x: 4, y: 4, z: 4 (z_hi: 2, z_lo: 2; z = z_hi * 2 + z_lo), core: 2. Of those that a mesh axis runs over, the one named last changes fastest.
Arguments:
- raw: bfloat16 [2, 8192, 16384], P(None, 'az', 'rg'), may hold values from -6 to 6
- chirp: bfloat16 [2, 256], replicated, may hold values from -0.25 to 0.25
- az_ref: bfloat16 [2, 64, 512], replicated, may hold values from -0.1875 to 0.1875
- set_index: int32 [16384], P('rg'), may hold values from 0 to 63, as said below
Outputs:
- focused: bfloat16 [2, 8192, 16384], P(None, 'az', 'rg')
Inputs may be any that keep to these rules, and one draw needn't show every extreme that they name: `set_index`: range columns come in aligned runs of 128 that share one set index.
All inputs are finite; a program needn't handle non-finite values.
Results may differ from a plain program's by a relative error of at most 0.0049.
Values may be sent and summed in bfloat16 or wider, within the bound.
No kernel may reach another device: no remote copies, remote signals or barrier semaphores. Data moves between devices by JAX's collectives and lax.ppermute only.
A program may use at most 64 MiB of HBM per device.

v0:
```python
import functools

import jax
import jax.numpy as jnp
from jax import lax
from jax.experimental import pallas as pl
from jax.experimental.pallas import tpu as pltpu
from jax.sharding import PartitionSpec as P


LANES = 128
BLOCK = 256
VMEM_LIMIT = 32 * 1024 * 1024
WHOLE = pl.BlockSpec(memory_space=pltpu.VMEM)
ANYWHERE = pl.BlockSpec(memory_space=pl.ANY)


def split_columns(blocks):
    if blocks < 5:
        return [1] * blocks
    sizes = [1]
    left = blocks - 2
    while left > 0:
        sizes.append(min(2, left))
        left -= sizes[-1]
    return sizes + [1]


def shifted_rows(row, count):
    wide = jnp.broadcast_to(row, (count, row.shape[1]))
    return pltpu.roll(wide, 0, 1, stride=1, stride_axis=0)


def build_range_weights(chirp_ref, weights_ref):
    filled = jnp.zeros((2, BLOCK), jnp.float32)
    padded = jnp.concatenate([chirp_ref[...].astype(jnp.float32), filled], axis=1)
    real = jnp.transpose(shifted_rows(padded[0:1], BLOCK)).astype(jnp.bfloat16)
    imag = jnp.transpose(shifted_rows(padded[1:2], BLOCK)).astype(jnp.bfloat16)
    half = 2 * BLOCK
    weights_ref[:half, :BLOCK] = real
    weights_ref[:half, BLOCK:] = -imag
    weights_ref[half:, :BLOCK] = imag
    weights_ref[half:, BLOCK:] = real


def range_kernel(leading, final, chirp_ref, here_ref, after_ref, *rest):
    out_ref = rest[-3] if leading else rest[-2]
    weights_ref = rest[-1]
    step = pl.program_id(0)

    @pl.when(step == 0)
    def _():
        build_range_weights(chirp_ref, weights_ref)

    if leading:
        rest[-2][...] = here_ref[...]
    after = after_ref[...]
    if final:
        turn = lax.axis_size("rg") // 2
        after = jnp.where(lax.axis_index("rg") % turn == turn - 1, rest[0][...], after)
    segment = jnp.concatenate([here_ref[0], after[0], here_ref[1], after[1]], axis=1)
    product = jnp.dot(segment, weights_ref[...], preferred_element_type=jnp.float32)
    columns = pl.ds(pl.multiple_of(step * BLOCK, BLOCK), BLOCK)
    out_ref[0, :, columns] = product[:, :BLOCK].astype(out_ref.dtype)
    out_ref[1, :, columns] = product[:, BLOCK:].astype(out_ref.dtype)


def range_compress(raw, beyond, chirp, previous, first, count):
    lines = raw.shape[1]
    shape = (2, lines, BLOCK)
    final = beyond is not None
    if final:
        after = list(beyond)
        after_specs = [WHOLE, WHOLE]
    else:
        after = [raw]
        after_specs = [pl.BlockSpec(shape, lambda i: (0, 0, first + i + 1))]
    in_specs = [
        pl.BlockSpec(chirp.shape, lambda i: (0, 0)),
        pl.BlockSpec(shape, lambda i: (0, 0, first + i)),
        *after_specs,
    ]
    operands = [chirp, raw, *after]
    out_shape = [jax.ShapeDtypeStruct((2, lines, BLOCK * count), raw.dtype)]
    out_specs = [WHOLE]
    leading = previous is None
    if leading:
        out_shape.append(jax.ShapeDtypeStruct(shape, raw.dtype))
        out_specs.append(WHOLE)
    else:
        in_specs.append(ANYWHERE)
        operands.append(previous)
    return pl.pallas_call(
        functools.partial(range_kernel, leading, final),
        grid=(count,),
        in_specs=in_specs,
        out_specs=out_specs,
        out_shape=out_shape,
        scratch_shapes=[pltpu.VMEM((4 * BLOCK, 2 * BLOCK), jnp.bfloat16)],
        compiler_params=pltpu.CompilerParams(vmem_limit_bytes=VMEM_LIMIT),
        name="range_compress",
    )(*operands)


def azimuth_kernel(first, sets_ref, refs_ref, here_ref, after_ref, *rest):
    out_ref, weights_ref = rest[-2:]
    lines = here_ref.shape[1]
    set_count = refs_ref.shape[1]
    span = refs_ref.shape[2] + BLOCK
    step = pl.program_id(0)
    for group in range(BLOCK // LANES):
        offset = pl.multiple_of(step * BLOCK + group * LANES, LANES)
        chosen = sets_ref[first * BLOCK + offset]
        picks = lax.broadcasted_iota(jnp.int32, (8, set_count), 1) == chosen
        picks = picks.astype(jnp.bfloat16)
        for part in range(2):
            rows = jnp.dot(picks, refs_ref[part], preferred_element_type=jnp.float32)
            padded = jnp.concatenate([rows, jnp.zeros((8, 2 * BLOCK), jnp.float32)], axis=1)
            base = pltpu.roll(padded, 0, 1, stride=1, stride_axis=0)
            pieces = [base] + [pltpu.roll(base, 8 * q, 1) for q in range(1, LANES // 8)]
            top = jnp.concatenate(pieces, axis=0).astype(jnp.bfloat16)
            low = jnp.concatenate([top[:, -LANES:], top[:, : span - LANES]], axis=1)
            start = part * BLOCK
            weights_ref[start : start + LANES, :] = top[:, :span]
            weights_ref[start + LANES : start + BLOCK, :] = low
        at = pl.ds(offset, LANES)
        here = jnp.concatenate([here_ref[0, :, at], here_ref[1, :, at]], axis=1)
        after = jnp.concatenate([after_ref[0, :, at], after_ref[1, :, at]], axis=1)
        whole = jnp.concatenate([here, after], axis=0)
        columns = slice(group * LANES, (group + 1) * LANES)
        for start in range(0, lines, BLOCK):
            product = jnp.dot(
                weights_ref[...], whole[start : start + span], preferred_element_type=jnp.float32
            )
            real = product[:BLOCK, :LANES] + product[BLOCK:, LANES:]
            imag = product[:BLOCK, LANES:] - product[BLOCK:, :LANES]
            out_ref[0, start : start + BLOCK, columns] = real.astype(out_ref.dtype)
            out_ref[1, start : start + BLOCK, columns] = imag.astype(out_ref.dtype)


def azimuth_compress(sets, refs, here, after, current, columns, first):
    lines = here.shape[1]
    count = here.shape[2] // BLOCK
    span = refs.shape[2] + BLOCK
    in_specs = [pl.BlockSpec(refs.shape, lambda i, s: (0, 0, 0)), WHOLE, WHOLE]
    operands = [sets, refs, here, after]
    aliases = {}
    if current is not None:
        in_specs.append(ANYWHERE)
        operands.append(current)
        aliases = {4: 0}
    return pl.pallas_call(
        functools.partial(azimuth_kernel, first),
        grid_spec=pltpu.PrefetchScalarGridSpec(
            num_scalar_prefetch=1,
            grid=(count,),
            in_specs=in_specs,
            out_specs=pl.BlockSpec((2, lines, BLOCK), lambda i, s: (0, 0, first + i)),
            scratch_shapes=[pltpu.VMEM((2 * BLOCK, span), jnp.bfloat16)],
        ),
        out_shape=jax.ShapeDtypeStruct((2, lines, columns), here.dtype),
        input_output_aliases=aliases,
        compiler_params=pltpu.CompilerParams(vmem_limit_bytes=VMEM_LIMIT),
        name="azimuth_compress",
    )(*operands)


def passed_back(block, axis):
    size = lax.axis_size(axis)
    return lax.ppermute(block, axis, [(i + 1, i) for i in range(size - 1)])


def edge_routes(az_size, rg_size):
    upper, turn = az_size // 2, rg_size // 2
    flat = lambda i, j: i * rg_size + j
    first, second = [], []
    for i in range(az_size):
        for j in range(rg_size - 1):
            if j != turn - 1:
                first.append((flat(i, j + 1), flat(i, j)))
            elif i < upper:
                first.append((flat(i, turn), flat(i + upper, rg_size - 1)))
                second.append((flat(i + upper, rg_size - 1), flat(i, j)))
            else:
                first.append((flat(i, turn), flat(i - upper, j)))
                second.append((flat(i - upper, j), flat(i, j)))
    return first, second


def local(raw, chirp, az_ref, set_index):
    columns = raw.shape[2]
    blocks = columns // BLOCK
    sizes = split_columns(blocks)
    starts = [sum(sizes[:k]) for k in range(len(sizes))]
    axes = ("az", "rg")
    first_route, second_route = edge_routes(lax.axis_size("az"), lax.axis_size("rg"))
    here, after = [], []
    previous, beyond = None, None
    raw = pltpu.with_memory_space_constraint(raw, pltpu.HBM)
    for start, size in zip(starts, sizes):
        final = start + size == blocks
        made = range_compress(raw, beyond if final else None, chirp, previous, start, size)
        previous = made[0]
        here.append(previous)
        after.append(passed_back(previous, "az"))
        if start == 0:
            near = lax.ppermute(made[1], axes, first_route)
            far = lax.ppermute(near, axes, second_route)
            beyond = (near, far)
    focused = None
    for k, start in enumerate(starts):
        focused = azimuth_compress(
            set_index, az_ref, here[k], after[k], focused, columns, start
        )
    return focused


def solution(mesh):
    in_specs = (P(None, "az", "rg"), P(), P(), P("rg"))
    out_specs = P(None, "az", "rg")
    return jax.shard_map(local, mesh=mesh, in_specs=in_specs, out_specs=out_specs, check_vma=False)
```

profile of v0, /device:TPU:71, one launch (start us, length us, event | category | flops | bytes accessed | tf_op | source)
XLA Modules:
  0.0 78.6 jit_solution(1173789042377659939)
XLA Ops:
  0.0 0.0 copy-start.2
  0.0 0.7 copy-done.2
  0.7 2.1 %range_compress.5 = (bf16[2,512,256]{2,1,0:T(8,128)(2,1)S(1)}, bf16[2,512,256]{2,1,0:T(8,128)(2,1)S(1)}) custom-call(bf16[2,256]{1,0:T(2,128)(2,1)S(1)} %copy-done.2, bf16[2,512,2048]{2,1,0:T(8,128)(2,1)} %here_ref.9, bf16[2,512,2048]{2,1,0:T(8,128)(2,1)} %here_ref.9), custom_call_target="tpu_custom_call" | custom-call | tf_op jit(solution)/shard_map/range_compress/pallas_call | solution.py:93
  2.8 5.7 %collective-permute-start = (bf16[2,512,256]{2,1,0:T(8,128)(2,1)S(1)}, bf16[2,512,256]{2,1,0:T(8,128)(2,1)S(1)}, u32[]{:S(2)}, u32[]{:S(2)}) collective-permute-start(bf16[2,512,256]{2,1,0:T(8,128)(2,1)S(1)} %get-tuple-element.7), channel_id=1, source_target_pairs={{1,0},{2,1},{3,2},{4,71},{5,4},{6,5},{7,6},{9,8},{10,9},{11,10},{1... | collective-permute-start | bytes 1572872 | tf_op jit(solution)/shard_map/ppermute | solution.py:207
  8.5 2.9 %range_compress.6.rest_0_.here_ref = bf16[2,512,512]{2,1,0:T(8,128)(2,1)S(1)} custom-call(bf16[2,256]{1,0:T(2,128)(2,1)S(1)} %copy-done.2, bf16[2,512,2048]{2,1,0:T(8,128)(2,1)} %here_ref.9, bf16[2,512,2048]{2,1,0:T(8,128)(2,1)} %here_ref.9, bf16[2,512,256]{2,1,0:T(8,128)(2,1)S(1)} %get-tuple-element.8.rest_0_.here_ref), custom_call_target="tpu_custom_call" | custom-call | tf_op jit(solution)/shard_map/range_compress/pallas_call | solution.py:93
  11.4 2.9 %collective-permute-start.5 = (bf16[2,512,512]{2,1,0:T(8,128)(2,1)S(1)}, bf16[2,512,512]{2,1,0:T(8,128)(2,1)S(1)}, u32[]{:S(2)}, u32[]{:S(2)}) collective-permute-start(bf16[2,512,512]{2,1,0:T(8,128)(2,1)S(1)} %range_compress.6.rest_0_.here_ref), channel_id=1, source_target_pairs={{8,0},{16,8},{24,16},{32,24},{40,32},{48,40},{56,48},{64,56},{72,6... | collective-permute-start | bytes 3145736 | tf_op jit(solution)/shard_map/ppermute | solution.py:170
  14.3 2.9 %range_compress.7.rest_0_.here_ref = bf16[2,512,512]{2,1,0:T(8,128)(2,1)S(1)} custom-call(bf16[2,256]{1,0:T(2,128)(2,1)S(1)} %copy-done.2, bf16[2,512,2048]{2,1,0:T(8,128)(2,1)} %here_ref.9, bf16[2,512,2048]{2,1,0:T(8,128)(2,1)} %here_ref.9, bf16[2,512,512]{2,1,0:T(8,128)(2,1)S(1)} %range_compress.6.rest_0_.here_ref), custom_call_target="tpu_custom_call" | custom-call | tf_op jit(solution)/shard_map/range_compress/pallas_call | solution.py:93
  17.2 1.9 %collective-permute-start.4 = (bf16[2,512,512]{2,1,0:T(8,128)(2,1)S(1)}, bf16[2,512,512]{2,1,0:T(8,128)(2,1)S(1)}, u32[]{:S(2)}, u32[]{:S(2)}) collective-permute-start(bf16[2,512,512]{2,1,0:T(8,128)(2,1)S(1)} %range_compress.7.rest_0_.here_ref), channel_id=1, source_target_pairs={{8,0},{16,8},{24,16},{32,24},{40,32},{48,40},{56,48},{64,56},{72,6... | collective-permute-start | bytes 3145736 | tf_op jit(solution)/shard_map/ppermute | solution.py:170
  19.2 2.9 %range_compress.8.rest_1_.here_ref = bf16[2,512,512]{2,1,0:T(8,128)(2,1)S(1)} custom-call(bf16[2,256]{1,0:T(2,128)(2,1)S(1)} %copy-done.2, bf16[2,512,2048]{2,1,0:T(8,128)(2,1)} %here_ref.9, bf16[2,512,2048]{2,1,0:T(8,128)(2,1)} %here_ref.9, bf16[2,512,512]{2,1,0:T(8,128)(2,1)S(1)} %range_compress.7.rest_0_.here_ref), custom_call_target="tpu_custom_call" | custom-call | tf_op jit(solution)/shard_map/range_compress/pallas_call | solution.py:93
  22.1 0.0 copy-start
  22.1 0.0 copy-start.1
  22.1 3.0 %collective-permute-start.3 = (bf16[2,512,512]{2,1,0:T(8,128)(2,1)S(1)}, bf16[2,512,512]{2,1,0:T(8,128)(2,1)S(1)}, u32[]{:S(2)}, u32[]{:S(2)}) collective-permute-start(bf16[2,512,512]{2,1,0:T(8,128)(2,1)S(1)} %range_compress.8.rest_1_.here_ref), channel_id=1, source_target_pairs={{8,0},{16,8},{24,16},{32,24},{40,32},{48,40},{56,48},{64,56},{72,6... | collective-permute-start | bytes 3145736 | tf_op jit(solution)/shard_map/ppermute | solution.py:170
  25.1 0.0 collective-permute-done.after_ref
  25.1 0.7 collective-permute-start.1
  25.8 1.9 %collective-permute-start.6 = (bf16[2,512,256]{2,1,0:T(8,128)(2,1)S(1)}, bf16[2,512,256]{2,1,0:T(8,128)(2,1)S(1)}, u32[]{:S(2)}, u32[]{:S(2)}) collective-permute-start(bf16[2,512,256]{2,1,0:T(8,128)(2,1)S(1)} %get-tuple-element.8.rest_0_.here_ref), channel_id=1, source_target_pairs={{8,0},{16,8},{24,16},{32,24},{40,32},{48,40},{56,48},{64,56},{72,6... | collective-permute-start | bytes 1572872 | tf_op jit(solution)/shard_map/ppermute | solution.py:170
  27.7 0.0 collective-permute-done.1.rest_0_
  27.7 1.9 %range_compress.9.here_ref = bf16[2,512,256]{2,1,0:T(8,128)(2,1)S(1)} custom-call(bf16[2,256]{1,0:T(2,128)(2,1)S(1)} %copy-done.2, bf16[2,512,2048]{2,1,0:T(8,128)(2,1)} %here_ref.9, bf16[2,512,256]{2,1,0:T(8,128)(2,1)S(1)} %collective-permute-done.after_ref, bf16[2,512,256]{2,1,0:T(8,128)(2,1)S(1)} %collective-permute-done.1.rest_0_, ...), custom_call_target="tpu_custom_call" | custom-call | tf_op jit(solution)/shard_map/range_compress/pallas_call | solution.py:93
  29.7 2.5 %collective-permute-start.2 = (bf16[2,512,256]{2,1,0:T(8,128)(2,1)S(1)}, bf16[2,512,256]{2,1,0:T(8,128)(2,1)S(1)}, u32[]{:S(2)}, u32[]{:S(2)}) collective-permute-start(bf16[2,512,256]{2,1,0:T(8,128)(2,1)S(1)} %range_compress.9.here_ref), channel_id=1, source_target_pairs={{8,0},{16,8},{24,16},{32,24},{40,32},{48,40},{56,48},{64,56},{72,6... | collective-permute-start | bytes 1572872 | tf_op jit(solution)/shard_map/ppermute | solution.py:170
  32.2 25.5 %collective-permute-done.6.after_ref = bf16[2,512,256]{2,1,0:T(8,128)(2,1)S(1)} collective-permute-done((bf16[2,512,256]{2,1,0:T(8,128)(2,1)S(1)}, bf16[2,512,256]{2,1,0:T(8,128)(2,1)S(1)}, u32[]{:S(2)}, u32[]{:S(2)}) %collective-permute-start.6) | collective-permute-done | bytes 524320 | tf_op jit(solution)/shard_map/ppermute | solution.py:170
  57.8 0.0 copy-done
  57.8 0.0 copy-done.1
  57.8 3.1 %azimuth_compress.5.rest_0_ = bf16[2,512,2048]{2,1,0:T(8,128)(2,1)} custom-call(s32[2048]{0:T(1024)S(1)} %copy-done.1, bf16[2,64,512]{2,1,0:T(8,128)(2,1)S(1)} %copy-done, bf16[2,512,256]{2,1,0:T(8,128)(2,1)S(1)} %get-tuple-element.8.rest_0_.here_ref, bf16[2,512,256]{2,1,0:T(8,128)(2,1)S(1)} %collective-permute-done.6.after_ref), custom_call_target="tpu_custom_call" | custom-call | tf_op jit(solution)/shard_map/azimuth_compress/pallas_call | solution.py:152
  60.9 0.0 collective-permute-done.5.after_ref
  60.9 4.9 %azimuth_compress.6.rest_0_ = bf16[2,512,2048]{2,1,0:T(8,128)(2,1)} custom-call(s32[2048]{0:T(1024)S(1)} %copy-done.1, bf16[2,64,512]{2,1,0:T(8,128)(2,1)S(1)} %copy-done, bf16[2,512,512]{2,1,0:T(8,128)(2,1)S(1)} %range_compress.6.rest_0_.here_ref, bf16[2,512,512]{2,1,0:T(8,128)(2,1)S(1)} %collective-permute-done.5.after_ref, ...), custom_call_target="tpu_custom_call", output_to_operand_aliasing={{}: (4, {})} | custom-call | tf_op jit(solution)/shard_map/azimuth_compress/pallas_call | solution.py:152
  65.8 0.0 collective-permute-done.4.after_ref
  65.8 4.9 %azimuth_compress.7.rest_0_ = bf16[2,512,2048]{2,1,0:T(8,128)(2,1)} custom-call(s32[2048]{0:T(1024)S(1)} %copy-done.1, bf16[2,64,512]{2,1,0:T(8,128)(2,1)S(1)} %copy-done, bf16[2,512,512]{2,1,0:T(8,128)(2,1)S(1)} %range_compress.7.rest_0_.here_ref, bf16[2,512,512]{2,1,0:T(8,128)(2,1)S(1)} %collective-permute-done.4.after_ref, ...), custom_call_target="tpu_custom_call", output_to_operand_aliasing={{}: (4, {})} | custom-call | tf_op jit(solution)/shard_map/azimuth_compress/pallas_call | solution.py:152
  70.6 0.0 collective-permute-done.3.after_ref
  70.6 4.9 %azimuth_compress.8.rest_0_ = bf16[2,512,2048]{2,1,0:T(8,128)(2,1)} custom-call(s32[2048]{0:T(1024)S(1)} %copy-done.1, bf16[2,64,512]{2,1,0:T(8,128)(2,1)S(1)} %copy-done, bf16[2,512,512]{2,1,0:T(8,128)(2,1)S(1)} %range_compress.8.rest_1_.here_ref, bf16[2,512,512]{2,1,0:T(8,128)(2,1)S(1)} %collective-permute-done.3.after_ref, ...), custom_call_target="tpu_custom_call", output_to_operand_aliasing={{}: (4, {})} | custom-call | tf_op jit(solution)/shard_map/azimuth_compress/pallas_call | solution.py:152
  75.5 0.0 collective-permute-done.2.after_ref
  75.5 3.1 %azimuth_compress.9 = bf16[2,512,2048]{2,1,0:T(8,128)(2,1)} custom-call(s32[2048]{0:T(1024)S(1)} %copy-done.1, bf16[2,64,512]{2,1,0:T(8,128)(2,1)S(1)} %copy-done, bf16[2,512,256]{2,1,0:T(8,128)(2,1)S(1)} %range_compress.9.here_ref, bf16[2,512,256]{2,1,0:T(8,128)(2,1)S(1)} %collective-permute-done.2.after_ref, ...), custom_call_target="tpu_custom_call", output_to_operand_aliasing={{}: (4, {})} | custom-call | tf_op jit(solution)/shard_map/azimuth_compress/pallas_call | solution.py:152
Async XLA Ops:
  0.0 0.7 copy-start.2
  2.8 22.3 %collective-permute-start = (bf16[2,512,256]{2,1,0:T(8,128)(2,1)S(1)}, bf16[2,512,256]{2,1,0:T(8,128)(2,1)S(1)}, u32[]{:S(2)}, u32[]{:S(2)}) collective-permute-start(bf16[2,512,256]{2,1,0:T(8,128)(2,1)S(1)} %get-tuple-element.7), channel_id=1, source_target_pairs={{1,0},{2,1},{3,2},{4,71},{5,4},{6,5},{7,6},{9,8},{10,9},{11,10},{1... | collective-permute-start | bytes 1572872 | tf_op jit(solution)/shard_map/ppermute | solution.py:207
  11.4 49.5 %collective-permute-start.5 = (bf16[2,512,512]{2,1,0:T(8,128)(2,1)S(1)}, bf16[2,512,512]{2,1,0:T(8,128)(2,1)S(1)}, u32[]{:S(2)}, u32[]{:S(2)}) collective-permute-start(bf16[2,512,512]{2,1,0:T(8,128)(2,1)S(1)} %range_compress.6.rest_0_.here_ref), channel_id=1, source_target_pairs={{8,0},{16,8},{24,16},{32,24},{40,32},{48,40},{56,48},{64,56},{72,6... | collective-permute-start | bytes 3145736 | tf_op jit(solution)/shard_map/ppermute | solution.py:170
  17.2 48.5 %collective-permute-start.4 = (bf16[2,512,512]{2,1,0:T(8,128)(2,1)S(1)}, bf16[2,512,512]{2,1,0:T(8,128)(2,1)S(1)}, u32[]{:S(2)}, u32[]{:S(2)}) collective-permute-start(bf16[2,512,512]{2,1,0:T(8,128)(2,1)S(1)} %range_compress.7.rest_0_.here_ref), channel_id=1, source_target_pairs={{8,0},{16,8},{24,16},{32,24},{40,32},{48,40},{56,48},{64,56},{72,6... | collective-permute-start | bytes 3145736 | tf_op jit(solution)/shard_map/ppermute | solution.py:170
  22.1 35.7 %copy-start = (bf16[2,64,512]{2,1,0:T(8,128)(2,1)S(1)}, bf16[2,64,512]{2,1,0:T(8,128)(2,1)}, u32[]{:S(2)}) copy-start(bf16[2,64,512]{2,1,0:T(8,128)(2,1)} %refs_ref.9) | copy-start | bytes 393220
  22.1 35.7 %copy-start.1 = (s32[2048]{0:T(1024)S(1)}, s32[2048]{0:T(1024)}, u32[]{:S(2)}) copy-start(s32[2048]{0:T(1024)} %sets_ref.9) | copy-start | bytes 24580
  22.1 48.5 %collective-permute-start.3 = (bf16[2,512,512]{2,1,0:T(8,128)(2,1)S(1)}, bf16[2,512,512]{2,1,0:T(8,128)(2,1)S(1)}, u32[]{:S(2)}, u32[]{:S(2)}) collective-permute-start(bf16[2,512,512]{2,1,0:T(8,128)(2,1)S(1)} %range_compress.8.rest_1_.here_ref), channel_id=1, source_target_pairs={{8,0},{16,8},{24,16},{32,24},{40,32},{48,40},{56,48},{64,56},{72,6... | collective-permute-start | bytes 3145736 | tf_op jit(solution)/shard_map/ppermute | solution.py:170
  25.1 2.6 %collective-permute-start.1 = (bf16[2,512,256]{2,1,0:T(8,128)(2,1)S(1)}, bf16[2,512,256]{2,1,0:T(8,128)(2,1)S(1)}, u32[]{:S(2)}, u32[]{:S(2)}) collective-permute-start(bf16[2,512,256]{2,1,0:T(8,128)(2,1)S(1)} %collective-permute-done.after_ref), channel_id=1, source_target_pairs={{71,3},{79,11},{87,19},{95,27},{103,35},{111,43},{119,51},{127,59}... | collective-permute-start | bytes 1572872 | tf_op jit(solution)/shard_map/ppermute | solution.py:208
  25.8 32.0 %collective-permute-start.6 = (bf16[2,512,256]{2,1,0:T(8,128)(2,1)S(1)}, bf16[2,512,256]{2,1,0:T(8,128)(2,1)S(1)}, u32[]{:S(2)}, u32[]{:S(2)}) collective-permute-start(bf16[2,512,256]{2,1,0:T(8,128)(2,1)S(1)} %get-tuple-element.8.rest_0_.here_ref), channel_id=1, source_target_pairs={{8,0},{16,8},{24,16},{32,24},{40,32},{48,40},{56,48},{64,56},{72,6... | collective-permute-start | bytes 1572872 | tf_op jit(solution)/shard_map/ppermute | solution.py:170
  29.7 45.8 %collective-permute-start.2 = (bf16[2,512,256]{2,1,0:T(8,128)(2,1)S(1)}, bf16[2,512,256]{2,1,0:T(8,128)(2,1)S(1)}, u32[]{:S(2)}, u32[]{:S(2)}) collective-permute-start(bf16[2,512,256]{2,1,0:T(8,128)(2,1)S(1)} %range_compress.9.here_ref), channel_id=1, source_target_pairs={{8,0},{16,8},{24,16},{32,24},{40,32},{48,40},{56,48},{64,56},{72,6... | collective-permute-start | bytes 1572872 | tf_op jit(solution)/shard_map/ppermute | solution.py:170
where the time goes:
time: 79.1 us; the launch traced here: 78.6 us
  Pallas kernels  33.6 us (42%)
  waiting for transfers between devices  25.6 us (32%)
  starting transfers between devices  18.6 us (24%)
    ppermute x5, waiting for transfers between devices, passed_back(): return lax.ppermute(block, axis, [(i + 1, i) for i in range(size - 1)])  25.5 us
    pallas_call x5, Pallas kernels, azimuth_compress(): pl.pallas_call(functools.partial(azimuth_kernel, first), grid_spec=pltpu....  20.9 us
    pallas_call x5, Pallas kernels, range_compress(): pl.pallas_call(functools.partial(range_kernel, leading, final), grid=(cou...  12.8 us
    ppermute x5, starting transfers between devices, passed_back(): return lax.ppermute(block, axis, [(i + 1, i) for i in range(size - 1)])  12.2 us
    ppermute x1, starting transfers between devices, local(): near = lax.ppermute(made[1], axes, first_route)  5.7 us
  transfers between devices with their start and end apart: 7, of which 1 were waited for; matrix products, arithmetic and copies ran while one was open for 0% of the time, Pallas kernels for 36%

commit v1 on v0

v1 whole, which is shorter than its diff:
```python
import functools

import jax
import jax.numpy as jnp
from jax import lax
from jax.experimental import pallas as pl
from jax.experimental.pallas import tpu as pltpu
from jax.sharding import PartitionSpec as P


LANES = 128
BLOCK = 256
HEAD_ROWS = 128
VMEM_LIMIT = 16 * 1024 * 1024
WHOLE = pl.BlockSpec(memory_space=pltpu.VMEM)
ANYWHERE = pl.BlockSpec(memory_space=pl.ANY)
PARAMS = pltpu.CompilerParams(vmem_limit_bytes=VMEM_LIMIT)


def shifted_rows(row, count):
    wide = jnp.broadcast_to(row, (count, row.shape[1]))
    return pltpu.roll(wide, 0, 1, stride=1, stride_axis=0)


def build_range_weights(chirp_ref, weights_ref):
    filled = jnp.zeros((2, BLOCK), jnp.float32)
    padded = jnp.concatenate([chirp_ref[...].astype(jnp.float32), filled], axis=1)
    real = jnp.transpose(shifted_rows(padded[0:1], BLOCK)).astype(jnp.bfloat16)
    imag = jnp.transpose(shifted_rows(padded[1:2], BLOCK)).astype(jnp.bfloat16)
    half = 2 * BLOCK
    weights_ref[:half, :BLOCK] = real
    weights_ref[:half, BLOCK:] = -imag
    weights_ref[half:, :BLOCK] = imag
    weights_ref[half:, BLOCK:] = real


def correlate(segment, weights_ref):
    product = jnp.dot(segment, weights_ref[...], preferred_element_type=jnp.float32)
    product = product.astype(jnp.bfloat16)
    return product[:, :BLOCK], product[:, BLOCK:]


def head_kernel(chirp_ref, raw_ref, out_ref, weights_ref):
    step = pl.program_id(0)

    @pl.when(step == 0)
    def _():
        build_range_weights(chirp_ref, weights_ref)

    segment = jnp.concatenate([raw_ref[0], raw_ref[1]], axis=1)
    rows = pl.ds(pl.multiple_of(step * HEAD_ROWS, HEAD_ROWS), HEAD_ROWS)
    out_ref[0, rows], out_ref[1, rows] = correlate(segment, weights_ref)


def range_head(raw, chirp):
    lines = raw.shape[1]
    return pl.pallas_call(
        head_kernel,
        grid=(lines // HEAD_ROWS,),
        in_specs=[
            pl.BlockSpec(chirp.shape, lambda i: (0, 0)),
            pl.BlockSpec((2, HEAD_ROWS, 2 * BLOCK), lambda i: (0, i, 0)),
        ],
        out_specs=[WHOLE, WHOLE],
        out_shape=[
            jax.ShapeDtypeStruct((2, lines, BLOCK), raw.dtype),
            jax.ShapeDtypeStruct((4 * BLOCK, 2 * BLOCK), raw.dtype),
        ],
        compiler_params=PARAMS,
        name="range_head",
    )(chirp, raw)


def range_kernel(first, sizes, with_edge, weights_ref, raw_ref, *rest):
    outs = rest[-len(sizes) - with_edge :]
    if with_edge:
        outs[-1][...] = raw_ref[:, :, :BLOCK]
    block = first
    for out_ref, size in zip(outs, sizes):
        for k in range(size):
            span = slice(block * BLOCK, (block + 2) * BLOCK)
            segment = jnp.concatenate([raw_ref[0, :, span], raw_ref[1, :, span]], axis=1)
            columns = slice(k * BLOCK, (k + 1) * BLOCK)
            out_ref[0, :, columns], out_ref[1, :, columns] = correlate(segment, weights_ref)
            block += 1


def range_compress(raw, weights, previous, first, sizes, with_edge):
    lines = raw.shape[1]
    widths = [BLOCK * size for size in sizes] + [BLOCK] * with_edge
    return pl.pallas_call(
        functools.partial(range_kernel, first, sizes, with_edge),
        in_specs=[WHOLE, WHOLE, ANYWHERE],
        out_specs=[WHOLE] * len(widths),
        out_shape=[jax.ShapeDtypeStruct((2, lines, width), raw.dtype) for width in widths],
        compiler_params=PARAMS,
        name="range_compress",
    )(weights, raw, previous)


def tail_kernel(weights_ref, raw_ref, near_ref, far_ref, out_ref):
    turn = lax.axis_size("rg") // 2
    crossing = lax.axis_index("rg") % turn == turn - 1
    after = jnp.where(crossing, far_ref[...], near_ref[...])
    here = raw_ref[:, :, raw_ref.shape[2] - BLOCK :]
    segment = jnp.concatenate([here[0], after[0], here[1], after[1]], axis=1)
    out_ref[0], out_ref[1] = correlate(segment, weights_ref)


def range_tail(raw, weights, near, far):
    return pl.pallas_call(
        tail_kernel,
        in_specs=[WHOLE] * 4,
        out_specs=WHOLE,
        out_shape=jax.ShapeDtypeStruct((2, raw.shape[1], BLOCK), raw.dtype),
        compiler_params=PARAMS,
        name="range_tail",
    )(weights, raw, near, far)


def azimuth_weights_kernel(sets_ref, refs_ref, previous_ref, weights_ref, wide_ref):
    taps = refs_ref.shape[2]
    span = taps + BLOCK
    group = pl.program_id(0)

    @pl.when(group == 0)
    def _():
        wide_ref[...] = refs_ref[...].astype(jnp.float32)

    chosen = sets_ref[group * LANES]
    for part in range(2):
        row = wide_ref[part, pl.ds(chosen, 1), :]
        padded = jnp.concatenate([row, jnp.zeros((1, 2 * BLOCK), jnp.float32)], axis=1)
        base = shifted_rows(padded, 8)
        start = part * BLOCK
        for q in range(0, LANES, 16):
            upper = pltpu.roll(base, q, 1) if q else base
            lower = pltpu.roll(base, q + 8, 1)
            top = jnp.concatenate([upper, lower], axis=0).astype(jnp.bfloat16)
            low = jnp.concatenate([top[:, -LANES:], top[:, : span - LANES]], axis=1)
            weights_ref[group, start + q : start + q + 16, :] = top[:, :span]
            weights_ref[group, start + LANES + q : start + LANES + q + 16, :] = low


def azimuth_weights(sets, refs, previous):
    taps = refs.shape[2]
    groups = sets.shape[0] // LANES
    return pl.pallas_call(
        azimuth_weights_kernel,
        grid_spec=pltpu.PrefetchScalarGridSpec(
            num_scalar_prefetch=1,
            grid=(groups,),
            in_specs=[WHOLE, ANYWHERE],
            out_specs=WHOLE,
            scratch_shapes=[pltpu.VMEM(refs.shape, jnp.float32)],
        ),
        out_shape=jax.ShapeDtypeStruct((groups, 2 * BLOCK, taps + BLOCK), refs.dtype),
        compiler_params=PARAMS,
        name="azimuth_weights",
    )(sets, refs, previous)


def azimuth_kernel(first, weights_ref, here_ref, after_ref, *rest):
    out_ref = rest[-1]
    lines = here_ref.shape[1]
    span = weights_ref.shape[2]
    step = pl.program_id(0)
    for group in range(BLOCK // LANES):
        at = pl.ds(pl.multiple_of(step * BLOCK + group * LANES, LANES), LANES)
        here = jnp.concatenate([here_ref[0, :, at], here_ref[1, :, at]], axis=1)
        after = jnp.concatenate([after_ref[0, :, at], after_ref[1, :, at]], axis=1)
        whole = jnp.concatenate([here, after], axis=0)
        weights = weights_ref[(first + step) * (BLOCK // LANES) + group]
        columns = slice(group * LANES, (group + 1) * LANES)
        for start in range(0, lines, BLOCK):
            product = jnp.dot(
                weights, whole[start : start + span], preferred_element_type=jnp.float32
            )
            real = product[:BLOCK, :LANES] + product[BLOCK:, LANES:]
            imag = product[:BLOCK, LANES:] - product[BLOCK:, :LANES]
            out_ref[0, start : start + BLOCK, columns] = real.astype(out_ref.dtype)
            out_ref[1, start : start + BLOCK, columns] = imag.astype(out_ref.dtype)


def azimuth_compress(weights, here, after, current, columns, first):
    lines = here.shape[1]
    count = here.shape[2] // BLOCK
    in_specs = [WHOLE, WHOLE, WHOLE]
    operands = [weights, here, after]
    aliases = {}
    if current is not None:
        in_specs.append(ANYWHERE)
        operands.append(current)
        aliases = {3: 0}
    return pl.pallas_call(
        functools.partial(azimuth_kernel, first),
        grid=(count,),
        in_specs=in_specs,
        out_specs=pl.BlockSpec((2, lines, BLOCK), lambda i: (0, 0, first + i)),
        out_shape=jax.ShapeDtypeStruct((2, lines, columns), here.dtype),
        input_output_aliases=aliases,
        compiler_params=PARAMS,
        name="azimuth_compress",
    )(*operands)


def passed_back(block, axis):
    size = lax.axis_size(axis)
    return lax.ppermute(block, axis, [(i + 1, i) for i in range(size - 1)])


def edge_routes(az_size, rg_size):
    upper, turn = az_size // 2, rg_size // 2
    flat = lambda i, j: i * rg_size + j
    first, second = [], []
    for i in range(az_size):
        for j in range(rg_size - 1):
            if j != turn - 1:
                first.append((flat(i, j + 1), flat(i, j)))
            elif i < upper:
                first.append((flat(i, turn), flat(i + upper, rg_size - 1)))
                second.append((flat(i + upper, rg_size - 1), flat(i, j)))
            else:
                first.append((flat(i, turn), flat(i - upper, j)))
                second.append((flat(i - upper, j), flat(i, j)))
    return first, second


def local(raw, chirp, az_ref, set_index):
    columns = raw.shape[2]
    axes = ("az", "rg")
    first_route, second_route = edge_routes(lax.axis_size("az"), lax.axis_size("rg"))
    distant = pltpu.with_memory_space_constraint(raw, pltpu.HBM)
    first, weights = range_head(
        distant, pltpu.with_memory_space_constraint(chirp, pltpu.HBM)
    )
    second, edge = range_compress(raw, weights, first, 1, (2,), True)
    third, fourth = range_compress(raw, weights, second, 3, (2, 2), False)
    here = [first, second, third, fourth]
    after = []
    for piece in here:
        after.append(passed_back(piece, "az"))
    near = lax.ppermute(edge, axes, first_route)
    far = lax.ppermute(near, axes, second_route)
    here.append(range_tail(raw, weights, near, far))
    after.append(passed_back(here[-1], "az"))
    turns = azimuth_weights(set_index, az_ref, third)
    focused = None
    start = 0
    for k, piece in enumerate(here):
        focused = azimuth_compress(turns, piece, after[k], focused, columns, start)
        start += piece.shape[2] // BLOCK
    return focused


def solution(mesh):
    in_specs = (P(None, "az", "rg"), P(), P(), P("rg"))
    out_specs = P(None, "az", "rg")
    return jax.shard_map(local, mesh=mesh, in_specs=in_specs, out_specs=out_specs, check_vma=False)
```

time: 79.1 us -> 68.8 us (0.87)
  Pallas kernels: 33.6 us -> 24.2 us
  waiting for transfers between devices: 25.6 us -> 24.6 us
  starting transfers between devices: 18.6 us -> 19.5 us
    pallas_call x10, Pallas kernels: 33.6 us -> 24.2 us  [the longest x5 11.9 us: azimuth_compress(): pl.pallas_call(functools.partial(azimuth_kernel, first), grid=(count,), i...]
    ppermute x5, waiting for transfers between devices: 25.5 us -> 24.2 us  [passed_back(): return lax.ppermute(block, axis, [(i + 1, i) for i in range(size - 1)])]
    ppermute x5, starting transfers between devices: 12.2 us -> 13.1 us  [passed_back(): return lax.ppermute(block, axis, [(i + 1, i) for i in range(size - 1)])]
  transfers between devices with their start and end apart: 7 -> 7, of which waited for: 1 -> 2; matrix products, arithmetic and copies ran while one was open for 0% -> 0% of each run, Pallas kernels for 36% -> 26%
where the time goes in v1:
time: 68.8 us; the launch traced here: 68.5 us
  waiting for transfers between devices  24.6 us (36%)
  Pallas kernels  24.2 us (35%)
  starting transfers between devices  19.5 us (28%)
    ppermute x5, waiting for transfers between devices, passed_back(): return lax.ppermute(block, axis, [(i + 1, i) for i in range(size - 1)])  24.2 us
    ppermute x5, starting transfers between devices, passed_back(): return lax.ppermute(block, axis, [(i + 1, i) for i in range(size - 1)])  13.1 us
    pallas_call x5, Pallas kernels, azimuth_compress(): pl.pallas_call(functools.partial(azimuth_kernel, first), grid=(count,), i...  11.9 us
    ppermute x1, starting transfers between devices, local(): near = lax.ppermute(edge, axes, first_route)  5.7 us
    pallas_call x1, Pallas kernels, azimuth_weights(): pl.pallas_call(azimuth_weights_kernel, grid_spec=pltpu.PrefetchScalarGrid...  4.72 us
    pallas_call x2, Pallas kernels, range_compress(): pl.pallas_call(functools.partial(range_kernel, first, sizes, with_edge),...  3.6 us
    pallas_call x1, Pallas kernels, range_head(): pl.pallas_call(head_kernel, grid=(lines // HEAD_ROWS,), in_specs=[pl.Bloc...  3.27 us
  transfers between devices with their start and end apart: 7, of which 2 were waited for; matrix products, arithmetic and copies ran while one was open for 0% of the time, Pallas kernels for 26%

profile of v1, /device:TPU:71, one launch (start us, length us, event | category | flops | bytes accessed | tf_op | source)
XLA Modules:
  0.0 68.5 jit_solution(6281111289952932413)
XLA Ops:
  0.0 0.0 copy-start
  0.0 3.3 %range_head.1 = (bf16[2,512,256]{2,1,0:T(8,128)(2,1)S(1)}, bf16[1024,512]{1,0:T(8,128)(2,1)S(1)}) custom-call(bf16[2,256]{1,0:T(2,128)(2,1)} %chirp_ref.1, bf16[2,512,2048]{2,1,0:T(8,128)(2,1)} %raw_ref.7), custom_call_target="tpu_custom_call" | custom-call | tf_op jit(solution)/shard_map/range_head/pallas_call | solution.py:57
  3.3 0.0 copy-done
  3.3 1.3 %range_compress.2 = (bf16[2,512,512]{2,1,0:T(8,128)(2,1)S(1)}, bf16[2,512,256]{2,1,0:T(8,128)(2,1)S(1)}) custom-call(bf16[1024,512]{1,0:T(8,128)(2,1)S(1)} %get-tuple-element.11.weights_ref, bf16[2,512,2048]{2,1,0:T(8,128)(2,1)S(1)} %copy-done, bf16[2,512,256]{2,1,0:T(8,128)(2,1)S(1)} %get-tuple-element.12.rest_0_.here_ref), custom_call_target="tpu_custom_call" | custom-call | tf_op jit(solution)/shard_map/range_compress/pallas_call | solution.py:91
  4.6 5.7 %collective-permute-start = (bf16[2,512,256]{2,1,0:T(8,128)(2,1)S(1)}, bf16[2,512,256]{2,1,0:T(8,128)(2,1)S(1)}, u32[]{:S(2)}, u32[]{:S(2)}) collective-permute-start(bf16[2,512,256]{2,1,0:T(8,128)(2,1)S(1)} %get-tuple-element.15), channel_id=1, source_target_pairs={{1,0},{2,1},{3,2},{4,71},{5,4},{6,5},{7,6},{9,8},{10,9},{11,10},{1... | collective-permute-start | bytes 1572872 | tf_op jit(solution)/shard_map/ppermute | solution.py:243
  10.3 2.9 %collective-permute-start.5 = (bf16[2,512,512]{2,1,0:T(8,128)(2,1)S(1)}, bf16[2,512,512]{2,1,0:T(8,128)(2,1)S(1)}, u32[]{:S(2)}, u32[]{:S(2)}) collective-permute-start(bf16[2,512,512]{2,1,0:T(8,128)(2,1)S(1)} %get-tuple-element.13.rest_0_.here_ref), channel_id=1, source_target_pairs={{8,0},{16,8},{24,16},{32,24},{40,32},{48,40},{56,48},{64,56},{72,6... | collective-permute-start | bytes 3145736 | tf_op jit(solution)/shard_map/ppermute | solution.py:209
  13.1 2.3 %range_compress.3 = (bf16[2,512,512]{2,1,0:T(8,128)(2,1)S(1)}, bf16[2,512,512]{2,1,0:T(8,128)(2,1)S(1)}) custom-call(bf16[1024,512]{1,0:T(8,128)(2,1)S(1)} %get-tuple-element.11.weights_ref, bf16[2,512,2048]{2,1,0:T(8,128)(2,1)S(1)} %copy-done, bf16[2,512,512]{2,1,0:T(8,128)(2,1)S(1)} %get-tuple-element.13.rest_0_.here_ref), custom_call_target="tpu_custom_call" | custom-call | tf_op jit(solution)/shard_map/range_compress/pallas_call | solution.py:91
  15.5 0.0 copy-start.1
  15.5 0.0 copy-start.2
  15.5 2.1 %collective-permute-start.4 = (bf16[2,512,512]{2,1,0:T(8,128)(2,1)S(1)}, bf16[2,512,512]{2,1,0:T(8,128)(2,1)S(1)}, u32[]{:S(2)}, u32[]{:S(2)}) collective-permute-start(bf16[2,512,512]{2,1,0:T(8,128)(2,1)S(1)} %get-tuple-element.14.previous_ref.here_ref), channel_id=1, source_target_pairs={{8,0},{16,8},{24,16},{32,24},{40,32},{48,40},{56,48},{64,56},{72,6... | collective-permute-start | bytes 3145736 | tf_op jit(solution)/shard_map/ppermute | solution.py:209
  17.6 2.8 %collective-permute-start.3 = (bf16[2,512,512]{2,1,0:T(8,128)(2,1)S(1)}, bf16[2,512,512]{2,1,0:T(8,128)(2,1)S(1)}, u32[]{:S(2)}, u32[]{:S(2)}) collective-permute-start(bf16[2,512,512]{2,1,0:T(8,128)(2,1)S(1)} %get-tuple-element.16.here_ref), channel_id=1, source_target_pairs={{8,0},{16,8},{24,16},{32,24},{40,32},{48,40},{56,48},{64,56},{72,6... | collective-permute-start | bytes 3145736 | tf_op jit(solution)/shard_map/ppermute | solution.py:209
  20.4 0.4 collective-permute-done.near_ref
  20.9 0.7 collective-permute-start.1
  21.5 3.4 %collective-permute-start.6 = (bf16[2,512,256]{2,1,0:T(8,128)(2,1)S(1)}, bf16[2,512,256]{2,1,0:T(8,128)(2,1)S(1)}, u32[]{:S(2)}, u32[]{:S(2)}) collective-permute-start(bf16[2,512,256]{2,1,0:T(8,128)(2,1)S(1)} %get-tuple-element.12.rest_0_.here_ref), channel_id=1, source_target_pairs={{8,0},{16,8},{24,16},{32,24},{40,32},{48,40},{56,48},{64,56},{72,6... | collective-permute-start | bytes 1572872 | tf_op jit(solution)/shard_map/ppermute | solution.py:209
  25.0 0.0 collective-permute-done.1.far_ref
  25.0 0.7 %range_tail.1.here_ref = bf16[2,512,256]{2,1,0:T(8,128)(2,1)S(1)} custom-call(bf16[1024,512]{1,0:T(8,128)(2,1)S(1)} %get-tuple-element.11.weights_ref, bf16[2,512,2048]{2,1,0:T(8,128)(2,1)S(1)} %copy-done, bf16[2,512,256]{2,1,0:T(8,128)(2,1)S(1)} %collective-permute-done.near_ref, bf16[2,512,256]{2,1,0:T(8,128)(2,1)S(1)} %collective-permute-done.1.far_ref), custom_call_target="tpu_custom_call" | custom-call | tf_op jit(solution)/shard_map/range_tail/pallas_call | solution.py:111
  25.7 1.9 %collective-permute-start.2 = (bf16[2,512,256]{2,1,0:T(8,128)(2,1)S(1)}, bf16[2,512,256]{2,1,0:T(8,128)(2,1)S(1)}, u32[]{:S(2)}, u32[]{:S(2)}) collective-permute-start(bf16[2,512,256]{2,1,0:T(8,128)(2,1)S(1)} %range_tail.1.here_ref), channel_id=1, source_target_pairs={{8,0},{16,8},{24,16},{32,24},{40,32},{48,40},{56,48},{64,56},{72,6... | collective-permute-start | bytes 1572872 | tf_op jit(solution)/shard_map/ppermute | solution.py:209
  27.6 0.0 copy-done.1
  27.7 0.0 copy-done.2
  27.7 4.7 %azimuth_weights.1.weights_ref = bf16[16,512,768]{2,1,0:T(8,128)(2,1)S(1)} custom-call(s32[2048]{0:T(1024)S(1)} %copy-done.2, bf16[2,64,512]{2,1,0:T(8,128)(2,1)S(1)} %copy-done.1, bf16[2,512,512]{2,1,0:T(8,128)(2,1)S(1)} %get-tuple-element.14.previous_ref.here_ref), custom_call_target="tpu_custom_call" | custom-call | tf_op jit(solution)/shard_map/azimuth_weights/pallas_call | solution.py:148
  32.4 24.2 %collective-permute-done.6.after_ref = bf16[2,512,256]{2,1,0:T(8,128)(2,1)S(1)} collective-permute-done((bf16[2,512,256]{2,1,0:T(8,128)(2,1)S(1)}, bf16[2,512,256]{2,1,0:T(8,128)(2,1)S(1)}, u32[]{:S(2)}, u32[]{:S(2)}) %collective-permute-start.6) | collective-permute-done | bytes 524320 | tf_op jit(solution)/shard_map/ppermute | solution.py:209
  56.6 1.8 %azimuth_compress.5.rest_0_ = bf16[2,512,2048]{2,1,0:T(8,128)(2,1)} custom-call(bf16[16,512,768]{2,1,0:T(8,128)(2,1)S(1)} %azimuth_weights.1.weights_ref, bf16[2,512,256]{2,1,0:T(8,128)(2,1)S(1)} %get-tuple-element.12.rest_0_.here_ref, bf16[2,512,256]{2,1,0:T(8,128)(2,1)S(1)} %collective-permute-done.6.after_ref), custom_call_target="tpu_custom_call" | custom-call | tf_op jit(solution)/shard_map/azimuth_compress/pallas_call | solution.py:195
  58.4 0.0 collective-permute-done.5.after_ref
  58.4 2.8 %azimuth_compress.6.rest_0_ = bf16[2,512,2048]{2,1,0:T(8,128)(2,1)} custom-call(bf16[16,512,768]{2,1,0:T(8,128)(2,1)S(1)} %azimuth_weights.1.weights_ref, bf16[2,512,512]{2,1,0:T(8,128)(2,1)S(1)} %get-tuple-element.13.rest_0_.here_ref, bf16[2,512,512]{2,1,0:T(8,128)(2,1)S(1)} %collective-permute-done.5.after_ref, ...), custom_call_target="tpu_custom_call", output_to_operand_aliasing={{}: (3, {})} | custom-call | tf_op jit(solution)/shard_map/azimuth_compress/pallas_call | solution.py:195
  61.2 0.0 collective-permute-done.4.after_ref
  61.2 2.8 %azimuth_compress.7.rest_0_ = bf16[2,512,2048]{2,1,0:T(8,128)(2,1)} custom-call(bf16[16,512,768]{2,1,0:T(8,128)(2,1)S(1)} %azimuth_weights.1.weights_ref, bf16[2,512,512]{2,1,0:T(8,128)(2,1)S(1)} %get-tuple-element.14.previous_ref.here_ref, bf16[2,512,512]{2,1,0:T(8,128)(2,1)S(1)} %collective-permute-done.4.after_ref, ...), custom_call_target="tpu_custom_call", output_to_operand_aliasing={{}: (3, {})} | custom-call | tf_op jit(solution)/shard_map/azimuth_compress/pallas_call | solution.py:195
  64.0 0.0 collective-permute-done.3.after_ref
  64.0 2.8 %azimuth_compress.8.rest_0_ = bf16[2,512,2048]{2,1,0:T(8,128)(2,1)} custom-call(bf16[16,512,768]{2,1,0:T(8,128)(2,1)S(1)} %azimuth_weights.1.weights_ref, bf16[2,512,512]{2,1,0:T(8,128)(2,1)S(1)} %get-tuple-element.16.here_ref, bf16[2,512,512]{2,1,0:T(8,128)(2,1)S(1)} %collective-permute-done.3.after_ref, ...), custom_call_target="tpu_custom_call", output_to_operand_aliasing={{}: (3, {})} | custom-call | tf_op jit(solution)/shard_map/azimuth_compress/pallas_call | solution.py:195
  66.7 0.0 collective-permute-done.2.after_ref
  66.7 1.8 %azimuth_compress.9 = bf16[2,512,2048]{2,1,0:T(8,128)(2,1)} custom-call(bf16[16,512,768]{2,1,0:T(8,128)(2,1)S(1)} %azimuth_weights.1.weights_ref, bf16[2,512,256]{2,1,0:T(8,128)(2,1)S(1)} %range_tail.1.here_ref, bf16[2,512,256]{2,1,0:T(8,128)(2,1)S(1)} %collective-permute-done.2.after_ref, ...), custom_call_target="tpu_custom_call", output_to_operand_aliasing={{}: (3, {})} | custom-call | tf_op jit(solution)/shard_map/azimuth_compress/pallas_call | solution.py:195
Async XLA Ops:
  0.0 3.3 %copy-start = (bf16[2,512,2048]{2,1,0:T(8,128)(2,1)S(1)}, bf16[2,512,2048]{2,1,0:T(8,128)(2,1)}, u32[]{:S(2)}) copy-start(bf16[2,512,2048]{2,1,0:T(8,128)(2,1)} %raw_ref.7) | copy-start | bytes 12582916
  4.6 16.3 %collective-permute-start = (bf16[2,512,256]{2,1,0:T(8,128)(2,1)S(1)}, bf16[2,512,256]{2,1,0:T(8,128)(2,1)S(1)}, u32[]{:S(2)}, u32[]{:S(2)}) collective-permute-start(bf16[2,512,256]{2,1,0:T(8,128)(2,1)S(1)} %get-tuple-element.15), channel_id=1, source_target_pairs={{1,0},{2,1},{3,2},{4,71},{5,4},{6,5},{7,6},{9,8},{10,9},{11,10},{1... | collective-permute-start | bytes 1572872 | tf_op jit(solution)/shard_map/ppermute | solution.py:243
  10.3 48.1 %collective-permute-start.5 = (bf16[2,512,512]{2,1,0:T(8,128)(2,1)S(1)}, bf16[2,512,512]{2,1,0:T(8,128)(2,1)S(1)}, u32[]{:S(2)}, u32[]{:S(2)}) collective-permute-start(bf16[2,512,512]{2,1,0:T(8,128)(2,1)S(1)} %get-tuple-element.13.rest_0_.here_ref), channel_id=1, source_target_pairs={{8,0},{16,8},{24,16},{32,24},{40,32},{48,40},{56,48},{64,56},{72,6... | collective-permute-start | bytes 3145736 | tf_op jit(solution)/shard_map/ppermute | solution.py:209
  15.5 12.2 %copy-start.1 = (bf16[2,64,512]{2,1,0:T(8,128)(2,1)S(1)}, bf16[2,64,512]{2,1,0:T(8,128)(2,1)}, u32[]{:S(2)}) copy-start(bf16[2,64,512]{2,1,0:T(8,128)(2,1)} %refs_ref.1) | copy-start | bytes 393220
  15.5 12.2 %copy-start.2 = (s32[2048]{0:T(1024)S(1)}, s32[2048]{0:T(1024)}, u32[]{:S(2)}) copy-start(s32[2048]{0:T(1024)} %sets_ref.1) | copy-start | bytes 24580
  15.5 45.7 %collective-permute-start.4 = (bf16[2,512,512]{2,1,0:T(8,128)(2,1)S(1)}, bf16[2,512,512]{2,1,0:T(8,128)(2,1)S(1)}, u32[]{:S(2)}, u32[]{:S(2)}) collective-permute-start(bf16[2,512,512]{2,1,0:T(8,128)(2,1)S(1)} %get-tuple-element.14.previous_ref.here_ref), channel_id=1, source_target_pairs={{8,0},{16,8},{24,16},{32,24},{40,32},{48,40},{56,48},{64,56},{72,6... | collective-permute-start | bytes 3145736 | tf_op jit(solution)/shard_map/ppermute | solution.py:209
  17.6 46.4 %collective-permute-start.3 = (bf16[2,512,512]{2,1,0:T(8,128)(2,1)S(1)}, bf16[2,512,512]{2,1,0:T(8,128)(2,1)S(1)}, u32[]{:S(2)}, u32[]{:S(2)}) collective-permute-start(bf16[2,512,512]{2,1,0:T(8,128)(2,1)S(1)} %get-tuple-element.16.here_ref), channel_id=1, source_target_pairs={{8,0},{16,8},{24,16},{32,24},{40,32},{48,40},{56,48},{64,56},{72,6... | collective-permute-start | bytes 3145736 | tf_op jit(solution)/shard_map/ppermute | solution.py:209
  20.9 4.1 %collective-permute-start.1 = (bf16[2,512,256]{2,1,0:T(8,128)(2,1)S(1)}, bf16[2,512,256]{2,1,0:T(8,128)(2,1)S(1)}, u32[]{:S(2)}, u32[]{:S(2)}) collective-permute-start(bf16[2,512,256]{2,1,0:T(8,128)(2,1)S(1)} %collective-permute-done.near_ref), channel_id=1, source_target_pairs={{71,3},{79,11},{87,19},{95,27},{103,35},{111,43},{119,51},{127,59}... | collective-permute-start | bytes 1572872 | tf_op jit(solution)/shard_map/ppermute | solution.py:244
  21.5 35.0 %collective-permute-start.6 = (bf16[2,512,256]{2,1,0:T(8,128)(2,1)S(1)}, bf16[2,512,256]{2,1,0:T(8,128)(2,1)S(1)}, u32[]{:S(2)}, u32[]{:S(2)}) collective-permute-start(bf16[2,512,256]{2,1,0:T(8,128)(2,1)S(1)} %get-tuple-element.12.rest_0_.here_ref), channel_id=1, source_target_pairs={{8,0},{16,8},{24,16},{32,24},{40,32},{48,40},{56,48},{64,56},{72,6... | collective-permute-start | bytes 1572872 | tf_op jit(solution)/shard_map/ppermute | solution.py:209
  25.7 41.0 %collective-permute-start.2 = (bf16[2,512,256]{2,1,0:T(8,128)(2,1)S(1)}, bf16[2,512,256]{2,1,0:T(8,128)(2,1)S(1)}, u32[]{:S(2)}, u32[]{:S(2)}) collective-permute-start(bf16[2,512,256]{2,1,0:T(8,128)(2,1)S(1)} %range_tail.1.here_ref), channel_id=1, source_target_pairs={{8,0},{16,8},{24,16},{32,24},{40,32},{48,40},{56,48},{64,56},{72,6... | collective-permute-start | bytes 1572872 | tf_op jit(solution)/shard_map/ppermute | solution.py:209

commit v2 on v1

--- a/solution.py
+++ b/solution.py
@@ -160,8 +160,9 @@
     )(sets, refs, previous)
 
 
-def azimuth_kernel(first, weights_ref, here_ref, after_ref, *rest):
+def azimuth_kernel(first, relayed, weights_ref, here_ref, after_ref, *rest):
     out_ref = rest[-1]
+    by_relay = lax.axis_index("az") % 2 == 1
     lines = here_ref.shape[1]
     span = weights_ref.shape[2]
     step = pl.program_id(0)
@@ -169,6 +170,9 @@
         at = pl.ds(pl.multiple_of(step * BLOCK + group * LANES, LANES), LANES)
         here = jnp.concatenate([here_ref[0, :, at], here_ref[1, :, at]], axis=1)
         after = jnp.concatenate([after_ref[0, :, at], after_ref[1, :, at]], axis=1)
+        if relayed:
+            other = jnp.concatenate([rest[0][0, :, at], rest[0][1, :, at]], axis=1)
+            after = jnp.where(by_relay, other, after)
         whole = jnp.concatenate([here, after], axis=0)
         weights = weights_ref[(first + step) * (BLOCK // LANES) + group]
         columns = slice(group * LANES, (group + 1) * LANES)
@@ -185,15 +189,15 @@
 def azimuth_compress(weights, here, after, current, columns, first):
     lines = here.shape[1]
     count = here.shape[2] // BLOCK
-    in_specs = [WHOLE, WHOLE, WHOLE]
-    operands = [weights, here, after]
+    operands = [weights, here, *after]
+    in_specs = [WHOLE] * len(operands)
     aliases = {}
     if current is not None:
+        aliases = {len(operands): 0}
         in_specs.append(ANYWHERE)
         operands.append(current)
-        aliases = {3: 0}
-    return pl.pallas_call(
-        functools.partial(azimuth_kernel, first),
+    return pl.pallas_call(
+        functools.partial(azimuth_kernel, first, len(after) > 1),
         grid=(count,),
         in_specs=in_specs,
         out_specs=pl.BlockSpec((2, lines, BLOCK), lambda i: (0, 0, first + i)),
@@ -226,30 +230,56 @@
     return first, second
 
 
+def relay_routes(az_size):
+    upper = az_size // 2
+    ring = upper // 2
+    at = lambda z, x, core: z * upper + (x % ring) * 2 + core
+    hops = [[], [], []]
+    for z in range(2):
+        for x in range(ring):
+            hops[0].append((at(z, x, 1), at(z, x, 0)))
+            if x == 0 and z == 0:
+                continue
+            to = z if x else z - 1
+            hops[0].append((at(z, x, 0), at(to, x + 1, 1)))
+            hops[1].append((at(to, x + 1, 1), at(to, x + 2, 1)))
+            hops[2].append((at(to, x + 2, 1), at(to, x + 3, 1)))
+    return hops
+
+
 def local(raw, chirp, az_ref, set_index):
     columns = raw.shape[2]
     axes = ("az", "rg")
     first_route, second_route = edge_routes(lax.axis_size("az"), lax.axis_size("rg"))
-    distant = pltpu.with_memory_space_constraint(raw, pltpu.HBM)
+    hops = relay_routes(lax.axis_size("az"))
     first, weights = range_head(
-        distant, pltpu.with_memory_space_constraint(chirp, pltpu.HBM)
+        pltpu.with_memory_space_constraint(raw, pltpu.HBM),
+        pltpu.with_memory_space_constraint(chirp, pltpu.HBM),
     )
-    second, edge = range_compress(raw, weights, first, 1, (2,), True)
-    third, fourth = range_compress(raw, weights, second, 3, (2, 2), False)
-    here = [first, second, third, fourth]
-    after = []
-    for piece in here:
-        after.append(passed_back(piece, "az"))
+    raw, weights = lax.optimization_barrier((raw, weights))
+    turned, second, edge = range_compress(raw, weights, first, 1, (1, 2), True)
+    (third,) = range_compress(raw, weights, second, 4, (3,), False)
+    first_next = passed_back(first, "az")
+    second_next = passed_back(second, "az")
+    third_next = passed_back(third, "az")
     near = lax.ppermute(edge, axes, first_route)
     far = lax.ppermute(near, axes, second_route)
-    here.append(range_tail(raw, weights, near, far))
-    after.append(passed_back(here[-1], "az"))
+    carried = [turned]
+    for hop in hops:
+        carried.append(lax.ppermute(carried[-1], "az", hop))
+    fourth = range_tail(raw, weights, near, far)
+    fourth_next = passed_back(fourth, "az")
     turns = azimuth_weights(set_index, az_ref, third)
     focused = None
-    start = 0
-    for k, piece in enumerate(here):
-        focused = azimuth_compress(turns, piece, after[k], focused, columns, start)
-        start += piece.shape[2] // BLOCK
+    pieces = [
+        (first, [first_next], 0),
+        (second, [second_next], 2),
+        (third, [third_next], 4),
+        (turned, [carried[1], carried[3]], 1),
+        (fourth, [fourth_next], 7),
+    ]
+    for here, after, start in pieces:
+        focused = azimuth_compress(turns, here, after, focused, columns, start)
     return focused
 
 

time: 68.8 us -> 68.7 us (level)
  the two profiles are of different devices: /device:TPU:71 before, /device:TPU:25 now
where the time goes in v2:
time: 68.7 us; the launch traced here: 68.3 us
  Pallas kernels  24.2 us (35%)
  starting transfers between devices  22.6 us (33%)
  waiting for transfers between devices  21.3 us (31%)
    pallas_call x5, Pallas kernels, azimuth_compress(): pl.pallas_call(functools.partial(azimuth_kernel, first, len(after) > 1),...  11.9 us
    ppermute x4, starting transfers between devices, passed_back(): return lax.ppermute(block, axis, [(i + 1, i) for i in range(size - 1)])  10.5 us
    ppermute x1, waiting for transfers between devices, local(): far = lax.ppermute(near, axes, second_route)  9.42 us
    ppermute x3, starting transfers between devices, local(): carried.append(lax.ppermute(carried[-1], 'az', hop))  7.78 us
    ppermute x1, waiting for transfers between devices, local(): near = lax.ppermute(edge, axes, first_route)  6.14 us
    ppermute x3, waiting for transfers between devices, local(): carried.append(lax.ppermute(carried[-1], 'az', hop))  5.77 us
    pallas_call x1, Pallas kernels, azimuth_weights(): pl.pallas_call(azimuth_weights_kernel, grid_spec=pltpu.PrefetchScalarGrid...  4.72 us
    pallas_call x2, Pallas kernels, range_compress(): pl.pallas_call(functools.partial(range_kernel, first, sizes, with_edge),...  3.59 us
  transfers between devices with their start and end apart: 9, of which 3 were waited for; matrix products, arithmetic and copies ran while one was open for 0% of the time, Pallas kernels for 23%

profile of v2, /device:TPU:25, one launch (start us, length us, event | category | flops | bytes accessed | tf_op | source)
XLA Modules:
  0.0 68.3 jit_solution(10536708513265813298)
XLA Ops:
  0.0 3.3 %range_head.1 = (bf16[2,512,256]{2,1,0:T(8,128)(2,1)S(1)}, bf16[1024,512]{1,0:T(8,128)(2,1)S(1)}) custom-call(bf16[2,256]{1,0:T(2,128)(2,1)} %chirp_ref.1, bf16[2,512,2048]{2,1,0:T(8,128)(2,1)} %raw_ref.4), custom_call_target="tpu_custom_call" | custom-call | tf_op jit(solution)/shard_map/range_head/pallas_call | solution.py:57
  3.3 0.0 copy-done
  3.3 1.8 %range_compress.2 = (bf16[2,512,256]{2,1,0:T(8,128)(2,1)S(1)}, bf16[2,512,512]{2,1,0:T(8,128)(2,1)S(1)}, bf16[2,512,256]{2,1,0:T(8,128)(2,1)S(1)}) custom-call(bf16[1024,512]{1,0:T(8,128)(2,1)S(1)} %get-tuple-element.13.weights_ref, bf16[2,512,2048]{2,1,0:T(8,128)(2,1)S(1)} %copy-done, bf16[2,512,256]{2,1,0:T(8,128)(2,1)S(1)} %get-tuple-element.15.rest_0_.here_ref), custom_call_target="tpu_custom_call" | custom-call | tf_op jit(solution)/shard_map/range_compress/pallas_call | solution.py:91
  5.1 1.8 %range_compress.3.previous_ref.here_ref = bf16[2,512,768]{2,1,0:T(8,128)(2,1)S(1)} custom-call(bf16[1024,512]{1,0:T(8,128)(2,1)S(1)} %get-tuple-element.13.weights_ref, bf16[2,512,2048]{2,1,0:T(8,128)(2,1)S(1)} %copy-done, bf16[2,512,512]{2,1,0:T(8,128)(2,1)S(1)} %get-tuple-element.16.rest_0_.here_ref), custom_call_target="tpu_custom_call" | custom-call | tf_op jit(solution)/shard_map/range_compress/pallas_call | solution.py:91
  6.9 0.0 copy-start.1
  6.9 0.0 copy-start.2
  6.9 2.7 %collective-permute-start.6 = (bf16[2,512,768]{2,1,0:T(8,128)(2,1)S(1)}, bf16[2,512,768]{2,1,0:T(8,128)(2,1)S(1)}, u32[]{:S(2)}, u32[]{:S(2)}) collective-permute-start(bf16[2,512,768]{2,1,0:T(8,128)(2,1)S(1)} %range_compress.3.previous_ref.here_ref), channel_id=1, source_target_pairs={{8,0},{16,8},{24,16},{32,24},{40,32},{48,40},{56,48},{64,56},{72,6... | collective-permute-start | bytes 4718600 | tf_op jit(solution)/shard_map/ppermute | solution.py:213
  9.7 1.9 %collective-permute-start.3 = (bf16[2,512,256]{2,1,0:T(8,128)(2,1)S(1)}, bf16[2,512,256]{2,1,0:T(8,128)(2,1)S(1)}, u32[]{:S(2)}, u32[]{:S(2)}) collective-permute-start(bf16[2,512,256]{2,1,0:T(8,128)(2,1)S(1)} %get-tuple-element.18.here_ref), channel_id=1, source_target_pairs={{8,0},{24,16},{16,40},{40,32},{32,56},{56,48},{48,8},{72,64},{64,2... | collective-permute-start | bytes 1572872 | tf_op jit(solution)/shard_map/ppermute | solution.py:269
  11.6 2.4 %collective-permute-start = (bf16[2,512,256]{2,1,0:T(8,128)(2,1)S(1)}, bf16[2,512,256]{2,1,0:T(8,128)(2,1)S(1)}, u32[]{:S(2)}, u32[]{:S(2)}) collective-permute-start(bf16[2,512,256]{2,1,0:T(8,128)(2,1)S(1)} %get-tuple-element.17), channel_id=1, source_target_pairs={{1,0},{2,1},{3,2},{4,71},{5,4},{6,5},{7,6},{9,8},{10,9},{11,10},{1... | collective-permute-start | bytes 1572872 | tf_op jit(solution)/shard_map/ppermute | solution.py:265
  14.0 1.9 %collective-permute-start.7 = (bf16[2,512,512]{2,1,0:T(8,128)(2,1)S(1)}, bf16[2,512,512]{2,1,0:T(8,128)(2,1)S(1)}, u32[]{:S(2)}, u32[]{:S(2)}) collective-permute-start(bf16[2,512,512]{2,1,0:T(8,128)(2,1)S(1)} %get-tuple-element.16.rest_0_.here_ref), channel_id=1, source_target_pairs={{8,0},{16,8},{24,16},{32,24},{40,32},{48,40},{56,48},{64,56},{72,6... | collective-permute-start | bytes 3145736 | tf_op jit(solution)/shard_map/ppermute | solution.py:213
  15.9 5.8 %collective-permute-done.3.after_ref = bf16[2,512,256]{2,1,0:T(8,128)(2,1)S(1)} collective-permute-done((bf16[2,512,256]{2,1,0:T(8,128)(2,1)S(1)}, bf16[2,512,256]{2,1,0:T(8,128)(2,1)S(1)}, u32[]{:S(2)}, u32[]{:S(2)}) %collective-permute-start.3) | collective-permute-done | bytes 524320 | tf_op jit(solution)/shard_map/ppermute | solution.py:269
  21.7 3.4 %collective-permute-start.4 = (bf16[2,512,256]{2,1,0:T(8,128)(2,1)S(1)}, bf16[2,512,256]{2,1,0:T(8,128)(2,1)S(1)}, u32[]{:S(2)}, u32[]{:S(2)}) collective-permute-start(bf16[2,512,256]{2,1,0:T(8,128)(2,1)S(1)} %collective-permute-done.3.after_ref), channel_id=1, source_target_pairs={{40,56},{56,8},{8,24},{24,40},{104,120},{120,72},{72,88},{41,57},{... | collective-permute-start | bytes 1572872 | tf_op jit(solution)/shard_map/ppermute | solution.py:269
  25.1 6.1 %collective-permute-done.near_ref = bf16[2,512,256]{2,1,0:T(8,128)(2,1)S(1)} collective-permute-done((bf16[2,512,256]{2,1,0:T(8,128)(2,1)S(1)}, bf16[2,512,256]{2,1,0:T(8,128)(2,1)S(1)}, u32[]{:S(2)}, u32[]{:S(2)}) %collective-permute-start) | collective-permute-done | bytes 524320 | tf_op jit(solution)/shard_map/ppermute | solution.py:265
  31.2 1.9 %collective-permute-start.1 = (bf16[2,512,256]{2,1,0:T(8,128)(2,1)S(1)}, bf16[2,512,256]{2,1,0:T(8,128)(2,1)S(1)}, u32[]{:S(2)}, u32[]{:S(2)}) collective-permute-start(bf16[2,512,256]{2,1,0:T(8,128)(2,1)S(1)} %collective-permute-done.near_ref), channel_id=1, source_target_pairs={{71,3},{79,11},{87,19},{95,27},{103,35},{111,43},{119,51},{127,59}... | collective-permute-start | bytes 1572872 | tf_op jit(solution)/shard_map/ppermute | solution.py:266
  33.1 2.5 %collective-permute-start.8 = (bf16[2,512,256]{2,1,0:T(8,128)(2,1)S(1)}, bf16[2,512,256]{2,1,0:T(8,128)(2,1)S(1)}, u32[]{:S(2)}, u32[]{:S(2)}) collective-permute-start(bf16[2,512,256]{2,1,0:T(8,128)(2,1)S(1)} %get-tuple-element.15.rest_0_.here_ref), channel_id=1, source_target_pairs={{8,0},{16,8},{24,16},{32,24},{40,32},{48,40},{56,48},{64,56},{72,6... | collective-permute-start | bytes 1572872 | tf_op jit(solution)/shard_map/ppermute | solution.py:213
  35.6 0.0 collective-permute-done.4
  35.6 2.5 %collective-permute-start.5 = (bf16[2,512,256]{2,1,0:T(8,128)(2,1)S(1)}, bf16[2,512,256]{2,1,0:T(8,128)(2,1)S(1)}, u32[]{:S(2)}, u32[]{:S(2)}) collective-permute-start(bf16[2,512,256]{2,1,0:T(8,128)(2,1)S(1)} %collective-permute-done.4), channel_id=1, source_target_pairs={{56,8},{8,24},{24,40},{40,56},{120,72},{72,88},{88,104},{57,9},{9,... | collective-permute-start | bytes 1572872 | tf_op jit(solution)/shard_map/ppermute | solution.py:269
  38.1 9.4 %collective-permute-done.1.far_ref = bf16[2,512,256]{2,1,0:T(8,128)(2,1)S(1)} collective-permute-done((bf16[2,512,256]{2,1,0:T(8,128)(2,1)S(1)}, bf16[2,512,256]{2,1,0:T(8,128)(2,1)S(1)}, u32[]{:S(2)}, u32[]{:S(2)}) %collective-permute-start.1) | collective-permute-done | bytes 524320 | tf_op jit(solution)/shard_map/ppermute | solution.py:266
  47.5 0.7 %range_tail.1.here_ref = bf16[2,512,256]{2,1,0:T(8,128)(2,1)S(1)} custom-call(bf16[1024,512]{1,0:T(8,128)(2,1)S(1)} %get-tuple-element.13.weights_ref, bf16[2,512,2048]{2,1,0:T(8,128)(2,1)S(1)} %copy-done, bf16[2,512,256]{2,1,0:T(8,128)(2,1)S(1)} %collective-permute-done.near_ref, bf16[2,512,256]{2,1,0:T(8,128)(2,1)S(1)} %collective-permute-done.1.far_ref), custom_call_target="tpu_custom_call" | custom-call | tf_op jit(solution)/shard_map/range_tail/pallas_call | solution.py:111
  48.2 3.4 %collective-permute-start.2 = (bf16[2,512,256]{2,1,0:T(8,128)(2,1)S(1)}, bf16[2,512,256]{2,1,0:T(8,128)(2,1)S(1)}, u32[]{:S(2)}, u32[]{:S(2)}) collective-permute-start(bf16[2,512,256]{2,1,0:T(8,128)(2,1)S(1)} %range_tail.1.here_ref), channel_id=1, source_target_pairs={{8,0},{16,8},{24,16},{32,24},{40,32},{48,40},{56,48},{64,56},{72,6... | collective-permute-start | bytes 1572872 | tf_op jit(solution)/shard_map/ppermute | solution.py:213
  51.6 0.0 copy-done.1
  51.6 4.7 %azimuth_weights.1.weights_ref = bf16[16,512,768]{2,1,0:T(8,128)(2,1)S(1)} custom-call(s32[2048]{0:T(1024)S(1)} %copy-done.2, bf16[2,64,512]{2,1,0:T(8,128)(2,1)S(1)} %copy-done.1, bf16[2,512,768]{2,1,0:T(8,128)(2,1)S(1)} %range_compress.3.previous_ref.here_ref), custom_call_target="tpu_custom_call" | custom-call | tf_op jit(solution)/shard_map/azimuth_weights/pallas_call | solution.py:148
  56.4 0.0 collective-permute-done.8.after_ref
  56.4 1.8 %azimuth_compress.5.rest_0_ = bf16[2,512,2048]{2,1,0:T(8,128)(2,1)} custom-call(bf16[16,512,768]{2,1,0:T(8,128)(2,1)S(1)} %azimuth_weights.1.weights_ref, bf16[2,512,256]{2,1,0:T(8,128)(2,1)S(1)} %get-tuple-element.15.rest_0_.here_ref, bf16[2,512,256]{2,1,0:T(8,128)(2,1)S(1)} %collective-permute-done.8.after_ref), custom_call_target="tpu_custom_call" | custom-call | tf_op jit(solution)/shard_map/azimuth_compress/pallas_call | solution.py:199
  58.1 0.0 collective-permute-done.7.after_ref
  58.2 2.8 %azimuth_compress.6.rest_0_ = bf16[2,512,2048]{2,1,0:T(8,128)(2,1)} custom-call(bf16[16,512,768]{2,1,0:T(8,128)(2,1)S(1)} %azimuth_weights.1.weights_ref, bf16[2,512,512]{2,1,0:T(8,128)(2,1)S(1)} %get-tuple-element.16.rest_0_.here_ref, bf16[2,512,512]{2,1,0:T(8,128)(2,1)S(1)} %collective-permute-done.7.after_ref, ...), custom_call_target="tpu_custom_call", output_to_operand_aliasing={{}: (3, {})} | custom-call | tf_op jit(solution)/shard_map/azimuth_compress/pallas_call | solution.py:199
  60.9 0.0 collective-permute-done.6.after_ref
  60.9 3.8 %azimuth_compress.7.rest_1_ = bf16[2,512,2048]{2,1,0:T(8,128)(2,1)} custom-call(bf16[16,512,768]{2,1,0:T(8,128)(2,1)S(1)} %azimuth_weights.1.weights_ref, bf16[2,512,768]{2,1,0:T(8,128)(2,1)S(1)} %range_compress.3.previous_ref.here_ref, bf16[2,512,768]{2,1,0:T(8,128)(2,1)S(1)} %collective-permute-done.6.after_ref, ...), custom_call_target="tpu_custom_call", output_to_operand_aliasing={{}: (3, {})} | custom-call | tf_op jit(solution)/shard_map/azimuth_compress/pallas_call | solution.py:199
  64.7 0.0 collective-permute-done.5.rest_0_
  64.7 1.8 %azimuth_compress.8.rest_0_ = bf16[2,512,2048]{2,1,0:T(8,128)(2,1)} custom-call(bf16[16,512,768]{2,1,0:T(8,128)(2,1)S(1)} %azimuth_weights.1.weights_ref, bf16[2,512,256]{2,1,0:T(8,128)(2,1)S(1)} %get-tuple-element.18.here_ref, bf16[2,512,256]{2,1,0:T(8,128)(2,1)S(1)} %collective-permute-done.3.after_ref, ...), custom_call_target="tpu_custom_call", output_to_operand_aliasing={{}: (4, {})} | custom-call | tf_op jit(solution)/shard_map/azimuth_compress/pallas_call | solution.py:199
  66.5 0.0 collective-permute-done.2.after_ref
  66.5 1.8 %azimuth_compress.9 = bf16[2,512,2048]{2,1,0:T(8,128)(2,1)} custom-call(bf16[16,512,768]{2,1,0:T(8,128)(2,1)S(1)} %azimuth_weights.1.weights_ref, bf16[2,512,256]{2,1,0:T(8,128)(2,1)S(1)} %range_tail.1.here_ref, bf16[2,512,256]{2,1,0:T(8,128)(2,1)S(1)} %collective-permute-done.2.after_ref, ...), custom_call_target="tpu_custom_call", output_to_operand_aliasing={{}: (3, {})} | custom-call | tf_op jit(solution)/shard_map/azimuth_compress/pallas_call | solution.py:199
  (2 shorter events, 0.0 us)
Async XLA Ops:
  0.0 3.3 %copy-start = (bf16[2,512,2048]{2,1,0:T(8,128)(2,1)S(1)}, bf16[2,512,2048]{2,1,0:T(8,128)(2,1)}, u32[]{:S(2)}) copy-start(bf16[2,512,2048]{2,1,0:T(8,128)(2,1)} %raw_ref.4) | copy-start | bytes 12582916
  6.9 44.7 %copy-start.1 = (bf16[2,64,512]{2,1,0:T(8,128)(2,1)S(1)}, bf16[2,64,512]{2,1,0:T(8,128)(2,1)}, u32[]{:S(2)}) copy-start(bf16[2,64,512]{2,1,0:T(8,128)(2,1)} %refs_ref.1) | copy-start | bytes 393220
  6.9 44.7 %copy-start.2 = (s32[2048]{0:T(1024)S(1)}, s32[2048]{0:T(1024)}, u32[]{:S(2)}) copy-start(s32[2048]{0:T(1024)} %sets_ref.1) | copy-start | bytes 24580
  6.9 54.0 %collective-permute-start.6 = (bf16[2,512,768]{2,1,0:T(8,128)(2,1)S(1)}, bf16[2,512,768]{2,1,0:T(8,128)(2,1)S(1)}, u32[]{:S(2)}, u32[]{:S(2)}) collective-permute-start(bf16[2,512,768]{2,1,0:T(8,128)(2,1)S(1)} %range_compress.3.previous_ref.here_ref), channel_id=1, source_target_pairs={{8,0},{16,8},{24,16},{32,24},{40,32},{48,40},{56,48},{64,56},{72,6... | collective-permute-start | bytes 4718600 | tf_op jit(solution)/shard_map/ppermute | solution.py:213
  9.7 12.0 %collective-permute-start.3 = (bf16[2,512,256]{2,1,0:T(8,128)(2,1)S(1)}, bf16[2,512,256]{2,1,0:T(8,128)(2,1)S(1)}, u32[]{:S(2)}, u32[]{:S(2)}) collective-permute-start(bf16[2,512,256]{2,1,0:T(8,128)(2,1)S(1)} %get-tuple-element.18.here_ref), channel_id=1, source_target_pairs={{8,0},{24,16},{16,40},{40,32},{32,56},{56,48},{48,8},{72,64},{64,2... | collective-permute-start | bytes 1572872 | tf_op jit(solution)/shard_map/ppermute | solution.py:269
  11.6 19.6 %collective-permute-start = (bf16[2,512,256]{2,1,0:T(8,128)(2,1)S(1)}, bf16[2,512,256]{2,1,0:T(8,128)(2,1)S(1)}, u32[]{:S(2)}, u32[]{:S(2)}) collective-permute-start(bf16[2,512,256]{2,1,0:T(8,128)(2,1)S(1)} %get-tuple-element.17), channel_id=1, source_target_pairs={{1,0},{2,1},{3,2},{4,71},{5,4},{6,5},{7,6},{9,8},{10,9},{11,10},{1... | collective-permute-start | bytes 1572872 | tf_op jit(solution)/shard_map/ppermute | solution.py:265
  14.0 44.2 %collective-permute-start.7 = (bf16[2,512,512]{2,1,0:T(8,128)(2,1)S(1)}, bf16[2,512,512]{2,1,0:T(8,128)(2,1)S(1)}, u32[]{:S(2)}, u32[]{:S(2)}) collective-permute-start(bf16[2,512,512]{2,1,0:T(8,128)(2,1)S(1)} %get-tuple-element.16.rest_0_.here_ref), channel_id=1, source_target_pairs={{8,0},{16,8},{24,16},{32,24},{40,32},{48,40},{56,48},{64,56},{72,6... | collective-permute-start | bytes 3145736 | tf_op jit(solution)/shard_map/ppermute | solution.py:213
  21.7 14.0 %collective-permute-start.4 = (bf16[2,512,256]{2,1,0:T(8,128)(2,1)S(1)}, bf16[2,512,256]{2,1,0:T(8,128)(2,1)S(1)}, u32[]{:S(2)}, u32[]{:S(2)}) collective-permute-start(bf16[2,512,256]{2,1,0:T(8,128)(2,1)S(1)} %collective-permute-done.3.after_ref), channel_id=1, source_target_pairs={{40,56},{56,8},{8,24},{24,40},{104,120},{120,72},{72,88},{41,57},{... | collective-permute-start | bytes 1572872 | tf_op jit(solution)/shard_map/ppermute | solution.py:269
  31.2 16.3 %collective-permute-start.1 = (bf16[2,512,256]{2,1,0:T(8,128)(2,1)S(1)}, bf16[2,512,256]{2,1,0:T(8,128)(2,1)S(1)}, u32[]{:S(2)}, u32[]{:S(2)}) collective-permute-start(bf16[2,512,256]{2,1,0:T(8,128)(2,1)S(1)} %collective-permute-done.near_ref), channel_id=1, source_target_pairs={{71,3},{79,11},{87,19},{95,27},{103,35},{111,43},{119,51},{127,59}... | collective-permute-start | bytes 1572872 | tf_op jit(solution)/shard_map/ppermute | solution.py:266
  33.1 23.2 %collective-permute-start.8 = (bf16[2,512,256]{2,1,0:T(8,128)(2,1)S(1)}, bf16[2,512,256]{2,1,0:T(8,128)(2,1)S(1)}, u32[]{:S(2)}, u32[]{:S(2)}) collective-permute-start(bf16[2,512,256]{2,1,0:T(8,128)(2,1)S(1)} %get-tuple-element.15.rest_0_.here_ref), channel_id=1, source_target_pairs={{8,0},{16,8},{24,16},{32,24},{40,32},{48,40},{56,48},{64,56},{72,6... | collective-permute-start | bytes 1572872 | tf_op jit(solution)/shard_map/ppermute | solution.py:213
  35.6 29.1 %collective-permute-start.5 = (bf16[2,512,256]{2,1,0:T(8,128)(2,1)S(1)}, bf16[2,512,256]{2,1,0:T(8,128)(2,1)S(1)}, u32[]{:S(2)}, u32[]{:S(2)}) collective-permute-start(bf16[2,512,256]{2,1,0:T(8,128)(2,1)S(1)} %collective-permute-done.4), channel_id=1, source_target_pairs={{56,8},{8,24},{24,40},{40,56},{120,72},{72,88},{88,104},{57,9},{9,... | collective-permute-start | bytes 1572872 | tf_op jit(solution)/shard_map/ppermute | solution.py:269
  48.2 18.3 %collective-permute-start.2 = (bf16[2,512,256]{2,1,0:T(8,128)(2,1)S(1)}, bf16[2,512,256]{2,1,0:T(8,128)(2,1)S(1)}, u32[]{:S(2)}, u32[]{:S(2)}) collective-permute-start(bf16[2,512,256]{2,1,0:T(8,128)(2,1)S(1)} %range_tail.1.here_ref), channel_id=1, source_target_pairs={{8,0},{16,8},{24,16},{32,24},{40,32},{48,40},{56,48},{64,56},{72,6... | collective-permute-start | bytes 1572872 | tf_op jit(solution)/shard_map/ppermute | solution.py:213

commit v3 on v2

v3 whole, which is shorter than its diff:
```python
import functools

import jax
import jax.numpy as jnp
from jax import lax
from jax.experimental import pallas as pl
from jax.experimental.pallas import tpu as pltpu
from jax.sharding import PartitionSpec as P


LANES = 128
BLOCK = 256
TURNS = 4
VMEM_LIMIT = 16 * 1024 * 1024
WHOLE = pl.BlockSpec(memory_space=pltpu.VMEM)
ANYWHERE = pl.BlockSpec(memory_space=pl.ANY)
PARAMS = pltpu.CompilerParams(vmem_limit_bytes=VMEM_LIMIT)


def shifted_rows(row, count):
    wide = jnp.broadcast_to(row, (count, row.shape[1]))
    return pltpu.roll(wide, 0, 1, stride=1, stride_axis=0)


def build_range_weights(chirp_ref, weights_ref):
    filled = jnp.zeros((2, BLOCK), jnp.float32)
    padded = jnp.concatenate([chirp_ref[...].astype(jnp.float32), filled], axis=1)
    real = jnp.transpose(shifted_rows(padded[0:1], BLOCK)).astype(jnp.bfloat16)
    imag = jnp.transpose(shifted_rows(padded[1:2], BLOCK)).astype(jnp.bfloat16)
    half = 2 * BLOCK
    weights_ref[:half, :BLOCK] = real
    weights_ref[:half, BLOCK:] = -imag
    weights_ref[half:, :BLOCK] = imag
    weights_ref[half:, BLOCK:] = real


def correlate(segment, weights_ref):
    product = jnp.dot(segment, weights_ref[...], preferred_element_type=jnp.float32)
    product = product.astype(jnp.bfloat16)
    return product[:, :BLOCK], product[:, BLOCK:]


def block_at(ref, first, count=1):
    return ref.at[:, :, pl.ds(first * BLOCK, count * BLOCK)]


def head_kernel(
    chirp_hbm, raw_hbm, out_ref, edge_ref, kept_ref, weights_ref, chirp_ref, sems
):
    sources = [chirp_hbm, block_at(raw_hbm, 0)]
    targets = [chirp_ref, edge_ref]
    for k in range(kept_ref.shape[2] // BLOCK):
        sources.append(block_at(raw_hbm, k + 1))
        targets.append(block_at(kept_ref, k))
    copies = [
        pltpu.make_async_copy(source, target, sems.at[k])
        for k, (source, target) in enumerate(zip(sources, targets))
    ]
    for copy in copies:
        copy.start()
    copies[0].wait()
    build_range_weights(chirp_ref, weights_ref)
    copies[1].wait()
    copies[2].wait()
    after = kept_ref[:, :, :BLOCK]
    segment = jnp.concatenate([edge_ref[0], after[0], edge_ref[1], after[1]], axis=1)
    out_ref[0], out_ref[1] = correlate(segment, weights_ref)
    for copy in copies[3:]:
        copy.wait()


def range_head(raw, chirp, kept):
    lines = raw.shape[1]
    like = lambda *shape: jax.ShapeDtypeStruct(shape, raw.dtype)
    out_shape = [
        like(2, lines, BLOCK),
        like(2, lines, BLOCK),
        like(2, lines, kept * BLOCK),
        like(4 * BLOCK, 2 * BLOCK),
    ]
    return pl.pallas_call(
        head_kernel,
        in_specs=[ANYWHERE, ANYWHERE],
        out_specs=[WHOLE] * len(out_shape),
        out_shape=out_shape,
        scratch_shapes=[
            pltpu.VMEM(chirp.shape, chirp.dtype),
            pltpu.SemaphoreType.DMA((2 + kept,)),
        ],
        compiler_params=PARAMS,
        name="range_head",
    )(chirp, raw)


def range_blocks(sizes, blocks, weights_ref, outs):
    block = 0
    for out_ref, size in zip(outs, sizes):
        for k in range(size):
            here_ref, here = blocks[block]
            after_ref, after = blocks[block + 1]
            here = slice(here * BLOCK, (here + 1) * BLOCK)
            after = slice(after * BLOCK, (after + 1) * BLOCK)
            parts = []
            for part in range(2):
                parts += [here_ref[part, :, here], after_ref[part, :, after]]
            real, imag = correlate(jnp.concatenate(parts, axis=1), weights_ref)
            columns = slice(k * BLOCK, (k + 1) * BLOCK)
            out_ref[0, :, columns] = real
            out_ref[1, :, columns] = imag
            block += 1


def fetch_kernel(sizes, weights_ref, near_ref, raw_hbm, previous_ref, *refs):
    outs, kept_ref, sems = refs[: len(sizes)], refs[-2], refs[-1]
    count = kept_ref.shape[2] // BLOCK
    total = raw_hbm.shape[2] // BLOCK
    copies = [
        pltpu.make_async_copy(
            block_at(raw_hbm, total - count + k), block_at(kept_ref, k), sems.at[k]
        )
        for k in range(count)
    ]
    for copy in copies:
        copy.start()
    blocks = [(near_ref, k) for k in range(sum(sizes) + 1)]
    range_blocks(sizes, blocks, weights_ref, outs)
    for copy in copies:
        copy.wait()


def range_fetch(raw, weights, near, previous, sizes, kept):
    lines = raw.shape[1]
    widths = [BLOCK * size for size in sizes] + [BLOCK * kept]
    return pl.pallas_call(
        functools.partial(fetch_kernel, sizes),
        in_specs=[WHOLE, WHOLE, ANYWHERE, ANYWHERE],
        out_specs=[WHOLE] * len(widths),
        out_shape=[jax.ShapeDtypeStruct((2, lines, width), raw.dtype) for width in widths],
        scratch_shapes=[pltpu.SemaphoreType.DMA((kept,))],
        compiler_params=PARAMS,
        name="range_fetch",
    )(weights, near, raw, previous)


def range_kernel(size, weights_ref, near_ref, kept_ref, previous_ref, out_ref):
    last = near_ref.shape[2] // BLOCK - 1
    blocks = [(near_ref, last)] + [(kept_ref, k) for k in range(size)]
    range_blocks((size,), blocks, weights_ref, [out_ref])


def range_compress(near, kept, weights, previous, size):
    lines = near.shape[1]
    return pl.pallas_call(
        functools.partial(range_kernel, size),
        in_specs=[WHOLE, WHOLE, WHOLE, ANYWHERE],
        out_specs=WHOLE,
        out_shape=jax.ShapeDtypeStruct((2, lines, BLOCK * size), near.dtype),
        compiler_params=PARAMS,
        name="range_compress",
    )(weights, near, kept, previous)


def tail_kernel(weights_ref, kept_ref, near_ref, far_ref, out_ref):
    crossing = jnp.logical_and(
        lax.axis_index("rg") == lax.axis_size("rg") // 2 - 1,
        lax.axis_index("az") >= lax.axis_size("az") - 2,
    )
    here = kept_ref[:, :, kept_ref.shape[2] - BLOCK :]
    after = jnp.where(crossing, far_ref[...], near_ref[...])
    segment = jnp.concatenate([here[0], after[0], here[1], after[1]], axis=1)
    out_ref[0], out_ref[1] = correlate(segment, weights_ref)


def range_tail(kept, weights, near, far):
    return pl.pallas_call(
        tail_kernel,
        in_specs=[WHOLE] * 4,
        out_specs=WHOLE,
        out_shape=jax.ShapeDtypeStruct((2, kept.shape[1], BLOCK), kept.dtype),
        compiler_params=PARAMS,
        name="range_tail",
    )(weights, kept, near, far)


def azimuth_weights_kernel(sets_ref, refs_ref, previous_ref, weights_ref, wide_ref):
    width = weights_ref.shape[2]
    lead = jnp.zeros((1, LANES), jnp.float32)
    filled = jnp.zeros((1, 2 * BLOCK - LANES), jnp.float32)

    @pl.when(pl.program_id(0) == 0)
    def _():
        wide_ref[...] = refs_ref[...].astype(jnp.float32)

    for k in range(TURNS):
        group = pl.program_id(0) * TURNS + k
        chosen = sets_ref[group * LANES]
        for part in range(2):
            row = wide_ref[part, pl.ds(chosen, 1), :]
            base = shifted_rows(jnp.concatenate([lead, row, filled], axis=1), 8)
            start = part * LANES
            for q in range(0, LANES, 16):
                upper = pltpu.roll(base, q, 1) if q else base
                lower = pltpu.roll(base, q + 8, 1)
                both = jnp.concatenate([upper, lower], axis=0).astype(jnp.bfloat16)
                weights_ref[group, start + q : start + q + 16, :] = both[:, :width]


def azimuth_weights(sets, refs, previous):
    taps = refs.shape[2]
    groups = sets.shape[0] // LANES
    return pl.pallas_call(
        azimuth_weights_kernel,
        grid_spec=pltpu.PrefetchScalarGridSpec(
            num_scalar_prefetch=1,
            grid=(groups // TURNS,),
            in_specs=[WHOLE, ANYWHERE],
            out_specs=WHOLE,
            scratch_shapes=[pltpu.VMEM(refs.shape, jnp.float32)],
        ),
        out_shape=jax.ShapeDtypeStruct((groups, 2 * LANES, taps + BLOCK + LANES), refs.dtype),
        compiler_params=PARAMS,
        name="azimuth_weights",
    )(sets, refs, previous)


def azimuth_kernel(first, relayed, weights_ref, here_ref, after_ref, *rest):
    out_ref = rest[-1]
    by_relay = lax.axis_index("az") % 2 == 1
    lines = here_ref.shape[1]
    span = weights_ref.shape[2] - LANES
    step = pl.program_id(0)
    for group in range(BLOCK // LANES):
        at = pl.ds(pl.multiple_of(step * BLOCK + group * LANES, LANES), LANES)
        here = jnp.concatenate([here_ref[0, :, at], here_ref[1, :, at]], axis=1)
        after = jnp.concatenate([after_ref[0, :, at], after_ref[1, :, at]], axis=1)
        if relayed:
            other = jnp.concatenate([rest[0][0, :, at], rest[0][1, :, at]], axis=1)
            after = jnp.where(by_relay, other, after)
        whole = jnp.concatenate([here, after], axis=0)
        place = (first + step) * (BLOCK // LANES) + group
        weights = jnp.concatenate(
            [
                weights_ref[place, part * LANES : (part + 1) * LANES, lead : lead + span]
                for part in range(2)
                for lead in (LANES, 0)
            ],
            axis=0,
        )
        columns = slice(group * LANES, (group + 1) * LANES)
        for start in range(0, lines, BLOCK):
            product = jnp.dot(
                weights, whole[start : start + span], preferred_element_type=jnp.float32
            )
            real = product[:BLOCK, :LANES] + product[BLOCK:, LANES:]
            imag = product[:BLOCK, LANES:] - product[BLOCK:, :LANES]
            out_ref[0, start : start + BLOCK, columns] = real.astype(out_ref.dtype)
            out_ref[1, start : start + BLOCK, columns] = imag.astype(out_ref.dtype)


def azimuth_compress(weights, here, after, current, columns, first):
    lines = here.shape[1]
    count = here.shape[2] // BLOCK
    operands = [weights, here, *after]
    in_specs = [WHOLE] * len(operands)
    aliases = {}
    if current is not None:
        aliases = {len(operands): 0}
        in_specs.append(ANYWHERE)
        operands.append(current)
    return pl.pallas_call(
        functools.partial(azimuth_kernel, first, len(after) > 1),
        grid=(count,),
        in_specs=in_specs,
        out_specs=pl.BlockSpec((2, lines, BLOCK), lambda i: (0, 0, first + i)),
        out_shape=jax.ShapeDtypeStruct((2, lines, columns), here.dtype),
        input_output_aliases=aliases,
        compiler_params=PARAMS,
        name="azimuth_compress",
    )(*operands)


def passed_back(block, axis):
    size = lax.axis_size(axis)
    return lax.ppermute(block, axis, [(i + 1, i) for i in range(size - 1)])


def edge_routes(az_size, rg_size):
    upper, turn = az_size // 2, rg_size // 2
    flat = lambda i, j: i * rg_size + j
    near, first, second = [], [], []
    for i in range(az_size):
        for j in range(rg_size - 1):
            if j == turn - 1 and i >= az_size - 2:
                first.append((flat(i, turn), flat(i - upper, j)))
                second.append((flat(i - upper, j), flat(i, j)))
            else:
                near.append((flat(i, j + 1), flat(i, j)))
    return near, first, second


def relay_routes(az_size):
    upper = az_size // 2
    ring = upper // 2
    at = lambda z, x, core: z * upper + (x % ring) * 2 + core
    hops = [[], [], []]
    for z in range(2):
        for x in range(ring):
            hops[0].append((at(z, x, 1), at(z, x, 0)))
            if x == 0 and z == 0:
                continue
            to = z if x else z - 1
            hops[0].append((at(z, x, 0), at(to, x + 1, 1)))
            hops[1].append((at(to, x + 1, 1), at(to, x + 2, 1)))
            hops[2].append((at(to, x + 2, 1), at(to, x + 3, 1)))
    return hops


def local(raw, chirp, az_ref, set_index):
    columns = raw.shape[2]
    axes = ("az", "rg")
    near_route, first_route, second_route = edge_routes(lax.axis_size("az"), lax.axis_size("rg"))
    hops = relay_routes(lax.axis_size("az"))
    raw = pltpu.with_memory_space_constraint(raw, pltpu.HBM)
    chirp = pltpu.with_memory_space_constraint(chirp, pltpu.HBM)
    first, edge, near_raw, weights = range_head(raw, chirp, 5)
    turned, second, last_raw = range_fetch(raw, weights, near_raw, first, (1, 3), 2)
    third = range_compress(near_raw, last_raw, weights, second, 2)
    first_next = passed_back(first, "az")
    second_next = passed_back(second, "az")
    third_next = passed_back(third, "az")
    between = lax.ppermute(edge, axes, first_route)
    far = lax.ppermute(between, axes, second_route)
    near = lax.ppermute(edge, axes, near_route)
    carried = [turned]
    for hop in hops:
        carried.append(lax.ppermute(carried[-1], "az", hop))
    fourth = range_tail(last_raw, weights, near, far)
    fourth_next = passed_back(fourth, "az")
    turns = azimuth_weights(set_index, az_ref, third)
    focused = None
    pieces = [
        (first, [first_next], 0),
        (second, [second_next], 2),
        (third, [third_next], 5),
        (turned, [carried[1], carried[3]], 1),
        (fourth, [fourth_next], 7),
    ]
    for here, after, start in pieces:
        focused = azimuth_compress(turns, here, after, focused, columns, start)
    return focused


def solution(mesh):
    in_specs = (P(None, "az", "rg"), P(), P(), P("rg"))
    out_specs = P(None, "az", "rg")
    return jax.shard_map(local, mesh=mesh, in_specs=in_specs, out_specs=out_specs, check_vma=False)
```

time: 68.7 us -> 69.8 us (1.016)
  the two profiles are of different devices: /device:TPU:25 before, /device:TPU:63 now
where the time goes in v3:
time: 69.8 us; the launch traced here: 69.5 us
  starting transfers between devices  30.5 us (44%)
  Pallas kernels  23.4 us (34%)
  waiting for transfers between devices  15.3 us (22%)
    ppermute x4, starting transfers between devices, passed_back(): return lax.ppermute(block, axis, [(i + 1, i) for i in range(size - 1)])  13.1 us
    ppermute x3, starting transfers between devices, local(): carried.append(lax.ppermute(carried[-1], 'az', hop))  13 us
    pallas_call x5, Pallas kernels, azimuth_compress(): pl.pallas_call(functools.partial(azimuth_kernel, first, len(after) > 1),...  11.9 us
    ppermute x1, waiting for transfers between devices, local(): far = lax.ppermute(between, axes, second_route)  11.6 us
    pallas_call x1, Pallas kernels, azimuth_weights(): pl.pallas_call(azimuth_weights_kernel, grid_spec=pltpu.PrefetchScalarGrid...  4.34 us
    pallas_call x1, Pallas kernels, range_fetch(): pl.pallas_call(functools.partial(fetch_kernel, sizes), in_specs=[WHOLE, W...  3.19 us
    ppermute x3, waiting for transfers between devices, local(): carried.append(lax.ppermute(carried[-1], 'az', hop))  2.64 us
    ppermute x1, starting transfers between devices, local(): near = lax.ppermute(edge, axes, near_route)  2.4 us
  transfers between devices with their start and end apart: 10, of which 4 were waited for; matrix products, arithmetic and copies ran while one was open for 0% of the time, Pallas kernels for 24%

profile of v3, /device:TPU:63, one launch (start us, length us, event | category | flops | bytes accessed | tf_op | source)
XLA Modules:
  0.0 69.5 jit_solution(12282790558251771618)
XLA Ops:
  0.0 2.0 %range_head.1 = (bf16[2,512,256]{2,1,0:T(8,128)(2,1)S(1)}, bf16[2,512,256]{2,1,0:T(8,128)(2,1)S(1)}, bf16[2,512,1280]{2,1,0:T(8,128)(2,1)S(1)}, bf16[1024,512]{1,0:T(8,128)(2,1)S(1)}) custom-call(bf16[2,256]{1,0:T(2,128)(2,1)} %chirp_hbm.1, bf16[2,512,2048]{2,1,0:T(8,128)(2,1)} %raw_hbm.3), custom_call_target="tpu_custom_call" | custom-call | tf_op jit(solution)/shard_map/range_head/pallas_call | solution.py:81
  2.0 3.2 %range_fetch.1 = (bf16[2,512,256]{2,1,0:T(8,128)(2,1)S(1)}, bf16[2,512,768]{2,1,0:T(8,128)(2,1)S(1)}, bf16[2,512,512]{2,1,0:T(8,128)(2,1)S(1)}) custom-call(bf16[1024,512]{1,0:T(8,128)(2,1)S(1)} %get-tuple-element.12.weights_ref, bf16[2,512,1280]{2,1,0:T(8,128)(2,1)S(1)} %get-tuple-element.13.near_ref, bf16[2,512,2048]{2,1,0:T(8,128)(2,1)} %raw_hbm.3, ...), custom_call_target="tpu_custom_call" | custom-call | tf_op jit(solution)/shard_map/range_fetch/pallas_call | solution.py:134
  5.2 2.7 %collective-permute-start.8 = (bf16[2,512,768]{2,1,0:T(8,128)(2,1)S(1)}, bf16[2,512,768]{2,1,0:T(8,128)(2,1)S(1)}, u32[]{:S(2)}, u32[]{:S(2)}) collective-permute-start(bf16[2,512,768]{2,1,0:T(8,128)(2,1)S(1)} %get-tuple-element.16.previous_ref.here_ref), channel_id=1, source_target_pairs={{8,0},{16,8},{24,16},{32,24},{40,32},{48,40},{56,48},{64,56},{72,6... | collective-permute-start | bytes 4718600 | tf_op jit(solution)/shard_map/ppermute | solution.py:284
  7.9 2.1 %collective-permute-start.4 = (bf16[2,512,256]{2,1,0:T(8,128)(2,1)S(1)}, bf16[2,512,256]{2,1,0:T(8,128)(2,1)S(1)}, u32[]{:S(2)}, u32[]{:S(2)}) collective-permute-start(bf16[2,512,256]{2,1,0:T(8,128)(2,1)S(1)} %get-tuple-element.18.here_ref), channel_id=1, source_target_pairs={{8,0},{24,16},{16,40},{40,32},{32,56},{56,48},{48,8},{72,64},{64,2... | collective-permute-start | bytes 1572872 | tf_op jit(solution)/shard_map/ppermute | solution.py:336
  10.0 0.7 collective-permute-start.1
  10.7 2.4 %collective-permute-start = (bf16[2,512,256]{2,1,0:T(8,128)(2,1)S(1)}, bf16[2,512,256]{2,1,0:T(8,128)(2,1)S(1)}, u32[]{:S(2)}, u32[]{:S(2)}) collective-permute-start(bf16[2,512,256]{2,1,0:T(8,128)(2,1)S(1)} %get-tuple-element.17), channel_id=1, source_target_pairs={{1,0},{2,1},{3,2},{4,3},{5,4},{6,5},{7,6},{9,8},{10,9},{11,10},{12... | collective-permute-start | bytes 1572872 | tf_op jit(solution)/shard_map/ppermute | solution.py:333
  13.1 0.0 copy-start
  13.1 0.0 copy-start.1
  13.1 1.2 %range_compress.1.previous_ref.here_ref = bf16[2,512,512]{2,1,0:T(8,128)(2,1)S(1)} custom-call(bf16[1024,512]{1,0:T(8,128)(2,1)S(1)} %get-tuple-element.12.weights_ref, bf16[2,512,1280]{2,1,0:T(8,128)(2,1)S(1)} %get-tuple-element.13.near_ref, bf16[2,512,512]{2,1,0:T(8,128)(2,1)S(1)} %get-tuple-element.15.kept_ref, ...), custom_call_target="tpu_custom_call" | custom-call | tf_op jit(solution)/shard_map/range_compress/pallas_call | solution.py:153
  14.4 2.6 %collective-permute-start.7 = (bf16[2,512,512]{2,1,0:T(8,128)(2,1)S(1)}, bf16[2,512,512]{2,1,0:T(8,128)(2,1)S(1)}, u32[]{:S(2)}, u32[]{:S(2)}) collective-permute-start(bf16[2,512,512]{2,1,0:T(8,128)(2,1)S(1)} %range_compress.1.previous_ref.here_ref), channel_id=1, source_target_pairs={{8,0},{16,8},{24,16},{32,24},{40,32},{48,40},{56,48},{64,56},{72,6... | collective-permute-start | bytes 3145736 | tf_op jit(solution)/shard_map/ppermute | solution.py:284
  17.0 1.4 %collective-permute-done.4.after_ref = bf16[2,512,256]{2,1,0:T(8,128)(2,1)S(1)} collective-permute-done((bf16[2,512,256]{2,1,0:T(8,128)(2,1)S(1)}, bf16[2,512,256]{2,1,0:T(8,128)(2,1)S(1)}, u32[]{:S(2)}, u32[]{:S(2)}) %collective-permute-start.4) | collective-permute-done | bytes 524320 | tf_op jit(solution)/shard_map/ppermute | solution.py:336
  18.4 3.2 %collective-permute-start.5 = (bf16[2,512,256]{2,1,0:T(8,128)(2,1)S(1)}, bf16[2,512,256]{2,1,0:T(8,128)(2,1)S(1)}, u32[]{:S(2)}, u32[]{:S(2)}) collective-permute-start(bf16[2,512,256]{2,1,0:T(8,128)(2,1)S(1)} %collective-permute-done.4.after_ref), channel_id=1, source_target_pairs={{40,56},{56,8},{8,24},{24,40},{104,120},{120,72},{72,88},{41,57},{... | collective-permute-start | bytes 1572872 | tf_op jit(solution)/shard_map/ppermute | solution.py:336
  21.6 0.0 collective-permute-done.1
  21.6 1.3 %collective-permute-start.2 = (bf16[2,512,256]{2,1,0:T(8,128)(2,1)S(1)}, bf16[2,512,256]{2,1,0:T(8,128)(2,1)S(1)}, u32[]{:S(2)}, u32[]{:S(2)}) collective-permute-start(bf16[2,512,256]{2,1,0:T(8,128)(2,1)S(1)} %collective-permute-done.1), channel_id=1, source_target_pairs={{51,115},{59,123}} | collective-permute-start | bytes 1572872 | tf_op jit(solution)/shard_map/ppermute | solution.py:332
  22.9 1.1 %collective-permute-done.near_ref = bf16[2,512,256]{2,1,0:T(8,128)(2,1)S(1)} collective-permute-done((bf16[2,512,256]{2,1,0:T(8,128)(2,1)S(1)}, bf16[2,512,256]{2,1,0:T(8,128)(2,1)S(1)}, u32[]{:S(2)}, u32[]{:S(2)}) %collective-permute-start) | collective-permute-done | bytes 524320 | tf_op jit(solution)/shard_map/ppermute | solution.py:333
  24.0 3.1 %collective-permute-start.9 = (bf16[2,512,256]{2,1,0:T(8,128)(2,1)S(1)}, bf16[2,512,256]{2,1,0:T(8,128)(2,1)S(1)}, u32[]{:S(2)}, u32[]{:S(2)}) collective-permute-start(bf16[2,512,256]{2,1,0:T(8,128)(2,1)S(1)} %get-tuple-element.14.previous_ref.here_ref), channel_id=1, source_target_pairs={{8,0},{16,8},{24,16},{32,24},{40,32},{48,40},{56,48},{64,56},{72,6... | collective-permute-start | bytes 1572872 | tf_op jit(solution)/shard_map/ppermute | solution.py:284
  27.1 1.2 %collective-permute-done.5 = bf16[2,512,256]{2,1,0:T(8,128)(2,1)S(1)} collective-permute-done((bf16[2,512,256]{2,1,0:T(8,128)(2,1)S(1)}, bf16[2,512,256]{2,1,0:T(8,128)(2,1)S(1)}, u32[]{:S(2)}, u32[]{:S(2)}) %collective-permute-start.5) | collective-permute-done | bytes 524320 | tf_op jit(solution)/shard_map/ppermute | solution.py:336
  28.3 7.7 %collective-permute-start.6 = (bf16[2,512,256]{2,1,0:T(8,128)(2,1)S(1)}, bf16[2,512,256]{2,1,0:T(8,128)(2,1)S(1)}, u32[]{:S(2)}, u32[]{:S(2)}) collective-permute-start(bf16[2,512,256]{2,1,0:T(8,128)(2,1)S(1)} %collective-permute-done.5), channel_id=1, source_target_pairs={{56,8},{8,24},{24,40},{40,56},{120,72},{72,88},{88,104},{57,9},{9,... | collective-permute-start | bytes 1572872 | tf_op jit(solution)/shard_map/ppermute | solution.py:336
  36.1 11.6 %collective-permute-done.2.far_ref = bf16[2,512,256]{2,1,0:T(8,128)(2,1)S(1)} collective-permute-done((bf16[2,512,256]{2,1,0:T(8,128)(2,1)S(1)}, bf16[2,512,256]{2,1,0:T(8,128)(2,1)S(1)}, u32[]{:S(2)}, u32[]{:S(2)}) %collective-permute-start.2) | collective-permute-done | bytes 524320 | tf_op jit(solution)/shard_map/ppermute | solution.py:332
  47.7 0.7 %range_tail.1.here_ref = bf16[2,512,256]{2,1,0:T(8,128)(2,1)S(1)} custom-call(bf16[1024,512]{1,0:T(8,128)(2,1)S(1)} %get-tuple-element.12.weights_ref, bf16[2,512,512]{2,1,0:T(8,128)(2,1)S(1)} %get-tuple-element.15.kept_ref, bf16[2,512,256]{2,1,0:T(8,128)(2,1)S(1)} %collective-permute-done.near_ref, bf16[2,512,256]{2,1,0:T(8,128)(2,1)S(1)} %collective-permute-done.2.far_ref), custom_call_target="tpu_custom_call" | custom-call | tf_op jit(solution)/shard_map/range_tail/pallas_call | solution.py:175
  48.4 4.8 %collective-permute-start.3 = (bf16[2,512,256]{2,1,0:T(8,128)(2,1)S(1)}, bf16[2,512,256]{2,1,0:T(8,128)(2,1)S(1)}, u32[]{:S(2)}, u32[]{:S(2)}) collective-permute-start(bf16[2,512,256]{2,1,0:T(8,128)(2,1)S(1)} %range_tail.1.here_ref), channel_id=1, source_target_pairs={{8,0},{16,8},{24,16},{32,24},{40,32},{48,40},{56,48},{64,56},{72,6... | collective-permute-start | bytes 1572872 | tf_op jit(solution)/shard_map/ppermute | solution.py:284
  53.2 4.3 %azimuth_weights.1.weights_ref = bf16[16,256,896]{2,1,0:T(8,128)(2,1)S(1)} custom-call(s32[2048]{0:T(1024)S(1)} %copy-done.1, bf16[2,64,512]{2,1,0:T(8,128)(2,1)S(1)} %copy-done, bf16[2,512,512]{2,1,0:T(8,128)(2,1)S(1)} %range_compress.1.previous_ref.here_ref), custom_call_target="tpu_custom_call" | custom-call | tf_op jit(solution)/shard_map/azimuth_weights/pallas_call | solution.py:211
  57.5 0.0 collective-permute-done.9.after_ref
  57.5 1.8 %azimuth_compress.5.rest_0_ = bf16[2,512,2048]{2,1,0:T(8,128)(2,1)} custom-call(bf16[16,256,896]{2,1,0:T(8,128)(2,1)S(1)} %azimuth_weights.1.weights_ref, bf16[2,512,256]{2,1,0:T(8,128)(2,1)S(1)} %get-tuple-element.14.previous_ref.here_ref, bf16[2,512,256]{2,1,0:T(8,128)(2,1)S(1)} %collective-permute-done.9.after_ref), custom_call_target="tpu_custom_call" | custom-call | tf_op jit(solution)/shard_map/azimuth_compress/pallas_call | solution.py:270
  59.3 0.0 collective-permute-done.8.after_ref
  59.3 3.8 %azimuth_compress.6.rest_0_ = bf16[2,512,2048]{2,1,0:T(8,128)(2,1)} custom-call(bf16[16,256,896]{2,1,0:T(8,128)(2,1)S(1)} %azimuth_weights.1.weights_ref, bf16[2,512,768]{2,1,0:T(8,128)(2,1)S(1)} %get-tuple-element.16.previous_ref.here_ref, bf16[2,512,768]{2,1,0:T(8,128)(2,1)S(1)} %collective-permute-done.8.after_ref, ...), custom_call_target="tpu_custom_call", output_to_operand_aliasing={{}: (3, {})} | custom-call | tf_op jit(solution)/shard_map/azimuth_compress/pallas_call | solution.py:270
  63.1 0.0 collective-permute-done.7.after_ref
  63.1 2.8 %azimuth_compress.7.rest_1_ = bf16[2,512,2048]{2,1,0:T(8,128)(2,1)} custom-call(bf16[16,256,896]{2,1,0:T(8,128)(2,1)S(1)} %azimuth_weights.1.weights_ref, bf16[2,512,512]{2,1,0:T(8,128)(2,1)S(1)} %range_compress.1.previous_ref.here_ref, bf16[2,512,512]{2,1,0:T(8,128)(2,1)S(1)} %collective-permute-done.7.after_ref, ...), custom_call_target="tpu_custom_call", output_to_operand_aliasing={{}: (3, {})} | custom-call | tf_op jit(solution)/shard_map/azimuth_compress/pallas_call | solution.py:270
  65.9 0.0 collective-permute-done.6.rest_0_
  65.9 1.8 %azimuth_compress.8.rest_0_ = bf16[2,512,2048]{2,1,0:T(8,128)(2,1)} custom-call(bf16[16,256,896]{2,1,0:T(8,128)(2,1)S(1)} %azimuth_weights.1.weights_ref, bf16[2,512,256]{2,1,0:T(8,128)(2,1)S(1)} %get-tuple-element.18.here_ref, bf16[2,512,256]{2,1,0:T(8,128)(2,1)S(1)} %collective-permute-done.4.after_ref, ...), custom_call_target="tpu_custom_call", output_to_operand_aliasing={{}: (4, {})} | custom-call | tf_op jit(solution)/shard_map/azimuth_compress/pallas_call | solution.py:270
  67.7 0.0 collective-permute-done.3.after_ref
  67.7 1.8 %azimuth_compress.9 = bf16[2,512,2048]{2,1,0:T(8,128)(2,1)} custom-call(bf16[16,256,896]{2,1,0:T(8,128)(2,1)S(1)} %azimuth_weights.1.weights_ref, bf16[2,512,256]{2,1,0:T(8,128)(2,1)S(1)} %range_tail.1.here_ref, bf16[2,512,256]{2,1,0:T(8,128)(2,1)S(1)} %collective-permute-done.3.after_ref, ...), custom_call_target="tpu_custom_call", output_to_operand_aliasing={{}: (3, {})} | custom-call | tf_op jit(solution)/shard_map/azimuth_compress/pallas_call | solution.py:270
  (2 shorter events, 0.0 us)
Async XLA Ops:
  5.2 54.1 %collective-permute-start.8 = (bf16[2,512,768]{2,1,0:T(8,128)(2,1)S(1)}, bf16[2,512,768]{2,1,0:T(8,128)(2,1)S(1)}, u32[]{:S(2)}, u32[]{:S(2)}) collective-permute-start(bf16[2,512,768]{2,1,0:T(8,128)(2,1)S(1)} %get-tuple-element.16.previous_ref.here_ref), channel_id=1, source_target_pairs={{8,0},{16,8},{24,16},{32,24},{40,32},{48,40},{56,48},{64,56},{72,6... | collective-permute-start | bytes 4718600 | tf_op jit(solution)/shard_map/ppermute | solution.py:284
  7.9 10.5 %collective-permute-start.4 = (bf16[2,512,256]{2,1,0:T(8,128)(2,1)S(1)}, bf16[2,512,256]{2,1,0:T(8,128)(2,1)S(1)}, u32[]{:S(2)}, u32[]{:S(2)}) collective-permute-start(bf16[2,512,256]{2,1,0:T(8,128)(2,1)S(1)} %get-tuple-element.18.here_ref), channel_id=1, source_target_pairs={{8,0},{24,16},{16,40},{40,32},{32,56},{56,48},{48,8},{72,64},{64,2... | collective-permute-start | bytes 1572872 | tf_op jit(solution)/shard_map/ppermute | solution.py:336
  10.0 11.6 %collective-permute-start.1 = (bf16[2,512,256]{2,1,0:T(8,128)(2,1)S(1)}, bf16[2,512,256]{2,1,0:T(8,128)(2,1)S(1)}, u32[]{:S(2)}, u32[]{:S(2)}) collective-permute-start(bf16[2,512,256]{2,1,0:T(8,128)(2,1)S(1)} %get-tuple-element.17), channel_id=1, source_target_pairs={{116,51},{124,59}} | collective-permute-start | bytes 1572872 | tf_op jit(solution)/shard_map/ppermute | solution.py:331
  10.7 13.3 %collective-permute-start = (bf16[2,512,256]{2,1,0:T(8,128)(2,1)S(1)}, bf16[2,512,256]{2,1,0:T(8,128)(2,1)S(1)}, u32[]{:S(2)}, u32[]{:S(2)}) collective-permute-start(bf16[2,512,256]{2,1,0:T(8,128)(2,1)S(1)} %get-tuple-element.17), channel_id=1, source_target_pairs={{1,0},{2,1},{3,2},{4,3},{5,4},{6,5},{7,6},{9,8},{10,9},{11,10},{12... | collective-permute-start | bytes 1572872 | tf_op jit(solution)/shard_map/ppermute | solution.py:333
  13.1 40.1 %copy-start = (bf16[2,64,512]{2,1,0:T(8,128)(2,1)S(1)}, bf16[2,64,512]{2,1,0:T(8,128)(2,1)}, u32[]{:S(2)}) copy-start(bf16[2,64,512]{2,1,0:T(8,128)(2,1)} %refs_ref.1) | copy-start | bytes 393220
  13.1 40.1 %copy-start.1 = (s32[2048]{0:T(1024)S(1)}, s32[2048]{0:T(1024)}, u32[]{:S(2)}) copy-start(s32[2048]{0:T(1024)} %sets_ref.1) | copy-start | bytes 24580
  14.4 48.8 %collective-permute-start.7 = (bf16[2,512,512]{2,1,0:T(8,128)(2,1)S(1)}, bf16[2,512,512]{2,1,0:T(8,128)(2,1)S(1)}, u32[]{:S(2)}, u32[]{:S(2)}) collective-permute-start(bf16[2,512,512]{2,1,0:T(8,128)(2,1)S(1)} %range_compress.1.previous_ref.here_ref), channel_id=1, source_target_pairs={{8,0},{16,8},{24,16},{32,24},{40,32},{48,40},{56,48},{64,56},{72,6... | collective-permute-start | bytes 3145736 | tf_op jit(solution)/shard_map/ppermute | solution.py:284
  18.4 9.9 %collective-permute-start.5 = (bf16[2,512,256]{2,1,0:T(8,128)(2,1)S(1)}, bf16[2,512,256]{2,1,0:T(8,128)(2,1)S(1)}, u32[]{:S(2)}, u32[]{:S(2)}) collective-permute-start(bf16[2,512,256]{2,1,0:T(8,128)(2,1)S(1)} %collective-permute-done.4.after_ref), channel_id=1, source_target_pairs={{40,56},{56,8},{8,24},{24,40},{104,120},{120,72},{72,88},{41,57},{... | collective-permute-start | bytes 1572872 | tf_op jit(solution)/shard_map/ppermute | solution.py:336
  21.6 26.1 %collective-permute-start.2 = (bf16[2,512,256]{2,1,0:T(8,128)(2,1)S(1)}, bf16[2,512,256]{2,1,0:T(8,128)(2,1)S(1)}, u32[]{:S(2)}, u32[]{:S(2)}) collective-permute-start(bf16[2,512,256]{2,1,0:T(8,128)(2,1)S(1)} %collective-permute-done.1), channel_id=1, source_target_pairs={{51,115},{59,123}} | collective-permute-start | bytes 1572872 | tf_op jit(solution)/shard_map/ppermute | solution.py:332
  24.0 33.5 %collective-permute-start.9 = (bf16[2,512,256]{2,1,0:T(8,128)(2,1)S(1)}, bf16[2,512,256]{2,1,0:T(8,128)(2,1)S(1)}, u32[]{:S(2)}, u32[]{:S(2)}) collective-permute-start(bf16[2,512,256]{2,1,0:T(8,128)(2,1)S(1)} %get-tuple-element.14.previous_ref.here_ref), channel_id=1, source_target_pairs={{8,0},{16,8},{24,16},{32,24},{40,32},{48,40},{56,48},{64,56},{72,6... | collective-permute-start | bytes 1572872 | tf_op jit(solution)/shard_map/ppermute | solution.py:284
  28.3 37.6 %collective-permute-start.6 = (bf16[2,512,256]{2,1,0:T(8,128)(2,1)S(1)}, bf16[2,512,256]{2,1,0:T(8,128)(2,1)S(1)}, u32[]{:S(2)}, u32[]{:S(2)}) collective-permute-start(bf16[2,512,256]{2,1,0:T(8,128)(2,1)S(1)} %collective-permute-done.5), channel_id=1, source_target_pairs={{56,8},{8,24},{24,40},{40,56},{120,72},{72,88},{88,104},{57,9},{9,... | collective-permute-start | bytes 1572872 | tf_op jit(solution)/shard_map/ppermute | solution.py:336
  48.4 19.3 %collective-permute-start.3 = (bf16[2,512,256]{2,1,0:T(8,128)(2,1)S(1)}, bf16[2,512,256]{2,1,0:T(8,128)(2,1)S(1)}, u32[]{:S(2)}, u32[]{:S(2)}) collective-permute-start(bf16[2,512,256]{2,1,0:T(8,128)(2,1)S(1)} %range_tail.1.here_ref), channel_id=1, source_target_pairs={{8,0},{16,8},{24,16},{32,24},{40,32},{48,40},{56,48},{64,56},{72,6... | collective-permute-start | bytes 1572872 | tf_op jit(solution)/shard_map/ppermute | solution.py:284

commit v4 on v3

--- a/solution.py
+++ b/solution.py
@@ -62,10 +62,9 @@
     build_range_weights(chirp_ref, weights_ref)
     copies[1].wait()
     copies[2].wait()
-    after = kept_ref[:, :, :BLOCK]
-    segment = jnp.concatenate([edge_ref[0], after[0], edge_ref[1], after[1]], axis=1)
-    out_ref[0], out_ref[1] = correlate(segment, weights_ref)
-    for copy in copies[3:]:
+    blocks = [(edge_ref, 0), (kept_ref, 0), (kept_ref, 1)]
+    range_blocks((2,), blocks, weights_ref, [out_ref], lambda k: k == 2 and copies[3].wait())
+    for copy in copies[4:]:
         copy.wait()
 
 
@@ -73,7 +72,7 @@
     lines = raw.shape[1]
     like = lambda *shape: jax.ShapeDtypeStruct(shape, raw.dtype)
     out_shape = [
-        like(2, lines, BLOCK),
+        like(2, lines, 2 * BLOCK),
         like(2, lines, BLOCK),
         like(2, lines, kept * BLOCK),
         like(4 * BLOCK, 2 * BLOCK),
@@ -92,10 +91,11 @@
     )(chirp, raw)
 
 
-def range_blocks(sizes, blocks, weights_ref, outs):
+def range_blocks(sizes, blocks, weights_ref, outs, arrived=lambda k: None):
     block = 0
     for out_ref, size in zip(outs, sizes):
         for k in range(size):
+            arrived(block + 1)
             here_ref, here = blocks[block]
             after_ref, after = blocks[block + 1]
             here = slice(here * BLOCK, (here + 1) * BLOCK)
@@ -122,7 +122,7 @@
     ]
     for copy in copies:
         copy.start()
-    blocks = [(near_ref, k) for k in range(sum(sizes) + 1)]
+    blocks = [(near_ref, k + 1) for k in range(sum(sizes) + 1)]
     range_blocks(sizes, blocks, weights_ref, outs)
     for copy in copies:
         copy.wait()
@@ -142,19 +142,19 @@
     )(weights, near, raw, previous)
 
 
-def range_kernel(size, weights_ref, near_ref, kept_ref, previous_ref, out_ref):
+def range_kernel(sizes, weights_ref, near_ref, kept_ref, previous_ref, *outs):
     last = near_ref.shape[2] // BLOCK - 1
-    blocks = [(near_ref, last)] + [(kept_ref, k) for k in range(size)]
-    range_blocks((size,), blocks, weights_ref, [out_ref])
-
-
-def range_compress(near, kept, weights, previous, size):
+    blocks = [(near_ref, last)] + [(kept_ref, k) for k in range(sum(sizes))]
+    range_blocks(sizes, blocks, weights_ref, outs)
+
+
+def range_compress(near, kept, weights, previous, sizes):
     lines = near.shape[1]
     return pl.pallas_call(
-        functools.partial(range_kernel, size),
+        functools.partial(range_kernel, sizes),
         in_specs=[WHOLE, WHOLE, WHOLE, ANYWHERE],
-        out_specs=WHOLE,
-        out_shape=jax.ShapeDtypeStruct((2, lines, BLOCK * size), near.dtype),
+        out_specs=[WHOLE] * len(sizes),
+        out_shape=[jax.ShapeDtypeStruct((2, lines, BLOCK * size), near.dtype) for size in sizes],
         compiler_params=PARAMS,
         name="range_compress",
     )(weights, near, kept, previous)
@@ -182,27 +182,28 @@
     )(weights, kept, near, far)
 
 
-def azimuth_weights_kernel(sets_ref, refs_ref, previous_ref, weights_ref, wide_ref):
-    width = weights_ref.shape[2]
-    lead = jnp.zeros((1, LANES), jnp.float32)
-    filled = jnp.zeros((1, 2 * BLOCK - LANES), jnp.float32)
+def azimuth_weights_kernel(sets_ref, refs_ref, previous_ref, weights_ref, rows_ref):
+    filled = jnp.zeros((1, LANES), jnp.float32)
 
     @pl.when(pl.program_id(0) == 0)
     def _():
-        wide_ref[...] = refs_ref[...].astype(jnp.float32)
+        chosen = sets_ref[:, :1]
+        shape = (sets_ref.shape[0], refs_ref.shape[1])
+        picks = lax.broadcasted_iota(jnp.int32, shape, 1) == chosen
+        picks = picks.astype(refs_ref.dtype)
+        for part in range(2):
+            rows_ref[part] = jnp.dot(picks, refs_ref[part], preferred_element_type=jnp.float32)
 
     for k in range(TURNS):
         group = pl.program_id(0) * TURNS + k
-        chosen = sets_ref[group * LANES]
         for part in range(2):
-            row = wide_ref[part, pl.ds(chosen, 1), :]
-            base = shifted_rows(jnp.concatenate([lead, row, filled], axis=1), 8)
+            row = rows_ref[part, pl.ds(group, 1), :]
+            base = shifted_rows(jnp.concatenate([row, filled], axis=1), 16)
+            base = base.astype(jnp.bfloat16)
             start = part * LANES
             for q in range(0, LANES, 16):
-                upper = pltpu.roll(base, q, 1) if q else base
-                lower = pltpu.roll(base, q + 8, 1)
-                both = jnp.concatenate([upper, lower], axis=0).astype(jnp.bfloat16)
-                weights_ref[group, start + q : start + q + 16, :] = both[:, :width]
+                both = pltpu.roll(base, q, 1) if q else base
+                weights_ref[group, start + q : start + q + 16, :] = both
 
 
 def azimuth_weights(sets, refs, previous):
@@ -210,24 +211,22 @@
     groups = sets.shape[0] // LANES
     return pl.pallas_call(
         azimuth_weights_kernel,
-        grid_spec=pltpu.PrefetchScalarGridSpec(
-            num_scalar_prefetch=1,
-            grid=(groups // TURNS,),
-            in_specs=[WHOLE, ANYWHERE],
-            out_specs=WHOLE,
-            scratch_shapes=[pltpu.VMEM(refs.shape, jnp.float32)],
-        ),
-        out_shape=jax.ShapeDtypeStruct((groups, 2 * LANES, taps + BLOCK + LANES), refs.dtype),
+        grid=(groups // TURNS,),
+        in_specs=[WHOLE, WHOLE, ANYWHERE],
+        out_specs=WHOLE,
+        out_shape=jax.ShapeDtypeStruct((groups, 2 * LANES, taps + LANES), refs.dtype),
+        scratch_shapes=[pltpu.VMEM((2, groups, taps), jnp.float32)],
         compiler_params=PARAMS,
         name="azimuth_weights",
-    )(sets, refs, previous)
+    )(sets.reshape(groups, LANES), refs, previous)
 
 
 def azimuth_kernel(first, relayed, weights_ref, here_ref, after_ref, *rest):
     out_ref = rest[-1]
     by_relay = lax.axis_index("az") % 2 == 1
     lines = here_ref.shape[1]
-    span = weights_ref.shape[2] - LANES
+    span = weights_ref.shape[2] + LANES
+    filled = jnp.zeros((LANES, LANES), jnp.bfloat16)
     step = pl.program_id(0)
     for group in range(BLOCK // LANES):
         at = pl.ds(pl.multiple_of(step * BLOCK + group * LANES, LANES), LANES)
@@ -238,14 +237,12 @@
             after = jnp.where(by_relay, other, after)
         whole = jnp.concatenate([here, after], axis=0)
         place = (first + step) * (BLOCK // LANES) + group
-        weights = jnp.concatenate(
-            [
-                weights_ref[place, part * LANES : (part + 1) * LANES, lead : lead + span]
-                for part in range(2)
-                for lead in (LANES, 0)
-            ],
-            axis=0,
-        )
+        rows = []
+        for part in range(2):
+            band = weights_ref[place, part * LANES : (part + 1) * LANES]
+            rows.append(jnp.concatenate([band, filled], axis=1))
+            rows.append(jnp.concatenate([filled, band], axis=1))
+        weights = jnp.concatenate(rows, axis=0)
         columns = slice(group * LANES, (group + 1) * LANES)
         for start in range(0, lines, BLOCK):
             product = jnp.dot(
@@ -291,8 +288,9 @@
     for i in range(az_size):
         for j in range(rg_size - 1):
             if j == turn - 1 and i >= az_size - 2:
-                first.append((flat(i, turn), flat(i - upper, j)))
-                second.append((flat(i - upper, j), flat(i, j)))
+                between = flat(upper - 2, j if i % 2 else 0)
+                first.append((flat(i, turn), between))
+                second.append((between, flat(i, j)))
             else:
                 near.append((flat(i, j + 1), flat(i, j)))
     return near, first, second
@@ -322,9 +320,9 @@
     hops = relay_routes(lax.axis_size("az"))
     raw = pltpu.with_memory_space_constraint(raw, pltpu.HBM)
     chirp = pltpu.with_memory_space_constraint(chirp, pltpu.HBM)
-    first, edge, near_raw, weights = range_head(raw, chirp, 5)
-    turned, second, last_raw = range_fetch(raw, weights, near_raw, first, (1, 3), 2)
-    third = range_compress(near_raw, last_raw, weights, second, 2)
+    first, edge, near_raw, weights = range_head(raw, chirp, 3)
+    turned, last_raw = range_fetch(raw, weights, near_raw, first, (1,), 4)
+    second, third = range_compress(near_raw, last_raw, weights, turned, (2, 2))
     first_next = passed_back(first, "az")
     second_next = passed_back(second, "az")
     third_next = passed_back(third, "az")
@@ -340,12 +338,13 @@
     focused = None
     pieces = [
         (first, [first_next], 0),
-        (second, [second_next], 2),
+        (second, [second_next], 3),
         (third, [third_next], 5),
-        (turned, [carried[1], carried[3]], 1),
+        (turned, [carried[1], carried[3]], 2),
         (fourth, [fourth_next], 7),
     ]
-    for here, after, start in pieces:
+    for k in range(5):
+        here, after, start = pieces[k]
         focused = azimuth_compress(turns, here, after, focused, columns, start)
     return focused
 

time: 69.8 us -> 60.4 us (0.87)
  the two profiles are of different devices: /device:TPU:63 before, /device:TPU:71 now
where the time goes in v4:
time: 60.4 us; the launch traced here: 60 us
  Pallas kernels  22.9 us (38%)
  starting transfers between devices  22.2 us (37%)
  waiting for transfers between devices  14.7 us (24%)
    pallas_call x5, Pallas kernels, azimuth_compress(): pl.pallas_call(functools.partial(azimuth_kernel, first, len(after) > 1),...  11.9 us
    ppermute x4, starting transfers between devices, passed_back(): return lax.ppermute(block, axis, [(i + 1, i) for i in range(size - 1)])  8.91 us
    ppermute x3, starting transfers between devices, local(): carried.append(lax.ppermute(carried[-1], 'az', hop))  7.62 us
    ppermute x4, waiting for transfers between devices, passed_back(): return lax.ppermute(block, axis, [(i + 1, i) for i in range(size - 1)])  7.39 us
    ppermute x3, waiting for transfers between devices, local(): carried.append(lax.ppermute(carried[-1], 'az', hop))  7.11 us
    ppermute x1, starting transfers between devices, local(): near = lax.ppermute(edge, axes, near_route)  4.33 us
    pallas_call x1, Pallas kernels, azimuth_weights(): pl.pallas_call(azimuth_weights_kernel, grid=(groups // TURNS,), in_specs=...  3.61 us
    pallas_call x1, Pallas kernels, range_head(): pl.pallas_call(head_kernel, in_specs=[ANYWHERE, ANYWHERE], out_specs=[WHO...  2.69 us
  transfers between devices with their start and end apart: 10, of which 4 were waited for; matrix products, arithmetic and copies ran while one was open for 0% of the time, Pallas kernels for 31%

profile of v4, /device:TPU:71, one launch (start us, length us, event | category | flops | bytes accessed | tf_op | source)
XLA Modules:
  0.0 60.0 jit_solution(4824408111705943849)
XLA Ops:
  0.0 2.7 %range_head.1 = (bf16[2,512,512]{2,1,0:T(8,128)(2,1)S(1)}, bf16[2,512,256]{2,1,0:T(8,128)(2,1)S(1)}, bf16[2,512,768]{2,1,0:T(8,128)(2,1)S(1)}, bf16[1024,512]{1,0:T(8,128)(2,1)S(1)}) custom-call(bf16[2,256]{1,0:T(2,128)(2,1)} %chirp_hbm.1, bf16[2,512,2048]{2,1,0:T(8,128)(2,1)} %raw_hbm.3), custom_call_target="tpu_custom_call" | custom-call | tf_op jit(solution)/shard_map/range_head/pallas_call | solution.py:80
  2.7 0.7 %collective-permute-start.1 = (bf16[2,512,256]{2,1,0:T(8,128)(2,1)S(1)}, bf16[2,512,256]{2,1,0:T(8,128)(2,1)S(1)}, u32[]{:S(2)}, u32[]{:S(2)}) collective-permute-start(bf16[2,512,256]{2,1,0:T(8,128)(2,1)S(1)} %get-tuple-element.19), channel_id=1, source_target_pairs={{116,48},{124,51}} | collective-permute-start | bytes 1572872 | tf_op jit(solution)/shard_map/ppermute | solution.py:329
  3.4 1.6 %range_fetch.1 = (bf16[2,512,256]{2,1,0:T(8,128)(2,1)S(1)}, bf16[2,512,1024]{2,1,0:T(8,128)(2,1)S(1)}) custom-call(bf16[1024,512]{1,0:T(8,128)(2,1)S(1)} %get-tuple-element.13.weights_ref, bf16[2,512,768]{2,1,0:T(8,128)(2,1)S(1)} %get-tuple-element.14.near_ref, bf16[2,512,2048]{2,1,0:T(8,128)(2,1)} %raw_hbm.3, ...), custom_call_target="tpu_custom_call" | custom-call | tf_op jit(solution)/shard_map/range_fetch/pallas_call | solution.py:134
  5.0 2.6 %collective-permute-start.4 = (bf16[2,512,256]{2,1,0:T(8,128)(2,1)S(1)}, bf16[2,512,256]{2,1,0:T(8,128)(2,1)S(1)}, u32[]{:S(2)}, u32[]{:S(2)}) collective-permute-start(bf16[2,512,256]{2,1,0:T(8,128)(2,1)S(1)} %get-tuple-element.17.previous_ref.here_ref), channel_id=1, source_target_pairs={{8,0},{24,16},{16,40},{40,32},{32,56},{56,48},{48,8},{72,64},{64,2... | collective-permute-start | bytes 1572872 | tf_op jit(solution)/shard_map/ppermute | solution.py:334
  7.6 4.3 %collective-permute-start = (bf16[2,512,256]{2,1,0:T(8,128)(2,1)S(1)}, bf16[2,512,256]{2,1,0:T(8,128)(2,1)S(1)}, u32[]{:S(2)}, u32[]{:S(2)}) collective-permute-start(bf16[2,512,256]{2,1,0:T(8,128)(2,1)S(1)} %get-tuple-element.19), channel_id=1, source_target_pairs={{1,0},{2,1},{3,2},{4,3},{5,4},{6,5},{7,6},{9,8},{10,9},{11,10},{12... | collective-permute-start | bytes 1572872 | tf_op jit(solution)/shard_map/ppermute | solution.py:331
  11.9 2.2 %collective-permute-start.9 = (bf16[2,512,512]{2,1,0:T(8,128)(2,1)S(1)}, bf16[2,512,512]{2,1,0:T(8,128)(2,1)S(1)}, u32[]{:S(2)}, u32[]{:S(2)}) collective-permute-start(bf16[2,512,512]{2,1,0:T(8,128)(2,1)S(1)} %get-tuple-element.15.previous_ref.here_ref), channel_id=1, source_target_pairs={{8,0},{16,8},{24,16},{32,24},{40,32},{48,40},{56,48},{64,56},{72,6... | collective-permute-start | bytes 3145736 | tf_op jit(solution)/shard_map/ppermute | solution.py:281
  14.1 0.0 copy-start
  14.1 0.0 copy-start.1
  14.2 2.3 %range_compress.1 = (bf16[2,512,512]{2,1,0:T(8,128)(2,1)S(1)}, bf16[2,512,512]{2,1,0:T(8,128)(2,1)S(1)}) custom-call(bf16[1024,512]{1,0:T(8,128)(2,1)S(1)} %get-tuple-element.13.weights_ref, bf16[2,512,768]{2,1,0:T(8,128)(2,1)S(1)} %get-tuple-element.14.near_ref, bf16[2,512,1024]{2,1,0:T(8,128)(2,1)S(1)} %get-tuple-element.16.kept_ref, ...), custom_call_target="tpu_custom_call" | custom-call | tf_op jit(solution)/shard_map/range_compress/pallas_call | solution.py:153
  16.5 2.0 %collective-permute-start.8 = (bf16[2,512,512]{2,1,0:T(8,128)(2,1)S(1)}, bf16[2,512,512]{2,1,0:T(8,128)(2,1)S(1)}, u32[]{:S(2)}, u32[]{:S(2)}) collective-permute-start(bf16[2,512,512]{2,1,0:T(8,128)(2,1)S(1)} %get-tuple-element.20.here_ref), channel_id=1, source_target_pairs={{8,0},{16,8},{24,16},{32,24},{40,32},{48,40},{56,48},{64,56},{72,6... | collective-permute-start | bytes 3145736 | tf_op jit(solution)/shard_map/ppermute | solution.py:281
  18.5 0.0 collective-permute-done.1
  18.5 2.8 %collective-permute-start.7 = (bf16[2,512,512]{2,1,0:T(8,128)(2,1)S(1)}, bf16[2,512,512]{2,1,0:T(8,128)(2,1)S(1)}, u32[]{:S(2)}, u32[]{:S(2)}) collective-permute-start(bf16[2,512,512]{2,1,0:T(8,128)(2,1)S(1)} %get-tuple-element.18.previous_ref.here_ref), channel_id=1, source_target_pairs={{8,0},{16,8},{24,16},{32,24},{40,32},{48,40},{56,48},{64,56},{72,6... | collective-permute-start | bytes 3145736 | tf_op jit(solution)/shard_map/ppermute | solution.py:281
  21.3 0.0 collective-permute-done.4.after_ref
  21.3 1.9 %collective-permute-start.5 = (bf16[2,512,256]{2,1,0:T(8,128)(2,1)S(1)}, bf16[2,512,256]{2,1,0:T(8,128)(2,1)S(1)}, u32[]{:S(2)}, u32[]{:S(2)}) collective-permute-start(bf16[2,512,256]{2,1,0:T(8,128)(2,1)S(1)} %collective-permute-done.4.after_ref), channel_id=1, source_target_pairs={{40,56},{56,8},{8,24},{24,40},{104,120},{120,72},{72,88},{41,57},{... | collective-permute-start | bytes 1572872 | tf_op jit(solution)/shard_map/ppermute | solution.py:334
  23.3 0.2 collective-permute-done.near_ref
  23.5 0.7 %collective-permute-start.2 = (bf16[2,512,256]{2,1,0:T(8,128)(2,1)S(1)}, bf16[2,512,256]{2,1,0:T(8,128)(2,1)S(1)}, u32[]{:S(2)}, u32[]{:S(2)}) collective-permute-start(bf16[2,512,256]{2,1,0:T(8,128)(2,1)S(1)} %collective-permute-done.1), channel_id=1, source_target_pairs={{48,115},{51,123}} | collective-permute-start | bytes 1572872 | tf_op jit(solution)/shard_map/ppermute | solution.py:330
  24.1 7.1 %collective-permute-done.5 = bf16[2,512,256]{2,1,0:T(8,128)(2,1)S(1)} collective-permute-done((bf16[2,512,256]{2,1,0:T(8,128)(2,1)S(1)}, bf16[2,512,256]{2,1,0:T(8,128)(2,1)S(1)}, u32[]{:S(2)}, u32[]{:S(2)}) %collective-permute-start.5) | collective-permute-done | bytes 524320 | tf_op jit(solution)/shard_map/ppermute | solution.py:334
  31.2 3.1 %collective-permute-start.6 = (bf16[2,512,256]{2,1,0:T(8,128)(2,1)S(1)}, bf16[2,512,256]{2,1,0:T(8,128)(2,1)S(1)}, u32[]{:S(2)}, u32[]{:S(2)}) collective-permute-start(bf16[2,512,256]{2,1,0:T(8,128)(2,1)S(1)} %collective-permute-done.5), channel_id=1, source_target_pairs={{56,8},{8,24},{24,40},{40,56},{120,72},{72,88},{88,104},{57,9},{9,... | collective-permute-start | bytes 1572872 | tf_op jit(solution)/shard_map/ppermute | solution.py:334
  34.4 0.0 collective-permute-done.2.far_ref
  34.4 0.7 %range_tail.1.here_ref = bf16[2,512,256]{2,1,0:T(8,128)(2,1)S(1)} custom-call(bf16[1024,512]{1,0:T(8,128)(2,1)S(1)} %get-tuple-element.13.weights_ref, bf16[2,512,1024]{2,1,0:T(8,128)(2,1)S(1)} %get-tuple-element.16.kept_ref, bf16[2,512,256]{2,1,0:T(8,128)(2,1)S(1)} %collective-permute-done.near_ref, bf16[2,512,256]{2,1,0:T(8,128)(2,1)S(1)} %collective-permute-done.2.far_ref), custom_call_target="tpu_custom_call" | custom-call | tf_op jit(solution)/shard_map/range_tail/pallas_call | solution.py:175
  35.1 1.9 %collective-permute-start.3 = (bf16[2,512,256]{2,1,0:T(8,128)(2,1)S(1)}, bf16[2,512,256]{2,1,0:T(8,128)(2,1)S(1)}, u32[]{:S(2)}, u32[]{:S(2)}) collective-permute-start(bf16[2,512,256]{2,1,0:T(8,128)(2,1)S(1)} %range_tail.1.here_ref), channel_id=1, source_target_pairs={{8,0},{16,8},{24,16},{32,24},{40,32},{48,40},{56,48},{64,56},{72,6... | collective-permute-start | bytes 1572872 | tf_op jit(solution)/shard_map/ppermute | solution.py:281
  37.0 3.6 %azimuth_weights.1.weights_ref = bf16[16,256,640]{2,1,0:T(8,128)(2,1)S(1)} custom-call(s32[16,128]{1,0:T(8,128)S(1)} %bitcast.1, bf16[2,64,512]{2,1,0:T(8,128)(2,1)S(1)} %copy-done, bf16[2,512,512]{2,1,0:T(8,128)(2,1)S(1)} %get-tuple-element.18.previous_ref.here_ref), custom_call_target="tpu_custom_call" | custom-call | tf_op jit(solution)/shard_map/azimuth_weights/pallas_call | solution.py:212
  40.7 0.0 collective-permute-done.9.after_ref
  40.7 2.8 %azimuth_compress.5.rest_0_ = bf16[2,512,2048]{2,1,0:T(8,128)(2,1)} custom-call(bf16[16,256,640]{2,1,0:T(8,128)(2,1)S(1)} %azimuth_weights.1.weights_ref, bf16[2,512,512]{2,1,0:T(8,128)(2,1)S(1)} %get-tuple-element.15.previous_ref.here_ref, bf16[2,512,512]{2,1,0:T(8,128)(2,1)S(1)} %collective-permute-done.9.after_ref), custom_call_target="tpu_custom_call" | custom-call | tf_op jit(solution)/shard_map/azimuth_compress/pallas_call | solution.py:267
  43.5 0.0 collective-permute-done.8.after_ref
  43.5 2.8 %azimuth_compress.6.rest_0_ = bf16[2,512,2048]{2,1,0:T(8,128)(2,1)} custom-call(bf16[16,256,640]{2,1,0:T(8,128)(2,1)S(1)} %azimuth_weights.1.weights_ref, bf16[2,512,512]{2,1,0:T(8,128)(2,1)S(1)} %get-tuple-element.20.here_ref, bf16[2,512,512]{2,1,0:T(8,128)(2,1)S(1)} %collective-permute-done.8.after_ref, ...), custom_call_target="tpu_custom_call", output_to_operand_aliasing={{}: (3, {})} | custom-call | tf_op jit(solution)/shard_map/azimuth_compress/pallas_call | solution.py:267
  46.3 6.3 %collective-permute-done.7.after_ref = bf16[2,512,512]{2,1,0:T(8,128)(2,1)S(1)} collective-permute-done((bf16[2,512,512]{2,1,0:T(8,128)(2,1)S(1)}, bf16[2,512,512]{2,1,0:T(8,128)(2,1)S(1)}, u32[]{:S(2)}, u32[]{:S(2)}) %collective-permute-start.7) | collective-permute-done | bytes 1048608 | tf_op jit(solution)/shard_map/ppermute | solution.py:281
  52.6 2.8 %azimuth_compress.7.rest_1_ = bf16[2,512,2048]{2,1,0:T(8,128)(2,1)} custom-call(bf16[16,256,640]{2,1,0:T(8,128)(2,1)S(1)} %azimuth_weights.1.weights_ref, bf16[2,512,512]{2,1,0:T(8,128)(2,1)S(1)} %get-tuple-element.18.previous_ref.here_ref, bf16[2,512,512]{2,1,0:T(8,128)(2,1)S(1)} %collective-permute-done.7.after_ref, ...), custom_call_target="tpu_custom_call", output_to_operand_aliasing={{}: (3, {})} | custom-call | tf_op jit(solution)/shard_map/azimuth_compress/pallas_call | solution.py:267
  55.4 0.0 collective-permute-done.6.rest_0_
  55.4 1.8 %azimuth_compress.8.rest_0_ = bf16[2,512,2048]{2,1,0:T(8,128)(2,1)} custom-call(bf16[16,256,640]{2,1,0:T(8,128)(2,1)S(1)} %azimuth_weights.1.weights_ref, bf16[2,512,256]{2,1,0:T(8,128)(2,1)S(1)} %get-tuple-element.17.previous_ref.here_ref, bf16[2,512,256]{2,1,0:T(8,128)(2,1)S(1)} %collective-permute-done.4.after_ref, ...), custom_call_target="tpu_custom_call", output_to_operand_aliasing={{}: (4, {})} | custom-call | tf_op jit(solution)/shard_map/azimuth_compress/pallas_call | solution.py:267
  57.2 1.0 %collective-permute-done.3.after_ref = bf16[2,512,256]{2,1,0:T(8,128)(2,1)S(1)} collective-permute-done((bf16[2,512,256]{2,1,0:T(8,128)(2,1)S(1)}, bf16[2,512,256]{2,1,0:T(8,128)(2,1)S(1)}, u32[]{:S(2)}, u32[]{:S(2)}) %collective-permute-start.3) | collective-permute-done | bytes 524320 | tf_op jit(solution)/shard_map/ppermute | solution.py:281
  58.2 1.8 %azimuth_compress.9 = bf16[2,512,2048]{2,1,0:T(8,128)(2,1)} custom-call(bf16[16,256,640]{2,1,0:T(8,128)(2,1)S(1)} %azimuth_weights.1.weights_ref, bf16[2,512,256]{2,1,0:T(8,128)(2,1)S(1)} %range_tail.1.here_ref, bf16[2,512,256]{2,1,0:T(8,128)(2,1)S(1)} %collective-permute-done.3.after_ref, ...), custom_call_target="tpu_custom_call", output_to_operand_aliasing={{}: (3, {})} | custom-call | tf_op jit(solution)/shard_map/azimuth_compress/pallas_call | solution.py:267
  (2 shorter events, 0.0 us)
Async XLA Ops:
  2.7 15.8 %collective-permute-start.1 = (bf16[2,512,256]{2,1,0:T(8,128)(2,1)S(1)}, bf16[2,512,256]{2,1,0:T(8,128)(2,1)S(1)}, u32[]{:S(2)}, u32[]{:S(2)}) collective-permute-start(bf16[2,512,256]{2,1,0:T(8,128)(2,1)S(1)} %get-tuple-element.19), channel_id=1, source_target_pairs={{116,48},{124,51}} | collective-permute-start | bytes 1572872 | tf_op jit(solution)/shard_map/ppermute | solution.py:329
  5.0 16.3 %collective-permute-start.4 = (bf16[2,512,256]{2,1,0:T(8,128)(2,1)S(1)}, bf16[2,512,256]{2,1,0:T(8,128)(2,1)S(1)}, u32[]{:S(2)}, u32[]{:S(2)}) collective-permute-start(bf16[2,512,256]{2,1,0:T(8,128)(2,1)S(1)} %get-tuple-element.17.previous_ref.here_ref), channel_id=1, source_target_pairs={{8,0},{24,16},{16,40},{40,32},{32,56},{56,48},{48,8},{72,64},{64,2... | collective-permute-start | bytes 1572872 | tf_op jit(solution)/shard_map/ppermute | solution.py:334
  7.6 15.9 %collective-permute-start = (bf16[2,512,256]{2,1,0:T(8,128)(2,1)S(1)}, bf16[2,512,256]{2,1,0:T(8,128)(2,1)S(1)}, u32[]{:S(2)}, u32[]{:S(2)}) collective-permute-start(bf16[2,512,256]{2,1,0:T(8,128)(2,1)S(1)} %get-tuple-element.19), channel_id=1, source_target_pairs={{1,0},{2,1},{3,2},{4,3},{5,4},{6,5},{7,6},{9,8},{10,9},{11,10},{12... | collective-permute-start | bytes 1572872 | tf_op jit(solution)/shard_map/ppermute | solution.py:331
  11.9 28.7 %collective-permute-start.9 = (bf16[2,512,512]{2,1,0:T(8,128)(2,1)S(1)}, bf16[2,512,512]{2,1,0:T(8,128)(2,1)S(1)}, u32[]{:S(2)}, u32[]{:S(2)}) collective-permute-start(bf16[2,512,512]{2,1,0:T(8,128)(2,1)S(1)} %get-tuple-element.15.previous_ref.here_ref), channel_id=1, source_target_pairs={{8,0},{16,8},{24,16},{32,24},{40,32},{48,40},{56,48},{64,56},{72,6... | collective-permute-start | bytes 3145736 | tf_op jit(solution)/shard_map/ppermute | solution.py:281
  14.1 22.9 %copy-start = (bf16[2,64,512]{2,1,0:T(8,128)(2,1)S(1)}, bf16[2,64,512]{2,1,0:T(8,128)(2,1)}, u32[]{:S(2)}) copy-start(bf16[2,64,512]{2,1,0:T(8,128)(2,1)} %refs_ref.1) | copy-start | bytes 393220
  14.1 22.9 %copy-start.1 = (s32[2048]{0:T(1024)S(1)}, s32[2048]{0:T(1024)}, u32[]{:S(2)}) copy-start(s32[2048]{0:T(1024)} %param.7) | copy-start | bytes 24580
  16.5 27.0 %collective-permute-start.8 = (bf16[2,512,512]{2,1,0:T(8,128)(2,1)S(1)}, bf16[2,512,512]{2,1,0:T(8,128)(2,1)S(1)}, u32[]{:S(2)}, u32[]{:S(2)}) collective-permute-start(bf16[2,512,512]{2,1,0:T(8,128)(2,1)S(1)} %get-tuple-element.20.here_ref), channel_id=1, source_target_pairs={{8,0},{16,8},{24,16},{32,24},{40,32},{48,40},{56,48},{64,56},{72,6... | collective-permute-start | bytes 3145736 | tf_op jit(solution)/shard_map/ppermute | solution.py:281
  18.5 34.1 %collective-permute-start.7 = (bf16[2,512,512]{2,1,0:T(8,128)(2,1)S(1)}, bf16[2,512,512]{2,1,0:T(8,128)(2,1)S(1)}, u32[]{:S(2)}, u32[]{:S(2)}) collective-permute-start(bf16[2,512,512]{2,1,0:T(8,128)(2,1)S(1)} %get-tuple-element.18.previous_ref.here_ref), channel_id=1, source_target_pairs={{8,0},{16,8},{24,16},{32,24},{40,32},{48,40},{56,48},{64,56},{72,6... | collective-permute-start | bytes 3145736 | tf_op jit(solution)/shard_map/ppermute | solution.py:281
  21.3 9.9 %collective-permute-start.5 = (bf16[2,512,256]{2,1,0:T(8,128)(2,1)S(1)}, bf16[2,512,256]{2,1,0:T(8,128)(2,1)S(1)}, u32[]{:S(2)}, u32[]{:S(2)}) collective-permute-start(bf16[2,512,256]{2,1,0:T(8,128)(2,1)S(1)} %collective-permute-done.4.after_ref), channel_id=1, source_target_pairs={{40,56},{56,8},{8,24},{24,40},{104,120},{120,72},{72,88},{41,57},{... | collective-permute-start | bytes 1572872 | tf_op jit(solution)/shard_map/ppermute | solution.py:334
  23.5 10.9 %collective-permute-start.2 = (bf16[2,512,256]{2,1,0:T(8,128)(2,1)S(1)}, bf16[2,512,256]{2,1,0:T(8,128)(2,1)S(1)}, u32[]{:S(2)}, u32[]{:S(2)}) collective-permute-start(bf16[2,512,256]{2,1,0:T(8,128)(2,1)S(1)} %collective-permute-done.1), channel_id=1, source_target_pairs={{48,115},{51,123}} | collective-permute-start | bytes 1572872 | tf_op jit(solution)/shard_map/ppermute | solution.py:330
  31.2 24.2 %collective-permute-start.6 = (bf16[2,512,256]{2,1,0:T(8,128)(2,1)S(1)}, bf16[2,512,256]{2,1,0:T(8,128)(2,1)S(1)}, u32[]{:S(2)}, u32[]{:S(2)}) collective-permute-start(bf16[2,512,256]{2,1,0:T(8,128)(2,1)S(1)} %collective-permute-done.5), channel_id=1, source_target_pairs={{56,8},{8,24},{24,40},{40,56},{120,72},{72,88},{88,104},{57,9},{9,... | collective-permute-start | bytes 1572872 | tf_op jit(solution)/shard_map/ppermute | solution.py:334
  35.1 23.1 %collective-permute-start.3 = (bf16[2,512,256]{2,1,0:T(8,128)(2,1)S(1)}, bf16[2,512,256]{2,1,0:T(8,128)(2,1)S(1)}, u32[]{:S(2)}, u32[]{:S(2)}) collective-permute-start(bf16[2,512,256]{2,1,0:T(8,128)(2,1)S(1)} %range_tail.1.here_ref), channel_id=1, source_target_pairs={{8,0},{16,8},{24,16},{32,24},{40,32},{48,40},{56,48},{64,56},{72,6... | collective-permute-start | bytes 1572872 | tf_op jit(solution)/shard_map/ppermute | solution.py:281

commit v5 on v4

--- a/solution.py
+++ b/solution.py
@@ -276,6 +276,87 @@
     )(*operands)
 
 
+def turn_rows(weights_ref, place):
+    filled = jnp.zeros((LANES, LANES), jnp.bfloat16)
+    rows = []
+    for part in range(2):
+        band = weights_ref[place, part * LANES : (part + 1) * LANES]
+        rows.append(jnp.concatenate([band, filled], axis=1))
+        rows.append(jnp.concatenate([filled, band], axis=1))
+    return jnp.concatenate(rows, axis=0)
+
+
+def side_by_side(ref, at):
+    return jnp.concatenate([ref[0, :, at], ref[1, :, at]], axis=1)
+
+
+def combined(product):
+    real = product[:BLOCK, :LANES] + product[BLOCK:, LANES:]
+    imag = product[:BLOCK, LANES:] - product[BLOCK:, :LANES]
+    return real, imag
+
+
+def own_kernel(first, weights_ref, here_ref, previous_ref, out_ref):
+    lines = here_ref.shape[1]
+    for group in range(here_ref.shape[2] // LANES):
+        at = slice(group * LANES, (group + 1) * LANES)
+        weights = turn_rows(weights_ref, first * (BLOCK // LANES) + group)
+        here = side_by_side(here_ref, at)
+        for start in range(0, lines, BLOCK):
+            own = here[start:]
+            product = jnp.dot(
+                weights[:, : lines - start], own, preferred_element_type=jnp.float32
+            )
+            real, imag = combined(product)
+            out_ref[0, start : start + BLOCK, at] = real
+            out_ref[1, start : start + BLOCK, at] = imag
+
+
+def azimuth_own(weights, here, previous, first):
+    return pl.pallas_call(
+        functools.partial(own_kernel, first),
+        in_specs=[WHOLE, WHOLE, ANYWHERE],
+        out_specs=WHOLE,
+        out_shape=jax.ShapeDtypeStruct(here.shape, jnp.float32),
+        compiler_params=PARAMS,
+        name="azimuth_own",
+    )(weights, here, previous)
+
+
+def rest_kernel(first, weights_ref, own_ref, after_ref, current_ref, out_ref):
+    lines = after_ref.shape[1]
+    group = pl.program_id(0)
+    at = pl.ds(pl.multiple_of(group * LANES, LANES), LANES)
+    weights = turn_rows(weights_ref, first * (BLOCK // LANES) + group)
+    after = side_by_side(after_ref, at)
+    span = weights.shape[1]
+    for start in range(0, lines, BLOCK):
+        reach = start + span - lines
+        product = jnp.dot(
+            weights[:, span - reach :], after[:reach], preferred_element_type=jnp.float32
+        )
+        real, imag = combined(product)
+        rows = slice(start, start + BLOCK)
+        out_ref[0, rows] = (own_ref[0, rows, at] + real).astype(out_ref.dtype)
+        out_ref[1, rows] = (own_ref[1, rows, at] + imag).astype(out_ref.dtype)
+
+
+def azimuth_rest(weights, own, after, current, first):
+    lines = after.shape[1]
+    groups = after.shape[2] // LANES
+    place = first * (BLOCK // LANES)
+    return pl.pallas_call(
+        functools.partial(rest_kernel, first),
+        grid=(groups,),
+        in_specs=[WHOLE, WHOLE, WHOLE, ANYWHERE],
+        out_specs=pl.BlockSpec((2, lines, LANES), lambda i: (0, 0, place + i)),
+        out_shape=jax.ShapeDtypeStruct(current.shape, current.dtype),
+        input_output_aliases={3: 0},
+        compiler_params=PARAMS,
+        name="azimuth_rest",
+    )(weights, own, after, current)
+
+
 def passed_back(block, axis):
     size = lax.axis_size(axis)
     return lax.ppermute(block, axis, [(i + 1, i) for i in range(size - 1)])
@@ -343,9 +424,12 @@
         (turned, [carried[1], carried[3]], 2),
         (fourth, [fourth_next], 7),
     ]
-    for k in range(5):
+    for k in range(4):
         here, after, start = pieces[k]
         focused = azimuth_compress(turns, here, after, focused, columns, start)
+    here, after, start = pieces[4]
+    own = azimuth_own(turns, here, third, start)
+    focused = azimuth_rest(turns, own, after[0], focused, start)
     return focused
 
 

time: 60.4 us -> 60.1 us (level)
    pallas_call x0 -> x2, Pallas kernels: none -> 2.05 us  [the longest x1 1.47 us: azimuth_rest(): pl.pallas_call(functools.partial(rest_kernel, first), grid=(groups,), in_...]
    pallas_call x5 -> x4, Pallas kernels: 11.9 us -> 10.2 us  [azimuth_compress(): pl.pallas_call(functools.partial(azimuth_kernel, first, len(after) > 1),...]
  transfers between devices with their start and end apart: 10 -> 10, of which waited for: 4 -> 4; matrix products, arithmetic and copies ran while one was open for 0% -> 0% of each run, Pallas kernels for 31% -> 32%
where the time goes in v5:
time: 60.1 us; the launch traced here: 59.7 us
  Pallas kernels  23.1 us (38%)
  starting transfers between devices  22.2 us (37%)
  waiting for transfers between devices  14.1 us (23%)
    pallas_call x4, Pallas kernels, azimuth_compress(): pl.pallas_call(functools.partial(azimuth_kernel, first, len(after) > 1),...  10.2 us
    ppermute x4, starting transfers between devices, passed_back(): return lax.ppermute(block, axis, [(i + 1, i) for i in range(size - 1)])  8.91 us
    ppermute x3, starting transfers between devices, local(): carried.append(lax.ppermute(carried[-1], 'az', hop))  7.62 us
    ppermute x3, waiting for transfers between devices, local(): carried.append(lax.ppermute(carried[-1], 'az', hop))  7.11 us
    ppermute x4, waiting for transfers between devices, passed_back(): return lax.ppermute(block, axis, [(i + 1, i) for i in range(size - 1)])  6.81 us
    ppermute x1, starting transfers between devices, local(): near = lax.ppermute(edge, axes, near_route)  4.33 us
    pallas_call x1, Pallas kernels, azimuth_weights(): pl.pallas_call(azimuth_weights_kernel, grid=(groups // TURNS,), in_specs=...  3.61 us
    pallas_call x1, Pallas kernels, range_head(): pl.pallas_call(head_kernel, in_specs=[ANYWHERE, ANYWHERE], out_specs=[WHO...  2.69 us
  transfers between devices with their start and end apart: 10, of which 4 were waited for; matrix products, arithmetic and copies ran while one was open for 0% of the time, Pallas kernels for 32%

profile of v5, /device:TPU:71, one launch (start us, length us, event | category | flops | bytes accessed | tf_op | source)
XLA Modules:
  0.0 59.7 jit_solution(1680168091115248131)
XLA Ops:
  0.0 2.7 %range_head.1 = (bf16[2,512,512]{2,1,0:T(8,128)(2,1)S(1)}, bf16[2,512,256]{2,1,0:T(8,128)(2,1)S(1)}, bf16[2,512,768]{2,1,0:T(8,128)(2,1)S(1)}, bf16[1024,512]{1,0:T(8,128)(2,1)S(1)}) custom-call(bf16[2,256]{1,0:T(2,128)(2,1)} %chirp_hbm.1, bf16[2,512,2048]{2,1,0:T(8,128)(2,1)} %raw_hbm.3), custom_call_target="tpu_custom_call" | custom-call | tf_op jit(solution)/shard_map/range_head/pallas_call | solution.py:80
  2.7 0.7 %collective-permute-start.1 = (bf16[2,512,256]{2,1,0:T(8,128)(2,1)S(1)}, bf16[2,512,256]{2,1,0:T(8,128)(2,1)S(1)}, u32[]{:S(2)}, u32[]{:S(2)}) collective-permute-start(bf16[2,512,256]{2,1,0:T(8,128)(2,1)S(1)} %get-tuple-element.19), channel_id=1, source_target_pairs={{116,48},{124,51}} | collective-permute-start | bytes 1572872 | tf_op jit(solution)/shard_map/ppermute | solution.py:410
  3.4 1.6 %range_fetch.1 = (bf16[2,512,256]{2,1,0:T(8,128)(2,1)S(1)}, bf16[2,512,1024]{2,1,0:T(8,128)(2,1)S(1)}) custom-call(bf16[1024,512]{1,0:T(8,128)(2,1)S(1)} %get-tuple-element.13.weights_ref, bf16[2,512,768]{2,1,0:T(8,128)(2,1)S(1)} %get-tuple-element.14.near_ref, bf16[2,512,2048]{2,1,0:T(8,128)(2,1)} %raw_hbm.3, ...), custom_call_target="tpu_custom_call" | custom-call | tf_op jit(solution)/shard_map/range_fetch/pallas_call | solution.py:134
  5.0 2.6 %collective-permute-start.4 = (bf16[2,512,256]{2,1,0:T(8,128)(2,1)S(1)}, bf16[2,512,256]{2,1,0:T(8,128)(2,1)S(1)}, u32[]{:S(2)}, u32[]{:S(2)}) collective-permute-start(bf16[2,512,256]{2,1,0:T(8,128)(2,1)S(1)} %get-tuple-element.17.previous_ref.here_ref), channel_id=1, source_target_pairs={{8,0},{24,16},{16,40},{40,32},{32,56},{56,48},{48,8},{72,64},{64,2... | collective-permute-start | bytes 1572872 | tf_op jit(solution)/shard_map/ppermute | solution.py:415
  7.6 4.3 %collective-permute-start = (bf16[2,512,256]{2,1,0:T(8,128)(2,1)S(1)}, bf16[2,512,256]{2,1,0:T(8,128)(2,1)S(1)}, u32[]{:S(2)}, u32[]{:S(2)}) collective-permute-start(bf16[2,512,256]{2,1,0:T(8,128)(2,1)S(1)} %get-tuple-element.19), channel_id=1, source_target_pairs={{1,0},{2,1},{3,2},{4,3},{5,4},{6,5},{7,6},{9,8},{10,9},{11,10},{12... | collective-permute-start | bytes 1572872 | tf_op jit(solution)/shard_map/ppermute | solution.py:412
  11.9 2.2 %collective-permute-start.9 = (bf16[2,512,512]{2,1,0:T(8,128)(2,1)S(1)}, bf16[2,512,512]{2,1,0:T(8,128)(2,1)S(1)}, u32[]{:S(2)}, u32[]{:S(2)}) collective-permute-start(bf16[2,512,512]{2,1,0:T(8,128)(2,1)S(1)} %get-tuple-element.15.previous_ref.here_ref), channel_id=1, source_target_pairs={{8,0},{16,8},{24,16},{32,24},{40,32},{48,40},{56,48},{64,56},{72,6... | collective-permute-start | bytes 3145736 | tf_op jit(solution)/shard_map/ppermute | solution.py:362
  14.1 0.0 copy-start
  14.1 0.0 copy-start.1
  14.2 2.3 %range_compress.1 = (bf16[2,512,512]{2,1,0:T(8,128)(2,1)S(1)}, bf16[2,512,512]{2,1,0:T(8,128)(2,1)S(1)}) custom-call(bf16[1024,512]{1,0:T(8,128)(2,1)S(1)} %get-tuple-element.13.weights_ref, bf16[2,512,768]{2,1,0:T(8,128)(2,1)S(1)} %get-tuple-element.14.near_ref, bf16[2,512,1024]{2,1,0:T(8,128)(2,1)S(1)} %get-tuple-element.16.kept_ref, ...), custom_call_target="tpu_custom_call" | custom-call | tf_op jit(solution)/shard_map/range_compress/pallas_call | solution.py:153
  16.5 2.0 %collective-permute-start.8 = (bf16[2,512,512]{2,1,0:T(8,128)(2,1)S(1)}, bf16[2,512,512]{2,1,0:T(8,128)(2,1)S(1)}, u32[]{:S(2)}, u32[]{:S(2)}) collective-permute-start(bf16[2,512,512]{2,1,0:T(8,128)(2,1)S(1)} %get-tuple-element.20.here_ref), channel_id=1, source_target_pairs={{8,0},{16,8},{24,16},{32,24},{40,32},{48,40},{56,48},{64,56},{72,6... | collective-permute-start | bytes 3145736 | tf_op jit(solution)/shard_map/ppermute | solution.py:362
  18.5 0.0 collective-permute-done.1
  18.5 2.8 %collective-permute-start.7 = (bf16[2,512,512]{2,1,0:T(8,128)(2,1)S(1)}, bf16[2,512,512]{2,1,0:T(8,128)(2,1)S(1)}, u32[]{:S(2)}, u32[]{:S(2)}) collective-permute-start(bf16[2,512,512]{2,1,0:T(8,128)(2,1)S(1)} %get-tuple-element.18.previous_ref.here_ref), channel_id=1, source_target_pairs={{8,0},{16,8},{24,16},{32,24},{40,32},{48,40},{56,48},{64,56},{72,6... | collective-permute-start | bytes 3145736 | tf_op jit(solution)/shard_map/ppermute | solution.py:362
  21.3 0.0 collective-permute-done.4.after_ref
  21.3 1.9 %collective-permute-start.5 = (bf16[2,512,256]{2,1,0:T(8,128)(2,1)S(1)}, bf16[2,512,256]{2,1,0:T(8,128)(2,1)S(1)}, u32[]{:S(2)}, u32[]{:S(2)}) collective-permute-start(bf16[2,512,256]{2,1,0:T(8,128)(2,1)S(1)} %collective-permute-done.4.after_ref), channel_id=1, source_target_pairs={{40,56},{56,8},{8,24},{24,40},{104,120},{120,72},{72,88},{41,57},{... | collective-permute-start | bytes 1572872 | tf_op jit(solution)/shard_map/ppermute | solution.py:415
  23.3 0.2 collective-permute-done.near_ref
  23.5 0.7 %collective-permute-start.2 = (bf16[2,512,256]{2,1,0:T(8,128)(2,1)S(1)}, bf16[2,512,256]{2,1,0:T(8,128)(2,1)S(1)}, u32[]{:S(2)}, u32[]{:S(2)}) collective-permute-start(bf16[2,512,256]{2,1,0:T(8,128)(2,1)S(1)} %collective-permute-done.1), channel_id=1, source_target_pairs={{48,115},{51,123}} | collective-permute-start | bytes 1572872 | tf_op jit(solution)/shard_map/ppermute | solution.py:411
  24.1 7.1 %collective-permute-done.5 = bf16[2,512,256]{2,1,0:T(8,128)(2,1)S(1)} collective-permute-done((bf16[2,512,256]{2,1,0:T(8,128)(2,1)S(1)}, bf16[2,512,256]{2,1,0:T(8,128)(2,1)S(1)}, u32[]{:S(2)}, u32[]{:S(2)}) %collective-permute-start.5) | collective-permute-done | bytes 524320 | tf_op jit(solution)/shard_map/ppermute | solution.py:415
  31.2 3.1 %collective-permute-start.6 = (bf16[2,512,256]{2,1,0:T(8,128)(2,1)S(1)}, bf16[2,512,256]{2,1,0:T(8,128)(2,1)S(1)}, u32[]{:S(2)}, u32[]{:S(2)}) collective-permute-start(bf16[2,512,256]{2,1,0:T(8,128)(2,1)S(1)} %collective-permute-done.5), channel_id=1, source_target_pairs={{56,8},{8,24},{24,40},{40,56},{120,72},{72,88},{88,104},{57,9},{9,... | collective-permute-start | bytes 1572872 | tf_op jit(solution)/shard_map/ppermute | solution.py:415
  34.4 0.0 collective-permute-done.2.far_ref
  34.4 0.7 %range_tail.1.here_ref = bf16[2,512,256]{2,1,0:T(8,128)(2,1)S(1)} custom-call(bf16[1024,512]{1,0:T(8,128)(2,1)S(1)} %get-tuple-element.13.weights_ref, bf16[2,512,1024]{2,1,0:T(8,128)(2,1)S(1)} %get-tuple-element.16.kept_ref, bf16[2,512,256]{2,1,0:T(8,128)(2,1)S(1)} %collective-permute-done.near_ref, bf16[2,512,256]{2,1,0:T(8,128)(2,1)S(1)} %collective-permute-done.2.far_ref), custom_call_target="tpu_custom_call" | custom-call | tf_op jit(solution)/shard_map/range_tail/pallas_call | solution.py:175
  35.1 1.9 %collective-permute-start.3 = (bf16[2,512,256]{2,1,0:T(8,128)(2,1)S(1)}, bf16[2,512,256]{2,1,0:T(8,128)(2,1)S(1)}, u32[]{:S(2)}, u32[]{:S(2)}) collective-permute-start(bf16[2,512,256]{2,1,0:T(8,128)(2,1)S(1)} %range_tail.1.here_ref), channel_id=1, source_target_pairs={{8,0},{16,8},{24,16},{32,24},{40,32},{48,40},{56,48},{64,56},{72,6... | collective-permute-start | bytes 1572872 | tf_op jit(solution)/shard_map/ppermute | solution.py:362
  37.0 3.6 %azimuth_weights.1.weights_ref = bf16[16,256,640]{2,1,0:T(8,128)(2,1)S(1)} custom-call(s32[16,128]{1,0:T(8,128)S(1)} %bitcast.1, bf16[2,64,512]{2,1,0:T(8,128)(2,1)S(1)} %copy-done, bf16[2,512,512]{2,1,0:T(8,128)(2,1)S(1)} %get-tuple-element.18.previous_ref.here_ref), custom_call_target="tpu_custom_call" | custom-call | tf_op jit(solution)/shard_map/azimuth_weights/pallas_call | solution.py:212
  40.7 0.6 azimuth_own.1.own_ref
  41.3 2.8 %azimuth_compress.4.rest_0_ = bf16[2,512,2048]{2,1,0:T(8,128)(2,1)} custom-call(bf16[16,256,640]{2,1,0:T(8,128)(2,1)S(1)} %azimuth_weights.1.weights_ref, bf16[2,512,512]{2,1,0:T(8,128)(2,1)S(1)} %get-tuple-element.15.previous_ref.here_ref, bf16[2,512,512]{2,1,0:T(8,128)(2,1)S(1)} %collective-permute-done.9.after_ref), custom_call_target="tpu_custom_call" | custom-call | tf_op jit(solution)/shard_map/azimuth_compress/pallas_call | solution.py:267
  44.1 0.0 collective-permute-done.8.after_ref
  44.1 2.8 %azimuth_compress.5.rest_0_ = bf16[2,512,2048]{2,1,0:T(8,128)(2,1)} custom-call(bf16[16,256,640]{2,1,0:T(8,128)(2,1)S(1)} %azimuth_weights.1.weights_ref, bf16[2,512,512]{2,1,0:T(8,128)(2,1)S(1)} %get-tuple-element.20.here_ref, bf16[2,512,512]{2,1,0:T(8,128)(2,1)S(1)} %collective-permute-done.8.after_ref, ...), custom_call_target="tpu_custom_call", output_to_operand_aliasing={{}: (3, {})} | custom-call | tf_op jit(solution)/shard_map/azimuth_compress/pallas_call | solution.py:267
  46.9 5.8 %collective-permute-done.7.after_ref = bf16[2,512,512]{2,1,0:T(8,128)(2,1)S(1)} collective-permute-done((bf16[2,512,512]{2,1,0:T(8,128)(2,1)S(1)}, bf16[2,512,512]{2,1,0:T(8,128)(2,1)S(1)}, u32[]{:S(2)}, u32[]{:S(2)}) %collective-permute-start.7) | collective-permute-done | bytes 1048608 | tf_op jit(solution)/shard_map/ppermute | solution.py:362
  52.6 2.8 %azimuth_compress.6.rest_1_ = bf16[2,512,2048]{2,1,0:T(8,128)(2,1)} custom-call(bf16[16,256,640]{2,1,0:T(8,128)(2,1)S(1)} %azimuth_weights.1.weights_ref, bf16[2,512,512]{2,1,0:T(8,128)(2,1)S(1)} %get-tuple-element.18.previous_ref.here_ref, bf16[2,512,512]{2,1,0:T(8,128)(2,1)S(1)} %collective-permute-done.7.after_ref, ...), custom_call_target="tpu_custom_call", output_to_operand_aliasing={{}: (3, {})} | custom-call | tf_op jit(solution)/shard_map/azimuth_compress/pallas_call | solution.py:267
  55.4 0.0 collective-permute-done.6.rest_0_
  55.4 1.8 %azimuth_compress.7.current_ref = bf16[2,512,2048]{2,1,0:T(8,128)(2,1)} custom-call(bf16[16,256,640]{2,1,0:T(8,128)(2,1)S(1)} %azimuth_weights.1.weights_ref, bf16[2,512,256]{2,1,0:T(8,128)(2,1)S(1)} %get-tuple-element.17.previous_ref.here_ref, bf16[2,512,256]{2,1,0:T(8,128)(2,1)S(1)} %collective-permute-done.4.after_ref, ...), custom_call_target="tpu_custom_call", output_to_operand_aliasing={{}: (4, {})} | custom-call | tf_op jit(solution)/shard_map/azimuth_compress/pallas_call | solution.py:267
  57.2 1.0 %collective-permute-done.3.after_ref = bf16[2,512,256]{2,1,0:T(8,128)(2,1)S(1)} collective-permute-done((bf16[2,512,256]{2,1,0:T(8,128)(2,1)S(1)}, bf16[2,512,256]{2,1,0:T(8,128)(2,1)S(1)}, u32[]{:S(2)}, u32[]{:S(2)}) %collective-permute-start.3) | collective-permute-done | bytes 524320 | tf_op jit(solution)/shard_map/ppermute | solution.py:362
  58.2 1.5 %azimuth_rest.1 = bf16[2,512,2048]{2,1,0:T(8,128)(2,1)} custom-call(bf16[16,256,640]{2,1,0:T(8,128)(2,1)S(1)} %azimuth_weights.1.weights_ref, f32[2,512,256]{2,1,0:T(8,128)S(1)} %azimuth_own.1.own_ref, bf16[2,512,256]{2,1,0:T(8,128)(2,1)S(1)} %collective-permute-done.3.after_ref, ...), custom_call_target="tpu_custom_call", output_to_operand_aliasing={{}: (3, {})} | custom-call | tf_op jit(solution)/shard_map/azimuth_rest/pallas_call | solution.py:348
  (3 shorter events, 0.0 us)
Async XLA Ops:
  2.7 15.8 %collective-permute-start.1 = (bf16[2,512,256]{2,1,0:T(8,128)(2,1)S(1)}, bf16[2,512,256]{2,1,0:T(8,128)(2,1)S(1)}, u32[]{:S(2)}, u32[]{:S(2)}) collective-permute-start(bf16[2,512,256]{2,1,0:T(8,128)(2,1)S(1)} %get-tuple-element.19), channel_id=1, source_target_pairs={{116,48},{124,51}} | collective-permute-start | bytes 1572872 | tf_op jit(solution)/shard_map/ppermute | solution.py:410
  5.0 16.3 %collective-permute-start.4 = (bf16[2,512,256]{2,1,0:T(8,128)(2,1)S(1)}, bf16[2,512,256]{2,1,0:T(8,128)(2,1)S(1)}, u32[]{:S(2)}, u32[]{:S(2)}) collective-permute-start(bf16[2,512,256]{2,1,0:T(8,128)(2,1)S(1)} %get-tuple-element.17.previous_ref.here_ref), channel_id=1, source_target_pairs={{8,0},{24,16},{16,40},{40,32},{32,56},{56,48},{48,8},{72,64},{64,2... | collective-permute-start | bytes 1572872 | tf_op jit(solution)/shard_map/ppermute | solution.py:415
  7.6 15.9 %collective-permute-start = (bf16[2,512,256]{2,1,0:T(8,128)(2,1)S(1)}, bf16[2,512,256]{2,1,0:T(8,128)(2,1)S(1)}, u32[]{:S(2)}, u32[]{:S(2)}) collective-permute-start(bf16[2,512,256]{2,1,0:T(8,128)(2,1)S(1)} %get-tuple-element.19), channel_id=1, source_target_pairs={{1,0},{2,1},{3,2},{4,3},{5,4},{6,5},{7,6},{9,8},{10,9},{11,10},{12... | collective-permute-start | bytes 1572872 | tf_op jit(solution)/shard_map/ppermute | solution.py:412
  11.9 29.3 %collective-permute-start.9 = (bf16[2,512,512]{2,1,0:T(8,128)(2,1)S(1)}, bf16[2,512,512]{2,1,0:T(8,128)(2,1)S(1)}, u32[]{:S(2)}, u32[]{:S(2)}) collective-permute-start(bf16[2,512,512]{2,1,0:T(8,128)(2,1)S(1)} %get-tuple-element.15.previous_ref.here_ref), channel_id=1, source_target_pairs={{8,0},{16,8},{24,16},{32,24},{40,32},{48,40},{56,48},{64,56},{72,6... | collective-permute-start | bytes 3145736 | tf_op jit(solution)/shard_map/ppermute | solution.py:362
  14.1 22.9 %copy-start = (bf16[2,64,512]{2,1,0:T(8,128)(2,1)S(1)}, bf16[2,64,512]{2,1,0:T(8,128)(2,1)}, u32[]{:S(2)}) copy-start(bf16[2,64,512]{2,1,0:T(8,128)(2,1)} %refs_ref.1) | copy-start | bytes 393220
  14.1 22.9 %copy-start.1 = (s32[2048]{0:T(1024)S(1)}, s32[2048]{0:T(1024)}, u32[]{:S(2)}) copy-start(s32[2048]{0:T(1024)} %param.7) | copy-start | bytes 24580
  16.5 27.6 %collective-permute-start.8 = (bf16[2,512,512]{2,1,0:T(8,128)(2,1)S(1)}, bf16[2,512,512]{2,1,0:T(8,128)(2,1)S(1)}, u32[]{:S(2)}, u32[]{:S(2)}) collective-permute-start(bf16[2,512,512]{2,1,0:T(8,128)(2,1)S(1)} %get-tuple-element.20.here_ref), channel_id=1, source_target_pairs={{8,0},{16,8},{24,16},{32,24},{40,32},{48,40},{56,48},{64,56},{72,6... | collective-permute-start | bytes 3145736 | tf_op jit(solution)/shard_map/ppermute | solution.py:362
  18.5 34.1 %collective-permute-start.7 = (bf16[2,512,512]{2,1,0:T(8,128)(2,1)S(1)}, bf16[2,512,512]{2,1,0:T(8,128)(2,1)S(1)}, u32[]{:S(2)}, u32[]{:S(2)}) collective-permute-start(bf16[2,512,512]{2,1,0:T(8,128)(2,1)S(1)} %get-tuple-element.18.previous_ref.here_ref), channel_id=1, source_target_pairs={{8,0},{16,8},{24,16},{32,24},{40,32},{48,40},{56,48},{64,56},{72,6... | collective-permute-start | bytes 3145736 | tf_op jit(solution)/shard_map/ppermute | solution.py:362
  21.3 9.9 %collective-permute-start.5 = (bf16[2,512,256]{2,1,0:T(8,128)(2,1)S(1)}, bf16[2,512,256]{2,1,0:T(8,128)(2,1)S(1)}, u32[]{:S(2)}, u32[]{:S(2)}) collective-permute-start(bf16[2,512,256]{2,1,0:T(8,128)(2,1)S(1)} %collective-permute-done.4.after_ref), channel_id=1, source_target_pairs={{40,56},{56,8},{8,24},{24,40},{104,120},{120,72},{72,88},{41,57},{... | collective-permute-start | bytes 1572872 | tf_op jit(solution)/shard_map/ppermute | solution.py:415
  23.5 10.9 %collective-permute-start.2 = (bf16[2,512,256]{2,1,0:T(8,128)(2,1)S(1)}, bf16[2,512,256]{2,1,0:T(8,128)(2,1)S(1)}, u32[]{:S(2)}, u32[]{:S(2)}) collective-permute-start(bf16[2,512,256]{2,1,0:T(8,128)(2,1)S(1)} %collective-permute-done.1), channel_id=1, source_target_pairs={{48,115},{51,123}} | collective-permute-start | bytes 1572872 | tf_op jit(solution)/shard_map/ppermute | solution.py:411
  31.2 24.2 %collective-permute-start.6 = (bf16[2,512,256]{2,1,0:T(8,128)(2,1)S(1)}, bf16[2,512,256]{2,1,0:T(8,128)(2,1)S(1)}, u32[]{:S(2)}, u32[]{:S(2)}) collective-permute-start(bf16[2,512,256]{2,1,0:T(8,128)(2,1)S(1)} %collective-permute-done.5), channel_id=1, source_target_pairs={{56,8},{8,24},{24,40},{40,56},{120,72},{72,88},{88,104},{57,9},{9,... | collective-permute-start | bytes 1572872 | tf_op jit(solution)/shard_map/ppermute | solution.py:415
  35.1 23.1 %collective-permute-start.3 = (bf16[2,512,256]{2,1,0:T(8,128)(2,1)S(1)}, bf16[2,512,256]{2,1,0:T(8,128)(2,1)S(1)}, u32[]{:S(2)}, u32[]{:S(2)}) collective-permute-start(bf16[2,512,256]{2,1,0:T(8,128)(2,1)S(1)} %range_tail.1.here_ref), channel_id=1, source_target_pairs={{8,0},{16,8},{24,16},{32,24},{40,32},{48,40},{56,48},{64,56},{72,6... | collective-permute-start | bytes 1572872 | tf_op jit(solution)/shard_map/ppermute | solution.py:362

commit v6 on v5

--- a/solution.py
+++ b/solution.py
@@ -23,15 +23,30 @@
 
 
 def build_range_weights(chirp_ref, weights_ref):
+    half = 2 * BLOCK
     filled = jnp.zeros((2, BLOCK), jnp.float32)
     padded = jnp.concatenate([chirp_ref[...].astype(jnp.float32), filled], axis=1)
-    real = jnp.transpose(shifted_rows(padded[0:1], BLOCK)).astype(jnp.bfloat16)
-    imag = jnp.transpose(shifted_rows(padded[1:2], BLOCK)).astype(jnp.bfloat16)
-    half = 2 * BLOCK
-    weights_ref[:half, :BLOCK] = real
-    weights_ref[:half, BLOCK:] = -imag
-    weights_ref[half:, :BLOCK] = imag
-    weights_ref[half:, BLOCK:] = real
+    empty = jnp.zeros((LANES, LANES), jnp.bfloat16)
+    tiles = []
+    for part in range(2):
+        wide = shifted_rows(padded[part : part + 1], LANES)
+        near = [
+            jnp.transpose(wide[:, d * LANES : (d + 1) * LANES]).astype(jnp.bfloat16)
+            for d in range(half // LANES - 1)
+        ]
+        tiles.append(near)
+    real, imag = tiles
+    for i in range(half // LANES):
+        upper = slice(i * LANES, (i + 1) * LANES)
+        lower = slice(half + i * LANES, half + (i + 1) * LANES)
+        for j in range(BLOCK // LANES):
+            left = slice(j * LANES, (j + 1) * LANES)
+            right = slice(BLOCK + j * LANES, BLOCK + (j + 1) * LANES)
+            inside = 0 <= i - j < len(real)
+            weights_ref[upper, left] = real[i - j] if inside else empty
+            weights_ref[lower, right] = real[i - j] if inside else empty
+            weights_ref[upper, right] = -imag[i - j] if inside else empty
+            weights_ref[lower, left] = imag[i - j] if inside else empty
 
 
 def correlate(segment, weights_ref):
@@ -56,9 +71,11 @@
         pltpu.make_async_copy(source, target, sems.at[k])
         for k, (source, target) in enumerate(zip(sources, targets))
     ]
-    for copy in copies:
+    for copy in copies[:3]:
         copy.start()
     copies[0].wait()
+    for copy in copies[3:]:
+        copy.start()
     build_range_weights(chirp_ref, weights_ref)
     copies[1].wait()
     copies[2].wait()
@@ -325,31 +342,28 @@
 
 def rest_kernel(first, weights_ref, own_ref, after_ref, current_ref, out_ref):
     lines = after_ref.shape[1]
-    group = pl.program_id(0)
-    at = pl.ds(pl.multiple_of(group * LANES, LANES), LANES)
-    weights = turn_rows(weights_ref, first * (BLOCK // LANES) + group)
-    after = side_by_side(after_ref, at)
-    span = weights.shape[1]
-    for start in range(0, lines, BLOCK):
-        reach = start + span - lines
-        product = jnp.dot(
-            weights[:, span - reach :], after[:reach], preferred_element_type=jnp.float32
-        )
-        real, imag = combined(product)
-        rows = slice(start, start + BLOCK)
-        out_ref[0, rows] = (own_ref[0, rows, at] + real).astype(out_ref.dtype)
-        out_ref[1, rows] = (own_ref[1, rows, at] + imag).astype(out_ref.dtype)
+    for group in range(after_ref.shape[2] // LANES):
+        at = slice(group * LANES, (group + 1) * LANES)
+        weights = turn_rows(weights_ref, first * (BLOCK // LANES) + group)
+        after = side_by_side(after_ref, at)
+        span = weights.shape[1]
+        for start in range(0, lines, BLOCK):
+            reach = start + span - lines
+            product = jnp.dot(
+                weights[:, span - reach :], after[:reach], preferred_element_type=jnp.float32
+            )
+            real, imag = combined(product)
+            rows = slice(start, start + BLOCK)
+            out_ref[0, rows, at] = (own_ref[0, rows, at] + real).astype(out_ref.dtype)
+            out_ref[1, rows, at] = (own_ref[1, rows, at] + imag).astype(out_ref.dtype)
 
 
 def azimuth_rest(weights, own, after, current, first):
-    lines = after.shape[1]
-    groups = after.shape[2] // LANES
-    place = first * (BLOCK // LANES)
     return pl.pallas_call(
         functools.partial(rest_kernel, first),
-        grid=(groups,),
+        grid=(1,),
         in_specs=[WHOLE, WHOLE, WHOLE, ANYWHERE],
-        out_specs=pl.BlockSpec((2, lines, LANES), lambda i: (0, 0, place + i)),
+        out_specs=pl.BlockSpec(after.shape, lambda i: (0, 0, first)),
         out_shape=jax.ShapeDtypeStruct(current.shape, current.dtype),
         input_output_aliases={3: 0},
         compiler_params=PARAMS,

time: 60.1 us -> 60 us (level)
  no operation moved by 1% of the time
where the time goes in v6:
time: 60 us; the launch traced here: 59.6 us
  Pallas kernels  23 us (38%)
  starting transfers between devices  22.2 us (37%)
  waiting for transfers between devices  14.1 us (24%)
    pallas_call x4, Pallas kernels, azimuth_compress(): pl.pallas_call(functools.partial(azimuth_kernel, first, len(after) > 1),...  10.2 us
    ppermute x4, starting transfers between devices, passed_back(): return lax.ppermute(block, axis, [(i + 1, i) for i in range(size - 1)])  8.91 us
    ppermute x3, starting transfers between devices, local(): carried.append(lax.ppermute(carried[-1], 'az', hop))  7.62 us
    ppermute x3, waiting for transfers between devices, local(): carried.append(lax.ppermute(carried[-1], 'az', hop))  7.11 us
    ppermute x4, waiting for transfers between devices, passed_back(): return lax.ppermute(block, axis, [(i + 1, i) for i in range(size - 1)])  6.81 us
    ppermute x1, starting transfers between devices, local(): near = lax.ppermute(edge, axes, near_route)  4.33 us
    pallas_call x1, Pallas kernels, azimuth_weights(): pl.pallas_call(azimuth_weights_kernel, grid=(groups // TURNS,), in_specs=...  3.61 us
    pallas_call x1, Pallas kernels, range_head(): pl.pallas_call(head_kernel, in_specs=[ANYWHERE, ANYWHERE], out_specs=[WHO...  2.69 us
  transfers between devices with their start and end apart: 10, of which 4 were waited for; matrix products, arithmetic and copies ran while one was open for 0% of the time, Pallas kernels for 32%

profile of v6, /device:TPU:71, one launch (start us, length us, event | category | flops | bytes accessed | tf_op | source)
XLA Modules:
  0.0 59.6 jit_solution(12457318574255095471)
XLA Ops:
  0.0 2.7 %range_head.1 = (bf16[2,512,512]{2,1,0:T(8,128)(2,1)S(1)}, bf16[2,512,256]{2,1,0:T(8,128)(2,1)S(1)}, bf16[2,512,768]{2,1,0:T(8,128)(2,1)S(1)}, bf16[1024,512]{1,0:T(8,128)(2,1)S(1)}) custom-call(bf16[2,256]{1,0:T(2,128)(2,1)} %chirp_hbm.1, bf16[2,512,2048]{2,1,0:T(8,128)(2,1)} %raw_hbm.3), custom_call_target="tpu_custom_call" | custom-call | tf_op jit(solution)/shard_map/range_head/pallas_call | solution.py:97
  2.7 0.7 %collective-permute-start.1 = (bf16[2,512,256]{2,1,0:T(8,128)(2,1)S(1)}, bf16[2,512,256]{2,1,0:T(8,128)(2,1)S(1)}, u32[]{:S(2)}, u32[]{:S(2)}) collective-permute-start(bf16[2,512,256]{2,1,0:T(8,128)(2,1)S(1)} %get-tuple-element.19), channel_id=1, source_target_pairs={{116,48},{124,51}} | collective-permute-start | bytes 1572872 | tf_op jit(solution)/shard_map/ppermute | solution.py:424
  3.4 1.6 %range_fetch.1 = (bf16[2,512,256]{2,1,0:T(8,128)(2,1)S(1)}, bf16[2,512,1024]{2,1,0:T(8,128)(2,1)S(1)}) custom-call(bf16[1024,512]{1,0:T(8,128)(2,1)S(1)} %get-tuple-element.13.weights_ref, bf16[2,512,768]{2,1,0:T(8,128)(2,1)S(1)} %get-tuple-element.14.near_ref, bf16[2,512,2048]{2,1,0:T(8,128)(2,1)} %raw_hbm.3, ...), custom_call_target="tpu_custom_call" | custom-call | tf_op jit(solution)/shard_map/range_fetch/pallas_call | solution.py:151
  5.0 2.6 %collective-permute-start.4 = (bf16[2,512,256]{2,1,0:T(8,128)(2,1)S(1)}, bf16[2,512,256]{2,1,0:T(8,128)(2,1)S(1)}, u32[]{:S(2)}, u32[]{:S(2)}) collective-permute-start(bf16[2,512,256]{2,1,0:T(8,128)(2,1)S(1)} %get-tuple-element.17.previous_ref.here_ref), channel_id=1, source_target_pairs={{8,0},{24,16},{16,40},{40,32},{32,56},{56,48},{48,8},{72,64},{64,2... | collective-permute-start | bytes 1572872 | tf_op jit(solution)/shard_map/ppermute | solution.py:429
  7.6 4.3 %collective-permute-start = (bf16[2,512,256]{2,1,0:T(8,128)(2,1)S(1)}, bf16[2,512,256]{2,1,0:T(8,128)(2,1)S(1)}, u32[]{:S(2)}, u32[]{:S(2)}) collective-permute-start(bf16[2,512,256]{2,1,0:T(8,128)(2,1)S(1)} %get-tuple-element.19), channel_id=1, source_target_pairs={{1,0},{2,1},{3,2},{4,3},{5,4},{6,5},{7,6},{9,8},{10,9},{11,10},{12... | collective-permute-start | bytes 1572872 | tf_op jit(solution)/shard_map/ppermute | solution.py:426
  11.9 2.2 %collective-permute-start.9 = (bf16[2,512,512]{2,1,0:T(8,128)(2,1)S(1)}, bf16[2,512,512]{2,1,0:T(8,128)(2,1)S(1)}, u32[]{:S(2)}, u32[]{:S(2)}) collective-permute-start(bf16[2,512,512]{2,1,0:T(8,128)(2,1)S(1)} %get-tuple-element.15.previous_ref.here_ref), channel_id=1, source_target_pairs={{8,0},{16,8},{24,16},{32,24},{40,32},{48,40},{56,48},{64,56},{72,6... | collective-permute-start | bytes 3145736 | tf_op jit(solution)/shard_map/ppermute | solution.py:376
  14.1 0.0 copy-start
  14.1 0.0 copy-start.1
  14.2 2.3 %range_compress.1 = (bf16[2,512,512]{2,1,0:T(8,128)(2,1)S(1)}, bf16[2,512,512]{2,1,0:T(8,128)(2,1)S(1)}) custom-call(bf16[1024,512]{1,0:T(8,128)(2,1)S(1)} %get-tuple-element.13.weights_ref, bf16[2,512,768]{2,1,0:T(8,128)(2,1)S(1)} %get-tuple-element.14.near_ref, bf16[2,512,1024]{2,1,0:T(8,128)(2,1)S(1)} %get-tuple-element.16.kept_ref, ...), custom_call_target="tpu_custom_call" | custom-call | tf_op jit(solution)/shard_map/range_compress/pallas_call | solution.py:170
  16.5 2.0 %collective-permute-start.8 = (bf16[2,512,512]{2,1,0:T(8,128)(2,1)S(1)}, bf16[2,512,512]{2,1,0:T(8,128)(2,1)S(1)}, u32[]{:S(2)}, u32[]{:S(2)}) collective-permute-start(bf16[2,512,512]{2,1,0:T(8,128)(2,1)S(1)} %get-tuple-element.20.here_ref), channel_id=1, source_target_pairs={{8,0},{16,8},{24,16},{32,24},{40,32},{48,40},{56,48},{64,56},{72,6... | collective-permute-start | bytes 3145736 | tf_op jit(solution)/shard_map/ppermute | solution.py:376
  18.5 0.0 collective-permute-done.1
  18.5 2.8 %collective-permute-start.7 = (bf16[2,512,512]{2,1,0:T(8,128)(2,1)S(1)}, bf16[2,512,512]{2,1,0:T(8,128)(2,1)S(1)}, u32[]{:S(2)}, u32[]{:S(2)}) collective-permute-start(bf16[2,512,512]{2,1,0:T(8,128)(2,1)S(1)} %get-tuple-element.18.previous_ref.here_ref), channel_id=1, source_target_pairs={{8,0},{16,8},{24,16},{32,24},{40,32},{48,40},{56,48},{64,56},{72,6... | collective-permute-start | bytes 3145736 | tf_op jit(solution)/shard_map/ppermute | solution.py:376
  21.3 0.0 collective-permute-done.4.after_ref
  21.3 1.9 %collective-permute-start.5 = (bf16[2,512,256]{2,1,0:T(8,128)(2,1)S(1)}, bf16[2,512,256]{2,1,0:T(8,128)(2,1)S(1)}, u32[]{:S(2)}, u32[]{:S(2)}) collective-permute-start(bf16[2,512,256]{2,1,0:T(8,128)(2,1)S(1)} %collective-permute-done.4.after_ref), channel_id=1, source_target_pairs={{40,56},{56,8},{8,24},{24,40},{104,120},{120,72},{72,88},{41,57},{... | collective-permute-start | bytes 1572872 | tf_op jit(solution)/shard_map/ppermute | solution.py:429
  23.3 0.2 collective-permute-done.near_ref
  23.5 0.7 %collective-permute-start.2 = (bf16[2,512,256]{2,1,0:T(8,128)(2,1)S(1)}, bf16[2,512,256]{2,1,0:T(8,128)(2,1)S(1)}, u32[]{:S(2)}, u32[]{:S(2)}) collective-permute-start(bf16[2,512,256]{2,1,0:T(8,128)(2,1)S(1)} %collective-permute-done.1), channel_id=1, source_target_pairs={{48,115},{51,123}} | collective-permute-start | bytes 1572872 | tf_op jit(solution)/shard_map/ppermute | solution.py:425
  24.1 7.1 %collective-permute-done.5 = bf16[2,512,256]{2,1,0:T(8,128)(2,1)S(1)} collective-permute-done((bf16[2,512,256]{2,1,0:T(8,128)(2,1)S(1)}, bf16[2,512,256]{2,1,0:T(8,128)(2,1)S(1)}, u32[]{:S(2)}, u32[]{:S(2)}) %collective-permute-start.5) | collective-permute-done | bytes 524320 | tf_op jit(solution)/shard_map/ppermute | solution.py:429
  31.2 3.1 %collective-permute-start.6 = (bf16[2,512,256]{2,1,0:T(8,128)(2,1)S(1)}, bf16[2,512,256]{2,1,0:T(8,128)(2,1)S(1)}, u32[]{:S(2)}, u32[]{:S(2)}) collective-permute-start(bf16[2,512,256]{2,1,0:T(8,128)(2,1)S(1)} %collective-permute-done.5), channel_id=1, source_target_pairs={{56,8},{8,24},{24,40},{40,56},{120,72},{72,88},{88,104},{57,9},{9,... | collective-permute-start | bytes 1572872 | tf_op jit(solution)/shard_map/ppermute | solution.py:429
  34.4 0.0 collective-permute-done.2.far_ref
  34.4 0.7 %range_tail.1.here_ref = bf16[2,512,256]{2,1,0:T(8,128)(2,1)S(1)} custom-call(bf16[1024,512]{1,0:T(8,128)(2,1)S(1)} %get-tuple-element.13.weights_ref, bf16[2,512,1024]{2,1,0:T(8,128)(2,1)S(1)} %get-tuple-element.16.kept_ref, bf16[2,512,256]{2,1,0:T(8,128)(2,1)S(1)} %collective-permute-done.near_ref, bf16[2,512,256]{2,1,0:T(8,128)(2,1)S(1)} %collective-permute-done.2.far_ref), custom_call_target="tpu_custom_call" | custom-call | tf_op jit(solution)/shard_map/range_tail/pallas_call | solution.py:192
  35.1 1.9 %collective-permute-start.3 = (bf16[2,512,256]{2,1,0:T(8,128)(2,1)S(1)}, bf16[2,512,256]{2,1,0:T(8,128)(2,1)S(1)}, u32[]{:S(2)}, u32[]{:S(2)}) collective-permute-start(bf16[2,512,256]{2,1,0:T(8,128)(2,1)S(1)} %range_tail.1.here_ref), channel_id=1, source_target_pairs={{8,0},{16,8},{24,16},{32,24},{40,32},{48,40},{56,48},{64,56},{72,6... | collective-permute-start | bytes 1572872 | tf_op jit(solution)/shard_map/ppermute | solution.py:376
  37.0 3.6 %azimuth_weights.1.weights_ref = bf16[16,256,640]{2,1,0:T(8,128)(2,1)S(1)} custom-call(s32[16,128]{1,0:T(8,128)S(1)} %bitcast.1, bf16[2,64,512]{2,1,0:T(8,128)(2,1)S(1)} %copy-done, bf16[2,512,512]{2,1,0:T(8,128)(2,1)S(1)} %get-tuple-element.18.previous_ref.here_ref), custom_call_target="tpu_custom_call" | custom-call | tf_op jit(solution)/shard_map/azimuth_weights/pallas_call | solution.py:229
  40.7 0.6 azimuth_own.1.own_ref
  41.3 2.8 %azimuth_compress.4.rest_0_ = bf16[2,512,2048]{2,1,0:T(8,128)(2,1)} custom-call(bf16[16,256,640]{2,1,0:T(8,128)(2,1)S(1)} %azimuth_weights.1.weights_ref, bf16[2,512,512]{2,1,0:T(8,128)(2,1)S(1)} %get-tuple-element.15.previous_ref.here_ref, bf16[2,512,512]{2,1,0:T(8,128)(2,1)S(1)} %collective-permute-done.9.after_ref), custom_call_target="tpu_custom_call" | custom-call | tf_op jit(solution)/shard_map/azimuth_compress/pallas_call | solution.py:284
  44.1 0.0 collective-permute-done.8.after_ref
  44.1 2.8 %azimuth_compress.5.rest_0_ = bf16[2,512,2048]{2,1,0:T(8,128)(2,1)} custom-call(bf16[16,256,640]{2,1,0:T(8,128)(2,1)S(1)} %azimuth_weights.1.weights_ref, bf16[2,512,512]{2,1,0:T(8,128)(2,1)S(1)} %get-tuple-element.20.here_ref, bf16[2,512,512]{2,1,0:T(8,128)(2,1)S(1)} %collective-permute-done.8.after_ref, ...), custom_call_target="tpu_custom_call", output_to_operand_aliasing={{}: (3, {})} | custom-call | tf_op jit(solution)/shard_map/azimuth_compress/pallas_call | solution.py:284
  46.9 5.8 %collective-permute-done.7.after_ref = bf16[2,512,512]{2,1,0:T(8,128)(2,1)S(1)} collective-permute-done((bf16[2,512,512]{2,1,0:T(8,128)(2,1)S(1)}, bf16[2,512,512]{2,1,0:T(8,128)(2,1)S(1)}, u32[]{:S(2)}, u32[]{:S(2)}) %collective-permute-start.7) | collective-permute-done | bytes 1048608 | tf_op jit(solution)/shard_map/ppermute | solution.py:376
  52.6 2.8 %azimuth_compress.6.rest_1_ = bf16[2,512,2048]{2,1,0:T(8,128)(2,1)} custom-call(bf16[16,256,640]{2,1,0:T(8,128)(2,1)S(1)} %azimuth_weights.1.weights_ref, bf16[2,512,512]{2,1,0:T(8,128)(2,1)S(1)} %get-tuple-element.18.previous_ref.here_ref, bf16[2,512,512]{2,1,0:T(8,128)(2,1)S(1)} %collective-permute-done.7.after_ref, ...), custom_call_target="tpu_custom_call", output_to_operand_aliasing={{}: (3, {})} | custom-call | tf_op jit(solution)/shard_map/azimuth_compress/pallas_call | solution.py:284
  55.4 0.0 collective-permute-done.6.rest_0_
  55.4 1.8 %azimuth_compress.7.current_ref = bf16[2,512,2048]{2,1,0:T(8,128)(2,1)} custom-call(bf16[16,256,640]{2,1,0:T(8,128)(2,1)S(1)} %azimuth_weights.1.weights_ref, bf16[2,512,256]{2,1,0:T(8,128)(2,1)S(1)} %get-tuple-element.17.previous_ref.here_ref, bf16[2,512,256]{2,1,0:T(8,128)(2,1)S(1)} %collective-permute-done.4.after_ref, ...), custom_call_target="tpu_custom_call", output_to_operand_aliasing={{}: (4, {})} | custom-call | tf_op jit(solution)/shard_map/azimuth_compress/pallas_call | solution.py:284
  57.2 1.0 %collective-permute-done.3.after_ref = bf16[2,512,256]{2,1,0:T(8,128)(2,1)S(1)} collective-permute-done((bf16[2,512,256]{2,1,0:T(8,128)(2,1)S(1)}, bf16[2,512,256]{2,1,0:T(8,128)(2,1)S(1)}, u32[]{:S(2)}, u32[]{:S(2)}) %collective-permute-start.3) | collective-permute-done | bytes 524320 | tf_op jit(solution)/shard_map/ppermute | solution.py:376
  58.2 1.4 %azimuth_rest.1 = bf16[2,512,2048]{2,1,0:T(8,128)(2,1)} custom-call(bf16[16,256,640]{2,1,0:T(8,128)(2,1)S(1)} %azimuth_weights.1.weights_ref, f32[2,512,256]{2,1,0:T(8,128)S(1)} %azimuth_own.1.own_ref, bf16[2,512,256]{2,1,0:T(8,128)(2,1)S(1)} %collective-permute-done.3.after_ref, ...), custom_call_target="tpu_custom_call", output_to_operand_aliasing={{}: (3, {})} | custom-call | tf_op jit(solution)/shard_map/azimuth_rest/pallas_call | solution.py:362
  (3 shorter events, 0.0 us)
Async XLA Ops:
  2.7 15.8 %collective-permute-start.1 = (bf16[2,512,256]{2,1,0:T(8,128)(2,1)S(1)}, bf16[2,512,256]{2,1,0:T(8,128)(2,1)S(1)}, u32[]{:S(2)}, u32[]{:S(2)}) collective-permute-start(bf16[2,512,256]{2,1,0:T(8,128)(2,1)S(1)} %get-tuple-element.19), channel_id=1, source_target_pairs={{116,48},{124,51}} | collective-permute-start | bytes 1572872 | tf_op jit(solution)/shard_map/ppermute | solution.py:424
  5.0 16.3 %collective-permute-start.4 = (bf16[2,512,256]{2,1,0:T(8,128)(2,1)S(1)}, bf16[2,512,256]{2,1,0:T(8,128)(2,1)S(1)}, u32[]{:S(2)}, u32[]{:S(2)}) collective-permute-start(bf16[2,512,256]{2,1,0:T(8,128)(2,1)S(1)} %get-tuple-element.17.previous_ref.here_ref), channel_id=1, source_target_pairs={{8,0},{24,16},{16,40},{40,32},{32,56},{56,48},{48,8},{72,64},{64,2... | collective-permute-start | bytes 1572872 | tf_op jit(solution)/shard_map/ppermute | solution.py:429
  7.6 15.9 %collective-permute-start = (bf16[2,512,256]{2,1,0:T(8,128)(2,1)S(1)}, bf16[2,512,256]{2,1,0:T(8,128)(2,1)S(1)}, u32[]{:S(2)}, u32[]{:S(2)}) collective-permute-start(bf16[2,512,256]{2,1,0:T(8,128)(2,1)S(1)} %get-tuple-element.19), channel_id=1, source_target_pairs={{1,0},{2,1},{3,2},{4,3},{5,4},{6,5},{7,6},{9,8},{10,9},{11,10},{12... | collective-permute-start | bytes 1572872 | tf_op jit(solution)/shard_map/ppermute | solution.py:426
  11.9 29.3 %collective-permute-start.9 = (bf16[2,512,512]{2,1,0:T(8,128)(2,1)S(1)}, bf16[2,512,512]{2,1,0:T(8,128)(2,1)S(1)}, u32[]{:S(2)}, u32[]{:S(2)}) collective-permute-start(bf16[2,512,512]{2,1,0:T(8,128)(2,1)S(1)} %get-tuple-element.15.previous_ref.here_ref), channel_id=1, source_target_pairs={{8,0},{16,8},{24,16},{32,24},{40,32},{48,40},{56,48},{64,56},{72,6... | collective-permute-start | bytes 3145736 | tf_op jit(solution)/shard_map/ppermute | solution.py:376
  14.1 22.9 %copy-start = (bf16[2,64,512]{2,1,0:T(8,128)(2,1)S(1)}, bf16[2,64,512]{2,1,0:T(8,128)(2,1)}, u32[]{:S(2)}) copy-start(bf16[2,64,512]{2,1,0:T(8,128)(2,1)} %refs_ref.1) | copy-start | bytes 393220
  14.1 22.9 %copy-start.1 = (s32[2048]{0:T(1024)S(1)}, s32[2048]{0:T(1024)}, u32[]{:S(2)}) copy-start(s32[2048]{0:T(1024)} %param.7) | copy-start | bytes 24580
  16.5 27.6 %collective-permute-start.8 = (bf16[2,512,512]{2,1,0:T(8,128)(2,1)S(1)}, bf16[2,512,512]{2,1,0:T(8,128)(2,1)S(1)}, u32[]{:S(2)}, u32[]{:S(2)}) collective-permute-start(bf16[2,512,512]{2,1,0:T(8,128)(2,1)S(1)} %get-tuple-element.20.here_ref), channel_id=1, source_target_pairs={{8,0},{16,8},{24,16},{32,24},{40,32},{48,40},{56,48},{64,56},{72,6... | collective-permute-start | bytes 3145736 | tf_op jit(solution)/shard_map/ppermute | solution.py:376
  18.5 34.1 %collective-permute-start.7 = (bf16[2,512,512]{2,1,0:T(8,128)(2,1)S(1)}, bf16[2,512,512]{2,1,0:T(8,128)(2,1)S(1)}, u32[]{:S(2)}, u32[]{:S(2)}) collective-permute-start(bf16[2,512,512]{2,1,0:T(8,128)(2,1)S(1)} %get-tuple-element.18.previous_ref.here_ref), channel_id=1, source_target_pairs={{8,0},{16,8},{24,16},{32,24},{40,32},{48,40},{56,48},{64,56},{72,6... | collective-permute-start | bytes 3145736 | tf_op jit(solution)/shard_map/ppermute | solution.py:376
  21.3 9.9 %collective-permute-start.5 = (bf16[2,512,256]{2,1,0:T(8,128)(2,1)S(1)}, bf16[2,512,256]{2,1,0:T(8,128)(2,1)S(1)}, u32[]{:S(2)}, u32[]{:S(2)}) collective-permute-start(bf16[2,512,256]{2,1,0:T(8,128)(2,1)S(1)} %collective-permute-done.4.after_ref), channel_id=1, source_target_pairs={{40,56},{56,8},{8,24},{24,40},{104,120},{120,72},{72,88},{41,57},{... | collective-permute-start | bytes 1572872 | tf_op jit(solution)/shard_map/ppermute | solution.py:429
  23.5 10.9 %collective-permute-start.2 = (bf16[2,512,256]{2,1,0:T(8,128)(2,1)S(1)}, bf16[2,512,256]{2,1,0:T(8,128)(2,1)S(1)}, u32[]{:S(2)}, u32[]{:S(2)}) collective-permute-start(bf16[2,512,256]{2,1,0:T(8,128)(2,1)S(1)} %collective-permute-done.1), channel_id=1, source_target_pairs={{48,115},{51,123}} | collective-permute-start | bytes 1572872 | tf_op jit(solution)/shard_map/ppermute | solution.py:425
  31.2 24.2 %collective-permute-start.6 = (bf16[2,512,256]{2,1,0:T(8,128)(2,1)S(1)}, bf16[2,512,256]{2,1,0:T(8,128)(2,1)S(1)}, u32[]{:S(2)}, u32[]{:S(2)}) collective-permute-start(bf16[2,512,256]{2,1,0:T(8,128)(2,1)S(1)} %collective-permute-done.5), channel_id=1, source_target_pairs={{56,8},{8,24},{24,40},{40,56},{120,72},{72,88},{88,104},{57,9},{9,... | collective-permute-start | bytes 1572872 | tf_op jit(solution)/shard_map/ppermute | solution.py:429
  35.1 23.1 %collective-permute-start.3 = (bf16[2,512,256]{2,1,0:T(8,128)(2,1)S(1)}, bf16[2,512,256]{2,1,0:T(8,128)(2,1)S(1)}, u32[]{:S(2)}, u32[]{:S(2)}) collective-permute-start(bf16[2,512,256]{2,1,0:T(8,128)(2,1)S(1)} %range_tail.1.here_ref), channel_id=1, source_target_pairs={{8,0},{16,8},{24,16},{32,24},{40,32},{48,40},{56,48},{64,56},{72,6... | collective-permute-start | bytes 1572872 | tf_op jit(solution)/shard_map/ppermute | solution.py:376
